TPU v7x, 256 devices: a whole 4x4x8 slice. The times are simulated.
256 devices in a mesh: row: 32 (over z_hi, y, core), col: 8 (over z_lo, x).
Axes of the slice: x: 4, y: 4, z: 8 (z_hi: 4, z_lo: 2; z = z_hi * 2 + z_lo), core: 2. Of those that a mesh axis runs over, the one named last changes fastest.
Arguments:
- left: float32 [128, 16384], P('col', 'row'), may hold values from -12 to 12
- right: float32 [128, 16384], P('row', 'col'), may hold values from -12 to 12
- w_out: float32 [1024, 128], replicated, may hold values from -0.1875 to 0.1875
- b_out: float32 [128], replicated, may hold values from -3 to 3
- pair_grad: float32 [512, 512, 128], P('row', 'col'), may hold values from -6 to 6
Outputs:
- pair_out: float32 [512, 512, 128], P('row', 'col')
- grad_left: float32 [128, 16384], P('col', 'row')
- grad_right: float32 [128, 16384], P('row', 'col')
- grad_weight: float32 [1024, 128], replicated
- grad_bias: float32 [128], replicated
All inputs are finite; a program needn't handle non-finite values.
Results may differ from a plain program's by a relative error of at most 0.0001.
Values sent between devices are 32-bit elements; how exact they have to be, the bound alone decides.
No kernel may reach another device: no remote copies, remote signals or barrier semaphores. Data moves between devices by JAX's collectives and lax.ppermute only.
A program may use at most 128 MiB of HBM per device.

v0:
```python
import jax
import jax.numpy as jnp
from jax import lax
from jax.sharding import PartitionSpec as P

C = 32
Z = 128
S = 128


def body(left, right, w_out, b_out, pair_grad):
    highest = lax.Precision.HIGHEST
    tile_rows = left.shape[1] // C
    tile_cols = right.shape[1] // C
    residues = tile_rows * lax.axis_size("row")
    weight_cube = w_out.reshape(C, C, Z)
    contract_rows = (((0,), (0,)), ((), ()))
    contract_cols = (((1,), (1,)), ((), ()))
    left_all = lax.all_gather(left, "col", axis=0, tiled=True)
    right_all = lax.all_gather(right, "row", axis=0, tiled=True)
    outer = (
        lax.dot_general(
            left_all,
            right_all,
            contract_rows,
            precision=highest,
            preferred_element_type=jnp.float32,
        )
        / S
    )
    outer_split = outer.reshape(tile_rows, C, tile_cols, C)
    pair_out = jnp.einsum("icje,cez->ijz", outer_split, weight_cube, precision=highest) + b_out
    grad_outer = jnp.einsum("ijz,cez->icje", pair_grad, weight_cube, precision=highest)
    grad_outer = grad_outer.reshape(tile_rows * C, tile_cols * C)
    grad_left = lax.psum_scatter(
        lax.dot_general(
            right_all,
            grad_outer,
            contract_cols,
            precision=highest,
            preferred_element_type=jnp.float32,
        )
        / S,
        "col",
        scatter_dimension=0,
        tiled=True,
    )
    grad_right = lax.psum_scatter(
        jnp.dot(left_all, grad_outer, precision=highest) / S, "row", scatter_dimension=0, tiled=True
    )
    weight_term = jnp.einsum("icje,ijz->cez", outer_split, pair_grad, precision=highest).reshape(
        C * C, Z
    )
    bias_term = jnp.sum(pair_grad, axis=(0, 1))
    grad_weight, grad_bias = lax.psum((weight_term, bias_term), ("row", "col"))
    return (pair_out, grad_left, grad_right, grad_weight / residues, grad_bias / residues)


def solution(mesh):
    placed = (P("col", "row"), P("row", "col"), P(), P(), P("row", "col", None))
    return jax.shard_map(
        body,
        mesh=mesh,
        in_specs=placed,
        out_specs=(P("row", "col", None), P("col", "row"), P("row", "col"), P(), P()),
        check_vma=False,
    )
```

profile of v0, /device:TPU:32, one launch (start us, length us, event | category | flops | bytes accessed | tf_op | source)
XLA Modules:
  0.0 768.8 jit_solution(7213743941106208333)
XLA Ops:
  7.2 0.0 copy-start
  7.2 0.0 all-reduce.6.cloned.1.call-start
  7.2 28.8 %all_gather.6 = f32[128,512]{1,0:T(8,128)S(1)} all-gather(f32[16,512]{1,0:T(8,128)} %param.5), channel_id=1, replica_groups=mesh['row'=32,'col'=8] {'col'}, dimensions={0}, use_global_device_ids=true | all-gather | bytes 294912 | tf_op jit(solution)/shard_map/all_gather | solution.py:19
  36.0 0.0 copy-done
  36.0 9.8 %convolution_bitcast_fusion = f32[16,32,64,32]{2,3,0,1:T(8,128)} fusion(f32[32,32,128,1]{2,1,3,0:T(8,128)S(1)} %bitcast.42, f32[16,64,128]{2,1,0:T(8,128)} %param.9), kind=kOutput, calls=%fused_computation.1 | convolution fusion | flops 1610612736 | bytes 5242880 | tf_op jit(solution)/shard_map/ijz,cez->icje/dot_general | solution.py:33
  45.8 12.3 %copy.21 = f32[16,32,64,32]{3,2,1,0:T(8,128)} copy(f32[16,32,64,32]{2,3,0,1:T(8,128)} %convolution_bitcast_fusion) | data formatting | bytes 8388608 | tf_op jit(solution)/shard_map/ijz,cez->icje/transpose | solution.py:33
  58.1 0.0 copy-start.1
  58.1 0.0 copy-start.3
  58.1 13.5 %reshape.24 = f32[512,2048]{1,0:T(8,128)} reshape(f32[16,32,64,32]{3,2,1,0:T(8,128)} %copy.21) | data formatting | bytes 8388608 | tf_op jit(solution)/shard_map/reshape | solution.py:34
  71.6 9.9 %fusion = f32[128,2048]{0,1:T(8,128)} fusion(f32[512,2048]{1,0:T(8,128)} %reshape.24, f32[128,512]{1,0:T(8,128)S(1)} %all_gather.6), kind=kOutput, calls=%fused_computation.3 | convolution fusion | flops 1610874880 | bytes 5505024 | tf_op jit(solution)/shard_map/dot_general | solution.py:49
  81.5 0.0 all-reduce.6.cloned.1.call-update
  81.5 0.0 all-gather.3.cloned.1.call-start
  81.5 0.7 all-gather.3.cloned.1.call-update
  82.3 0.2 all-reduce.4.cloned.1.call-start
  82.5 0.0 copy-done.1
  82.5 0.2 reduce_sum.9
  82.6 0.0 copy-done.3
  82.7 0.6 dynamic-slice
  83.9 77.7 %psum.15 = f32[128]{0:T(128)S(1)} all-reduce(f32[128]{0:T(128)S(1)} %reduce_sum.9), channel_id=1, replica_groups=mesh['row'=32,'col'=8] {'row','col'}, use_global_device_ids=true, to_apply=%region_4.0 | all-reduce | flops 128 | bytes 1024 | tf_op jit(solution)/shard_map/psum | solution.py:55
  161.6 0.5 broadcast_multiply_fusion.1
  162.1 211.0 %all-reduce.6.cloned.1.call-done = f32[128,2048]{0,1:T(8,128)} async-done(((f32[128,2048]{0,1:T(8,128)}), f32[128,2048]{0,1:T(8,128)}) %all-reduce.6.cloned.1.call-update) | async-done | bytes 1048592
  373.1 1.6 constant_dynamic-slice_fusion
  374.7 0.9 copy.25
  375.6 50.7 %all-gather.3.cloned.1.call-done = f32[32,4,2048]{2,1,0:T(4,128)} async-done(((f32[1,4,2048]{2,1,0:T(4,128)}), f32[32,4,2048]{2,1,0:T(4,128)}) %all-gather.3.cloned.1.call-update) | async-done | bytes 1048592 | tf_op jit(solution)/shard_map/all_gather | solution.py:20
  426.3 1.6 reshape.26
  427.9 5.0 convolution_multiply_fusion
  432.9 11.4 %reshape.22 = f32[16,32,64,32]{3,2,1,0:T(8,128)} reshape(f32[512,2048]{1,0:T(8,128)} %convolution_multiply_fusion) | data formatting | bytes 8388608 | tf_op jit(solution)/shard_map/reshape | solution.py:31
  444.3 12.7 %copy.33 = f32[32,32,16,64]{3,1,0,2:T(8,128)} copy(f32[32,32,16,64]{1,3,0,2:T(8,128)} %bitcast.44) | data formatting | bytes 8388608 | tf_op jit(solution)/shard_map/icje,ijz->cez/dot_general | solution.py:51
  457.0 0.0 copy-start.2
  457.0 9.9 %convolution_bitcast_fusion.2 = f32[1024,128]{1,0:T(8,128)} fusion(f32[1024,16,64]{2,0,1:T(8,128)} %bitcast.45, f32[16,64,128]{2,1,0:T(8,128)S(1)} %copy-done.1), kind=kOutput, calls=%fused_computation.5 | convolution fusion | flops 1610612736 | bytes 5242880 | tf_op jit(solution)/shard_map/icje,ijz->cez/dot_general | solution.py:51
  466.9 0.0 all-reduce.4.cloned.1.call-update
  466.9 0.3 reduce-scatter.5.cloned.1.call-start
  467.2 5.2 fusion.2
  472.4 0.8 copy.29
  473.3 0.0 reduce-scatter.5.cloned.1.call-update
  473.3 0.0 copy-done.2
  473.3 17.6 %fusion.1 = f32[16,64,128]{2,1,0:T(8,128)} fusion(f32[16,32,64,32]{3,2,1,0:T(8,128)} %reshape.22, f32[32,32,128,1]{2,1,0,3:T(8,128)S(1)} %bitcast.43, f32[128]{0:T(128)S(1)} %copy-done.2), kind=kOutput, calls=%fused_computation.6 | convolution fusion | flops 1610743808 | bytes 5243392 | tf_op jit(solution)/shard_map/icje,cez->ijz/dot_general | solution.py:32
  490.9 228.1 %all-reduce.4.cloned.1.call-done = f32[1024,128]{1,0:T(8,128)} async-done(((f32[1024,128]{1,0:T(8,128)}), f32[1024,128]{1,0:T(8,128)}) %all-reduce.4.cloned.1.call-update) | async-done | bytes 524304 | tf_op jit(solution)/shard_map/psum | solution.py:55
  719.0 1.9 broadcast_multiply_fusion
  720.8 41.4 %reduce-scatter.5.cloned.1.call-done = f32[16,512]{1,0:T(8,128)} async-done(((f32[128,512]{1,0:T(8,128)}), f32[16,512]{1,0:T(8,128)}) %reduce-scatter.5.cloned.1.call-update) | async-done | bytes 32784
Async XLA Ops:
  7.2 28.8 %copy-start = (f32[1024,128]{1,0:T(8,128)S(1)}, f32[1024,128]{1,0:T(8,128)}, u32[]{:S(2)}) copy-start(f32[1024,128]{1,0:T(8,128)} %param.7) | copy-start | bytes 1572868
  7.2 365.9 %all-reduce.6.cloned.1.call-start = ((), (), s32[]{:S(2)}) async-start(), calls=%async_computation.4 | async-start | bytes 2097152
  58.1 24.3 %copy-start.1 = (f32[16,64,128]{2,1,0:T(8,128)S(1)}, f32[16,64,128]{2,1,0:T(8,128)}, u32[]{:S(2)}) copy-start(f32[16,64,128]{2,1,0:T(8,128)} %param.9) | copy-start | bytes 1572868
  58.1 24.5 %copy-start.3 = (u32[256]{0:T(256)S(1)}, u32[256]{0:T(256)}, u32[]{:S(2)}) copy-start(u32[256]{0:T(256)} %constant.18) | copy-start | bytes 3076
  81.5 344.8 %all-gather.3.cloned.1.call-start = ((), (), s32[]{:S(2)}) async-start(), calls=%async_computation.2 | async-start | bytes 1081344 | tf_op jit(solution)/shard_map/all_gather | solution.py:20
  82.3 636.7 %all-reduce.4.cloned.1.call-start = ((), (), s32[]{:S(2)}) async-start(), calls=%async_computation.1 | async-start | bytes 1048576 | tf_op jit(solution)/shard_map/psum | solution.py:55
  457.0 16.3 %copy-start.2 = (f32[128]{0:T(128)S(1)}, f32[128]{0:T(128)}, u32[]{:S(2)}) copy-start(f32[128]{0:T(128)} %param.8) | copy-start | bytes 1540
  466.9 295.3 %reduce-scatter.5.cloned.1.call-start = ((), (), s32[]{:S(2)}) async-start(), calls=%async_computation.3 | async-start | bytes 294912
Sparse Core Ops, SparseCore 0:
  81.6 291.4 all-reduce.5
  375.7 50.5 all-gather.2
  467.1 251.8 all-reduce.3
  721.9 40.2 reduce-scatter.4
where the time goes:
time: 771 us; the launch traced here: 769 us
  waiting for transfers between devices  532 us (69%)
  blocking collectives  106 us (14%)
  matrix products  57.4 us (7%)
  local copies, waits for them, and re-layouts  55.4 us (7%)
  between operations  14.5 us (2%)
    unnamed x6, waiting for transfers between devices  253 us
    psum x1, waiting for transfers between devices, body(): grad_weight, grad_bias = lax.psum((weight_term, bias_term), ('row', 'col'))  228 us
    psum x1, blocking collectives, body(): grad_weight, grad_bias = lax.psum((weight_term, bias_term), ('row', 'col'))  77.7 us
    all_gather x1, waiting for transfers between devices, body(): right_all = lax.all_gather(right, 'row', axis=0, tiled=True)  50.7 us
    all_gather x1, blocking collectives, body(): left_all = lax.all_gather(left, 'col', axis=0, tiled=True)  28.8 us
    dot_general x1, matrix products, body(): jnp.einsum('icje,cez->ijz', outer_split, weight_cube, precision=highest)  17.6 us
  transfers between devices with their start and end apart: 4, of which 4 were waited for; matrix products, arithmetic and copies ran while one was open for 4% of the time, Pallas kernels for 0%

commit v1 on v0

v1 whole, which is shorter than its diff:
```python
import jax
import jax.numpy as jnp
from jax import lax
from jax.experimental import pallas as pl
from jax.experimental.pallas import tpu as pltpu
from jax.sharding import PartitionSpec as P

C = 32
Z = 128
S = 128
TI = 16
TJ = 64
IC = TI * C
JE = TJ * C
IJ = TI * TJ
CE = C * C
F32 = jnp.float32
BF16 = jnp.bfloat16
NT = (((1,), (1,)), ((), ()))
NN = (((1,), (0,)), ((), ()))


def split(x):
    hi = x.astype(BF16)
    return hi, (x - hi.astype(F32)).astype(BF16)


def dot(x, y, dims=NN):
    return lax.dot_general(x, y, dims, preferred_element_type=F32)


def half_swap(x0, x1):
    lane = lax.broadcasted_iota(jnp.int32, x0.shape, 1)
    low = lane < 64
    r0 = pltpu.roll(x0, 64, 1)
    r1 = pltpu.roll(x1, 64, 1)
    return jnp.where(low, x0, r1), jnp.where(low, r0, x1)


def core_index():
    return lax.rem(lax.axis_index("row"), 2)


def order_left(left_ref, core):
    own, other = [], []
    for k in range(16):
        lo = left_ref[8 * k : 8 * k + 4, :]
        hi = left_ref[8 * k + 4 : 8 * k + 8, :]
        own.append(jnp.where(core == 0, lo, hi))
        other.append(jnp.where(core == 0, hi, lo))
    return own + other


def load_left(left_ref, a_scr, core):
    for k, part in enumerate(order_left(left_ref, core)):
        a_scr[4 * k : 4 * k + 4, :] = part


def load_weight(w_ref, wp_scr):
    for e in range(C):
        wp_scr[C * e : C * e + C, :] = w_ref[pl.ds(e, C, stride=C), :]


def grad_outer_kernel(g_ref, w_ref, goh_ref, gol_ref, wp_scr, r_scr):
    load_weight(w_ref, wp_scr)
    wh, wl = split(wp_scr[...])
    wcat = jnp.concatenate([wh, wl], axis=1)

    @pl.loop(0, 4)
    def _(n):
        gh, gl = split(g_ref[pl.ds(pl.multiple_of(n * 256, 256), 256), :])
        r_scr[...] = dot(wcat, jnp.concatenate([gh, gh], axis=1), NT) + dot(wh, gl, NT)
        for ip in range(2):
            for ep in range(16):
                x0 = r_scr[64 * ep : 64 * ep + 32, 128 * ip : 128 * ip + 128]
                x1 = r_scr[64 * ep + 32 : 64 * ep + 64, 128 * ip : 128 * ip + 128]
                for k, y in enumerate(half_swap(x0, x1)):
                    hi, lo = split(y)
                    rows = pl.ds(pl.multiple_of((4 * n + 2 * ip + k) * C, C), C)
                    goh_ref[rows, 128 * ep : 128 * ep + 128] = hi
                    gol_ref[rows, 128 * ep : 128 * ep + 128] = lo


def grad_right_kernel(left_ref, goh_ref, gol_ref, own_ref, other_ref, a_scr, t_scr):
    load_left(left_ref, a_scr, core_index())
    ah, al = split(a_scr[...])
    acat = jnp.concatenate([ah, al], axis=0)

    @pl.loop(0, 8)
    def _(n):
        cols = pl.ds(pl.multiple_of(n * 256, 256), 256)
        r = dot(acat, goh_ref[:, cols])
        r = r[:S] + r[S:] + dot(ah, gol_ref[:, cols])
        t_scr[cols, :] = (r * (1.0 / S)).T

    for m in range(16):
        block = jnp.concatenate([t_scr[pl.ds(4 * m + q, C, stride=TJ), :] for q in range(4)], axis=0)
        block = block.T
        for k in range(16):
            own_ref[k, :, 128 * m : 128 * m + 128] = block[4 * k : 4 * k + 4]
            other_ref[k, :, 128 * m : 128 * m + 128] = block[64 + 4 * k : 68 + 4 * k]


def outer_kernel(left_ref, own_ref, other_ref, g_ref, oh_ref, ol_ref, bh_ref, bl_ref, gwo_ref, gwx_ref,
                 a_scr, b_scr, t_scr, r_scr, w_scr):
    core = core_index()
    load_left(left_ref, a_scr, core)
    for k in range(16):
        b_scr[4 * k : 4 * k + 4, :] = own_ref[k]
        b_scr[64 + 4 * k : 68 + 4 * k, :] = other_ref[k]
    for m in range(16):
        t_scr[128 * m : 128 * m + 128, :] = b_scr[:, 128 * m : 128 * m + 128].T
    for e in range(C):
        hi, lo = split(t_scr[pl.ds(e, TJ, stride=C), :])
        bh_ref[TJ * e : TJ * e + TJ, :] = hi
        bl_ref[TJ * e : TJ * e + TJ, :] = lo
    ath, atl = split(a_scr[...].T)
    atcat = jnp.concatenate([ath, atl], axis=1)

    @pl.loop(0, 8)
    def _(n):
        rows = pl.ds(pl.multiple_of(n * 256, 256), 256)
        bh = bh_ref[rows, :]
        r_scr[...] = dot(atcat, jnp.concatenate([bh, bh], axis=1), NT) + dot(ath, bl_ref[rows, :], NT)
        for ep in range(2):
            for ip in range(8):
                x0 = r_scr[64 * ip : 64 * ip + 32, 128 * ep : 128 * ep + 128]
                x1 = r_scr[64 * ip + 32 : 64 * ip + 64, 128 * ep : 128 * ep + 128]
                for k, y in enumerate(half_swap(x0, x1)):
                    hi, lo = split(y)
                    out_rows = pl.ds(pl.multiple_of((4 * n + 2 * ep + k) * C, C), C)
                    oh_ref[out_rows, 128 * ip : 128 * ip + 128] = hi
                    ol_ref[out_rows, 128 * ip : 128 * ip + 128] = lo

    gh, gl = split(g_ref[...])
    gcat = jnp.concatenate([gh, gl], axis=1)

    @pl.loop(0, 4)
    def _(n):
        rows = pl.ds(pl.multiple_of(n * 256, 256), 256)
        r = dot(oh_ref[rows, :], gcat)
        w_scr[rows, :] = (r[:, :Z] + r[:, Z:] + dot(ol_ref[rows, :], gh)) * (1.0 / S)

    bias = jnp.broadcast_to(jnp.sum(g_ref[...], axis=0, keepdims=True), (8, Z))
    for k in range(16):
        lo = w_scr[pl.ds(k, C, stride=C), :]
        hi = w_scr[pl.ds(16 + k, C, stride=C), :]
        gwo_ref[k, 0:C, :] = jnp.where(core == 0, lo, hi)
        gwx_ref[k, 0:C, :] = jnp.where(core == 0, hi, lo)
        gwo_ref[k, C : C + 8, :] = bias
        gwx_ref[k, C : C + 8, :] = bias


def finish_kernel(oh_ref, ol_ref, w_ref, b_ref, goh_ref, gol_ref, bh_ref, bl_ref, p_ref, gl_ref, wp_scr, s_scr):
    core = core_index()
    load_weight(w_ref, wp_scr)
    wth, wtl = split(wp_scr[...].T)
    wcat = jnp.concatenate([wth, wtl], axis=0)

    @pl.loop(0, 4)
    def _(n):
        cols = pl.ds(pl.multiple_of(n * 256, 256), 256)
        r = dot(wcat, oh_ref[:, cols])
        r = r[:Z] + r[Z:] + dot(wth, ol_ref[:, cols])
        p_ref[cols, :] = (r * (1.0 / S)).T + b_ref[...]

    bh = bh_ref[...]
    bcat = jnp.concatenate([bh, bl_ref[...]], axis=1)
    r = dot(goh_ref[...], bcat)
    r = (r[:, :S] + r[:, S:] + dot(gol_ref[...], bh)) * (1.0 / S)
    s_scr[...] = r.T
    for k in range(16):
        own = s_scr[4 * k : 4 * k + 4, :]
        other = s_scr[64 + 4 * k : 68 + 4 * k, :]
        gl_ref[8 * k : 8 * k + 4, :] = jnp.where(core == 0, own, other)
        gl_ref[8 * k + 4 : 8 * k + 8, :] = jnp.where(core == 0, other, own)


def join_kernel(own_ref, other_ref, out_ref):
    core = core_index()
    for k in range(16):
        own = own_ref[k]
        other = other_ref[k]
        out_ref[C * k : C * k + C, :] = jnp.where(core == 0, own, other)
        out_ref[512 + C * k : 512 + C * k + C, :] = jnp.where(core == 0, other, own)


def call(kernel, outs, scratch, flops, nbytes):
    vmem = pl.BlockSpec(memory_space=pltpu.VMEM)

    def run(*args):
        return pl.pallas_call(
            kernel,
            out_shape=[jax.ShapeDtypeStruct(s, d) for s, d in outs],
            in_specs=[vmem] * len(args),
            out_specs=[vmem] * len(outs),
            scratch_shapes=[pltpu.VMEM(s, d) for s, d in scratch],
            cost_estimate=pl.CostEstimate(flops=flops, bytes_accessed=nbytes, transcendentals=0),
            compiler_params=pltpu.CompilerParams(vmem_limit_bytes=40 << 20),
        )(*args)

    return run


grad_outer_call = call(grad_outer_kernel, [((IC, JE), BF16)] * 2, [((CE, Z), F32), ((CE, 256), F32)], 10**9, 5 << 20)
grad_right_call = call(grad_right_kernel, [((16, 4, JE), F32)] * 2, [((S, IC), F32), ((JE, S), F32)], 10**9, 5 << 20)
outer_call = call(
    outer_kernel,
    [((CE, IJ), BF16)] * 2 + [((JE, S), BF16)] * 2 + [((16, 40, Z), F32)] * 2,
    [((S, IC), F32), ((S, JE), F32), ((JE, S), F32), ((IC, 256), F32), ((CE, Z), F32)],
    2 * 10**9, 7 << 20)
finish_call = call(finish_kernel, [((IJ, Z), F32), ((S, IC), F32)], [((CE, Z), F32), ((S, IC), F32)], 2 * 10**9, 9 << 20)
join_call = call(join_kernel, [((CE, Z), F32)], [], 10**5, 1 << 20)


def rid(z, y, c):
    return (z * 4 + y) * 2 + c


CORE = [(r, r ^ 1) for r in range(32)]
YZ = [[rid(z, y, c) for z in range(4) for y in range(4)] for c in range(2)]
XY = [[rid(z, y, c) * 8 + h * 4 + x for y in range(4) for x in range(4)] for z in range(4) for h in range(2) for c in range(2)]
Z8 = [[rid(z, y, c) * 8 + h * 4 + x for z in range(4) for h in range(2)] for y in range(4) for x in range(4) for c in range(2)]
BOTH = ("row", "col")


def spread(x, n, axis, groups=None):
    copies = jnp.broadcast_to(x[None], (n,) + x.shape)
    return lax.all_to_all(copies, axis, 0, 0, axis_index_groups=groups)


def body(left, right, w_out, b_out, pair_grad):
    g = pair_grad.reshape(IJ, Z)
    goh, gol = grad_outer_call(g, w_out)
    left_all = spread(left, 8, "col").reshape(S, IC)
    right_own = spread(right, 16, "row", YZ)
    right_other = lax.ppermute(right_own, "row", CORE)
    gr_own, gr_other = grad_right_call(left_all, goh, gol)
    oh, ol, bh, bl, gw_own, gw_other = outer_call(left_all, right_own, right_other, g)
    gw = gw_own + lax.ppermute(gw_other, "row", CORE)
    gw = jnp.sum(lax.all_to_all(gw, BOTH, 0, 0, axis_index_groups=XY), axis=0)
    gw = jnp.sum(spread(gw, 8, BOTH, Z8), axis=0) * (1.0 / 512)
    grad_bias = gw[C]
    gw_own = spread(gw[:C], 16, BOTH, XY)
    gw_other = lax.ppermute(gw_own, "row", CORE)
    (grad_weight,) = join_call(gw_own, gw_other)
    pair_out, gl = finish_call(oh, ol, w_out, b_out.reshape(1, Z), goh, gol, bh, bl)
    gr = gr_own + lax.ppermute(gr_other, "row", CORE)
    grad_right = jnp.sum(lax.all_to_all(gr, "row", 0, 0, axis_index_groups=YZ), axis=0)
    grad_left = jnp.sum(lax.all_to_all(gl.reshape(8, 16, IC), "col", 0, 0), axis=0)
    return (pair_out.reshape(TI, TJ, Z), grad_left, grad_right, grad_weight, grad_bias)


def solution(mesh):
    placed = (P("col", "row"), P("row", "col"), P(), P(), P("row", "col", None))
    return jax.shard_map(
        body,
        mesh=mesh,
        in_specs=placed,
        out_specs=(P("row", "col", None), P("col", "row"), P("row", "col"), P(), P()),
        check_vma=False,
    )
```

time: 771 us -> 140 us (0.18)
  waiting for transfers between devices: 532 us -> 26.1 us
  matrix products: 57.4 us -> 0 us
  blocking collectives: 106 us -> 53.1 us
  local copies, waits for them, and re-layouts: 55.4 us -> 16 us
  starting transfers between devices: 0.56 us -> 21.1 us
  Pallas kernels: 0 us -> 18.2 us
  between operations: 14.5 us -> 0.81 us
    unnamed x6 -> x0, waiting for transfers between devices: 253 us -> none
    psum x1 -> x0, waiting for transfers between devices: 228 us -> none  [body(): grad_weight, grad_bias = lax.psum((weight_term, bias_term), ('row', 'col'))]
    psum x1 -> x0, blocking collectives: 77.7 us -> none  [body(): grad_weight, grad_bias = lax.psum((weight_term, bias_term), ('row', 'col'))]
    dot_general x6 -> x0, matrix products: 57.4 us -> none  [the longest x1 17.6 us: body(): jnp.einsum('icje,cez->ijz', outer_split, weight_cube, precision=highest)]
    all_to_all x0 -> x3, blocking collectives: none -> 53.1 us  [the longest x2 39.6 us: spread(): return lax.all_to_all(copies, axis, 0, 0, axis_index_groups=groups)]
    all_gather x1 -> x0, waiting for transfers between devices: 50.7 us -> none  [body(): right_all = lax.all_gather(right, 'row', axis=0, tiled=True)]
    all_gather x1 -> x0, blocking collectives: 28.8 us -> none  [body(): left_all = lax.all_gather(left, 'col', axis=0, tiled=True)]
    reshape x2 -> x0, local copies, waits for them, and re-layouts: 24.9 us -> none  [the longest x1 13.5 us: body(): grad_outer = grad_outer.reshape(tile_rows * C, tile_cols * C)]
  transfers between devices with their start and end apart: 4 -> 8, of which waited for: 4 -> 3; matrix products, arithmetic and copies ran while one was open for 4% -> 4% of each run, Pallas kernels for 0% -> 7%
where the time goes in v1:
time: 140 us; the launch traced here: 139 us
  blocking collectives  53.1 us (38%)
  waiting for transfers between devices  26.1 us (19%)
  starting transfers between devices  21.1 us (15%)
  Pallas kernels  18.2 us (13%)
  local copies, waits for them, and re-layouts  16 us (11%)
  other arithmetic  4.22 us (3%)
    all_to_all x2, blocking collectives, spread(): return lax.all_to_all(copies, axis, 0, 0, axis_index_groups=groups)  39.6 us
    pallas_call x5, Pallas kernels, run(): pl.pallas_call(kernel, out_shape=[jax.ShapeDtypeStruct(s, d) for s, d in...  18.2 us
    all_to_all x1, waiting for transfers between devices, body(): lax.all_to_all(gr, 'row', 0, 0, axis_index_groups=YZ)  16.1 us
    all_to_all x1, blocking collectives, body(): gw = jnp.sum(lax.all_to_all(gw, BOTH, 0, 0, axis_index_groups=XY), axis=0)  13.5 us
    unnamed x26, local copies, waits for them, and re-layouts  12.4 us
    all_to_all x2, starting transfers between devices, spread(): return lax.all_to_all(copies, axis, 0, 0, axis_index_groups=groups)  9.42 us
    all_to_all x2, waiting for transfers between devices, spread(): return lax.all_to_all(copies, axis, 0, 0, axis_index_groups=groups)  8.4 us
    all_to_all x1, starting transfers between devices, body(): lax.all_to_all(gr, 'row', 0, 0, axis_index_groups=YZ)  7.46 us
  transfers between devices with their start and end apart: 8, of which 3 were waited for; matrix products, arithmetic and copies ran while one was open for 4% of the time, Pallas kernels for 7%

profile of v1, /device:TPU:32, one launch (start us, length us, event | category | flops | bytes accessed | tf_op | source)
XLA Modules:
  0.0 139.5 jit_solution(17924548114846522292)
XLA Ops:
  0.6 0.0 copy-start.11
  0.6 0.9 broadcast_in_dim.9
  1.6 27.6 %all_to_all.35.own_ref = f32[16,4,2048]{2,1,0:T(4,128)S(1)} all-to-all(f32[16,4,2048]{2,1,0:T(4,128)S(1)} %broadcast_in_dim.9), channel_id=1, replica_groups={{0,16,32,48,64,80,96,112,128,144,160,176,192,208,224,240},{8,24,40,56,7..., dimensions={0} | all-to-all | bytes 1048576 | tf_op jit(solution)/shard_map/all_to_all | solution.py:229
  29.1 0.0 collective-permute-start
  29.1 0.8 broadcast_in_dim.8
  29.9 12.0 %all_to_all.36 = f32[8,16,512]{2,1,0:T(8,128)S(1)} all-to-all(f32[8,16,512]{2,1,0:T(8,128)S(1)} %broadcast_in_dim.8), channel_id=1, replica_groups=mesh['row'=32,'col'=8] {'col'}, dimensions={0} | all-to-all | bytes 524288 | tf_op jit(solution)/shard_map/all_to_all | solution.py:229
  41.9 0.0 collective-permute-done.other_ref
  41.9 0.0 copy-done.11
  41.9 7.1 %shard_map.92 = (bf16[1024,1024]{1,0:T(8,128)(2,1)S(1)}, bf16[1024,1024]{1,0:T(8,128)(2,1)S(1)}, bf16[2048,128]{1,0:T(8,128)(2,1)S(1)}, bf16[2048,128]{1,0:T(8,1...) custom-call(f32[128,512]{1,0:T(8,128)S(1)} %bitcast.7, f32[16,4,2048]{2,1,0:T(4,128)S(1)} %all_to_all.35.own_ref, ...), custom_call_target="tpu_custom_call" | custom-call | flops 2000000000 | bytes 7340032 | tf_op jit(solution)/shard_map/pallas_call | solution.py:192
  49.0 0.0 copy-start.2
  49.0 1.3 copy-done.2
  50.4 0.0 copy-start.4
  50.4 1.3 copy-done.4
  51.7 0.0 copy-start.7
  51.7 0.8 copy-done.7
  52.5 0.0 copy-start.6
  52.5 0.0 collective-permute-start.2
  52.5 1.6 %collective-permute-done.2 = f32[16,40,128]{2,1,0:T(8,128)S(1)} collective-permute-done((f32[16,40,128]{2,1,0:T(8,128)S(1)}, f32[16,40,128]{2,1,0:T(8,128)S(1)}, u32[]{:S(2)}, u32[]{:S(2)}) %collective-permute-start.2) | collective-permute-done | bytes 327712 | tf_op jit(solution)/shard_map/ppermute | solution.py:240
  54.2 13.5 %all_to_all.37 = f32[16,40,128]{2,1,0:T(8,128)S(1)} all-to-all(f32[16,40,128]{2,1,0:T(8,128)S(1)} %add.7), channel_id=1, replica_groups={{0,1,2,3,16,17,18,19,32,33,34,35,48,49,50,51},{8,9,10,11,24,25,26,27,40..., dimensions={0} | all-to-all | bytes 655360 | tf_op jit(solution)/shard_map/all_to_all | solution.py:241
  67.7 0.0 copy-start.10
  67.7 0.7 broadcast_in_dim.10
  68.4 4.7 %all-to-all-start.5 = ((f32[8,40,128]{2,1,0:T(8,128)}), f32[8,40,128]{2,1,0:T(8,128)}, u32[]{:S(2)}, u32[]{:S(2)}) async-start(f32[8,40,128]{2,1,0:T(8,128)} %broadcast_in_dim.10), calls=%async_computation.5 | async-start | bytes 327680 | tf_op jit(solution)/shard_map/all_to_all | solution.py:229
  73.1 0.0 copy-done.6
  73.1 0.0 copy-start.12
  73.1 1.0 copy-done.12
  74.1 3.1 %shard_map.93 = (bf16[512,2048]{1,0:T(8,128)(2,1)S(1)}, bf16[512,2048]{1,0:T(8,128)(2,1)S(1)}) custom-call(f32[1024,128]{1,0:T(8,128)S(1)} %bitcast.12, f32[1024,128]{1,0:T(8,128)S(1)} %copy-done.6), custom_call_target="tpu_custom_call" | custom-call | flops 1000000000 | bytes 5242880 | tf_op jit(solution)/shard_map/pallas_call | solution.py:192
  77.2 0.0 copy-done.10
  77.2 0.0 copy-start.3
  77.2 1.6 %copy-done.3 = bf16[1024,1024]{1,0:T(8,128)(2,1)S(1)} copy-done((bf16[1024,1024]{1,0:T(8,128)(2,1)S(1)}, bf16[1024,1024]{1,0:T(8,128)(2,1)}, u32[]{:S(2)}) %copy-start.3) | copy-done | bytes 2097176
  78.8 0.0 copy-start.5
  78.8 1.6 %copy-done.5 = bf16[1024,1024]{1,0:T(8,128)(2,1)S(1)} copy-done((bf16[1024,1024]{1,0:T(8,128)(2,1)S(1)}, bf16[1024,1024]{1,0:T(8,128)(2,1)}, u32[]{:S(2)}) %copy-start.5) | copy-done | bytes 2097176
  80.4 0.0 copy-start.8
  80.4 1.0 copy-done.8
  81.5 3.5 %shard_map.94 = (f32[1024,128]{1,0:T(8,128)}, f32[128,512]{1,0:T(8,128)S(1)}) custom-call(bf16[1024,1024]{1,0:T(8,128)(2,1)S(1)} %copy-done.3, bf16[1024,1024]{1,0:T(8,128)(2,1)S(1)} %copy-done.5, f32[1024,128]{1,0:T(8,128)S(1)} %copy-done.6, f32[1,128]{1,0:T(1,128)S(1)} %bitcast.10, bf16[512,2048]{1,0:T(8,128)(2,1)S(1)} %get-tuple-element.19.goh_ref, ...), custom_call_target="tpu_custom_call" | custom-call | flops 2000000000 | bytes 9437184 | tf_op jit(solution)/shard_map/pallas_call | solution.py:192
  85.0 0.0 copy-start
  85.0 1.3 copy-done
  86.4 0.0 copy-start.9
  86.4 0.7 copy-done.9
  87.1 0.0 all-to-all-done.5
  87.1 4.1 %all-to-all-start.2 = ((f32[8,16,512]{2,1,0:T(8,128)}), f32[8,16,512]{2,1,0:T(8,128)}, u32[]{:S(2)}, u32[]{:S(2)}) async-start(f32[8,16,512]{2,1,0:T(8,128)} %bitcast.9), calls=%async_computation.2 | async-start | bytes 524288 | tf_op jit(solution)/shard_map/all_to_all | solution.py:250
  91.2 0.0 copy-start.1
  91.2 1.6 %copy-done.1 = bf16[512,2048]{1,0:T(8,128)(2,1)S(1)} copy-done((bf16[512,2048]{1,0:T(8,128)(2,1)S(1)}, bf16[512,2048]{1,0:T(8,128)(2,1)}, u32[]{:S(2)}) %copy-start.1) | copy-done | bytes 2097176
  92.7 3.6 %shard_map.95 = (f32[16,4,2048]{2,1,0:T(4,128)S(1)}, f32[16,4,2048]{2,1,0:T(4,128)S(1)}) custom-call(f32[128,512]{1,0:T(8,128)S(1)} %bitcast.8, bf16[512,2048]{1,0:T(8,128)(2,1)S(1)} %get-tuple-element.19.goh_ref, bf16[512,2048]{1,0:T(8,128)(2,1)S(1)} %copy-done.1), custom_call_target="tpu_custom_call" | custom-call | flops 1000000000 | bytes 5242880 | tf_op jit(solution)/shard_map/pallas_call | solution.py:192
  96.4 0.1 collective-permute-start.1
  96.5 0.9 reduce_sum.39
  97.4 0.0 all-to-all-done.2
  97.4 0.7 broadcast_in_dim.11
  98.2 4.7 %all-to-all-start.6 = ((f32[16,32,128]{2,1,0:T(8,128)}), f32[16,32,128]{2,1,0:T(8,128)S(1)}, u32[]{:S(2)}, u32[]{:S(2)}) async-start(f32[16,32,128]{2,1,0:T(8,128)} %broadcast_in_dim.11), calls=%async_computation.6 | async-start | bytes 524288 | tf_op jit(solution)/shard_map/all_to_all | solution.py:229
  102.8 0.0 collective-permute-done.1
  102.9 0.9 add.6
  103.8 8.4 %all-to-all-done.6.own_ref = f32[16,32,128]{2,1,0:T(8,128)S(1)} async-done(((f32[16,32,128]{2,1,0:T(8,128)}), f32[16,32,128]{2,1,0:T(8,128)S(1)}, u32[]{:S(2)}, u32[]{:S(2)}) %all-to-all-start.6) | async-done | bytes 262176 | tf_op jit(solution)/shard_map/all_to_all | solution.py:229
  112.2 7.5 %all-to-all-start.3 = ((f32[16,4,2048]{2,1,0:T(4,128)}), f32[16,4,2048]{2,1,0:T(4,128)S(1)}, u32[]{:S(2)}, u32[]{:S(2)}) async-start(f32[16,4,2048]{2,1,0:T(4,128)} %add.6), calls=%async_computation.3 | async-start | bytes 1048576 | tf_op jit(solution)/shard_map/all_to_all | solution.py:249
  119.7 0.1 collective-permute-start.3
  119.8 1.6 %reduce_sum.36 = f32[16,512]{1,0:T(8,128)} reduce(f32[8,16,512]{2,1,0:T(8,128)} %all-to-all-done.2, f32[]{:T(128)} %constant.0.clone.1), dimensions={0}, to_apply=%region_0.0 | reduce | flops 57344 | bytes 294916 | tf_op jit(solution)/shard_map/reduce_sum | solution.py:250
  121.3 16.1 %all-to-all-done.3 = f32[16,4,2048]{2,1,0:T(4,128)S(1)} async-done(((f32[16,4,2048]{2,1,0:T(4,128)}), f32[16,4,2048]{2,1,0:T(4,128)S(1)}, u32[]{:S(2)}, u32[]{:S(2)}) %all-to-all-start.3) | async-done | bytes 524320 | tf_op jit(solution)/shard_map/all_to_all | solution.py:249
  137.4 0.7 reduce_sum.37
  138.1 0.5 slice_bitcast_fusion
  138.6 0.0 collective-permute-done.3.other_ref
  138.6 0.8 shard_map.96
  (4 shorter events, 0.1 us)
Async XLA Ops:
  0.6 41.3 %copy-start.11 = (f32[16,64,128]{2,1,0:T(8,128)S(1)}, f32[16,64,128]{2,1,0:T(8,128)}, u32[]{:S(2)}) copy-start(f32[16,64,128]{2,1,0:T(8,128)} %param.9) | copy-start | bytes 1572868
  29.1 12.8 %collective-permute-start = (f32[16,4,2048]{2,1,0:T(4,128)S(1)}, f32[16,4,2048]{2,1,0:T(4,128)S(1)}, u32[]{:S(2)}, u32[]{:S(2)}) collective-permute-start(f32[16,4,2048]{2,1,0:T(4,128)S(1)} %all_to_all.35.own_ref), channel_id=1, source_target_pairs={{0,8},{8,0},{16,24},{24,16},{32,40},{40,32},{48,56},{56,48},{64,72... | collective-permute-start | bytes 1572872 | tf_op jit(solution)/shard_map/ppermute | solution.py:237
  49.0 1.3 copy-start.2
  50.4 1.3 copy-start.4
  51.7 0.8 copy-start.7
  52.5 20.6 %copy-start.6 = (f32[1024,128]{1,0:T(8,128)S(1)}, f32[1024,128]{1,0:T(8,128)}, u32[]{:S(2)}) copy-start(f32[1024,128]{1,0:T(8,128)} %w_ref.3) | copy-start | bytes 1572868
  52.5 1.6 %collective-permute-start.2 = (f32[16,40,128]{2,1,0:T(8,128)S(1)}, f32[16,40,128]{2,1,0:T(8,128)S(1)}, u32[]{:S(2)}, u32[]{:S(2)}) collective-permute-start(f32[16,40,128]{2,1,0:T(8,128)S(1)} %get-tuple-element.28), channel_id=1, source_target_pairs={{0,8},{8,0},{16,24},{24,16},{32,40},{40,32},{48,56},{56,48},{64,72... | collective-permute-start | bytes 983048 | tf_op jit(solution)/shard_map/ppermute | solution.py:240
  67.7 9.6 %copy-start.10 = (f32[128]{0:T(128)S(1)}, f32[128]{0:T(128)}, u32[]{:S(2)}) copy-start(f32[128]{0:T(128)} %param.8) | copy-start | bytes 1540
  68.4 18.7 %all-to-all-start.5 = ((f32[8,40,128]{2,1,0:T(8,128)}), f32[8,40,128]{2,1,0:T(8,128)}, u32[]{:S(2)}, u32[]{:S(2)}) async-start(f32[8,40,128]{2,1,0:T(8,128)} %broadcast_in_dim.10), calls=%async_computation.5 | async-start | bytes 327680 | tf_op jit(solution)/shard_map/all_to_all | solution.py:229
  73.1 1.0 copy-start.12
  77.2 1.6 %copy-start.3 = (bf16[1024,1024]{1,0:T(8,128)(2,1)S(1)}, bf16[1024,1024]{1,0:T(8,128)(2,1)}, u32[]{:S(2)}) copy-start(bf16[1024,1024]{1,0:T(8,128)(2,1)} %copy-done.2) | copy-start | bytes 6291460
  78.8 1.6 %copy-start.5 = (bf16[1024,1024]{1,0:T(8,128)(2,1)S(1)}, bf16[1024,1024]{1,0:T(8,128)(2,1)}, u32[]{:S(2)}) copy-start(bf16[1024,1024]{1,0:T(8,128)(2,1)} %copy-done.4) | copy-start | bytes 6291460
  80.4 1.0 copy-start.8
  85.0 1.3 copy-start
  86.4 0.7 copy-start.9
  87.1 10.4 %all-to-all-start.2 = ((f32[8,16,512]{2,1,0:T(8,128)}), f32[8,16,512]{2,1,0:T(8,128)}, u32[]{:S(2)}, u32[]{:S(2)}) async-start(f32[8,16,512]{2,1,0:T(8,128)} %bitcast.9), calls=%async_computation.2 | async-start | bytes 524288 | tf_op jit(solution)/shard_map/all_to_all | solution.py:250
  91.2 1.6 %copy-start.1 = (bf16[512,2048]{1,0:T(8,128)(2,1)S(1)}, bf16[512,2048]{1,0:T(8,128)(2,1)}, u32[]{:S(2)}) copy-start(bf16[512,2048]{1,0:T(8,128)(2,1)} %copy-done) | copy-start | bytes 6291460
  96.4 6.5 %collective-permute-start.1 = (f32[16,4,2048]{2,1,0:T(4,128)S(1)}, f32[16,4,2048]{2,1,0:T(4,128)S(1)}, u32[]{:S(2)}, u32[]{:S(2)}) collective-permute-start(f32[16,4,2048]{2,1,0:T(4,128)S(1)} %get-tuple-element.26), channel_id=1, source_target_pairs={{0,8},{8,0},{16,24},{24,16},{32,40},{40,32},{48,56},{56,48},{64,72... | collective-permute-start | bytes 1572872 | tf_op jit(solution)/shard_map/ppermute | solution.py:248
  98.2 14.0 %all-to-all-start.6 = ((f32[16,32,128]{2,1,0:T(8,128)}), f32[16,32,128]{2,1,0:T(8,128)S(1)}, u32[]{:S(2)}, u32[]{:S(2)}) async-start(f32[16,32,128]{2,1,0:T(8,128)} %broadcast_in_dim.11), calls=%async_computation.6 | async-start | bytes 524288 | tf_op jit(solution)/shard_map/all_to_all | solution.py:229
  112.2 25.2 %all-to-all-start.3 = ((f32[16,4,2048]{2,1,0:T(4,128)}), f32[16,4,2048]{2,1,0:T(4,128)S(1)}, u32[]{:S(2)}, u32[]{:S(2)}) async-start(f32[16,4,2048]{2,1,0:T(4,128)} %add.6), calls=%async_computation.3 | async-start | bytes 1048576 | tf_op jit(solution)/shard_map/all_to_all | solution.py:249
  119.7 19.0 %collective-permute-start.3 = (f32[16,32,128]{2,1,0:T(8,128)S(1)}, f32[16,32,128]{2,1,0:T(8,128)S(1)}, u32[]{:S(2)}, u32[]{:S(2)}) collective-permute-start(f32[16,32,128]{2,1,0:T(8,128)S(1)} %all-to-all-done.6.own_ref), channel_id=1, source_target_pairs={{0,8},{8,0},{16,24},{24,16},{32,40},{40,32},{48,56},{56,48},{64,72... | collective-permute-start | bytes 786440 | tf_op jit(solution)/shard_map/ppermute | solution.py:245

commit v2 on v0

v2 whole, which is shorter than its diff:
```python
import jax
import jax.numpy as jnp
from jax import lax
from jax.experimental import pallas as pl
from jax.experimental.pallas import tpu as pltpu
from jax.sharding import PartitionSpec as P

C = 32
Z = 128
S = 128
TI = 16
TJ = 64
IC = TI * C
JE = TJ * C
IJ = TI * TJ
CE = C * C
F32 = jnp.float32
BF16 = jnp.bfloat16
NT = (((1,), (1,)), ((), ()))
NN = (((1,), (0,)), ((), ()))


def split(x):
    hi = x.astype(BF16)
    return hi, (x - hi.astype(F32)).astype(BF16)


def dot(x, y, dims=NN):
    return lax.dot_general(x, y, dims, preferred_element_type=F32)


def half_swap(x0, x1):
    lane = lax.broadcasted_iota(jnp.int32, x0.shape, 1)
    low = lane < 64
    r0 = pltpu.roll(x0, 64, 1)
    r1 = pltpu.roll(x1, 64, 1)
    return jnp.where(low, x0, r1), jnp.where(low, r0, x1)


def core_index():
    return lax.rem(lax.axis_index("row"), 2)


def load_left(near_ref, far_ref, a_scr):
    core = core_index()
    col = lax.axis_index("col")
    for ref, half in ((near_ref, col // 4), (far_ref, 1 - col // 4)):
        for p in range(4):
            q = half * 4 + lax.rem(col + 4 - p, 4)
            x = ref[p]
            lo = jnp.concatenate([x[0:4], x[8:12]], axis=0)
            hi = jnp.concatenate([x[4:8], x[12:16]], axis=0)
            a_scr[pl.ds(pl.multiple_of(q * 8, 8), 8), :] = jnp.where(core == 0, lo, hi)
            a_scr[pl.ds(pl.multiple_of(64 + q * 8, 8), 8), :] = jnp.where(core == 0, hi, lo)


def load_weight(w_ref, wp_scr):
    for e in range(C):
        wp_scr[C * e : C * e + C, :] = w_ref[pl.ds(e, C, stride=C), :]


def grad_outer_kernel(g_ref, w_ref, goh_ref, gol_ref, wp_scr, wc_scr, r_scr):
    @pl.when(pl.program_id(0) == 0)
    def _():
        load_weight(w_ref, wp_scr)
        wh, wl = split(wp_scr[...])
        wc_scr[:, 0:Z] = wh
        wc_scr[:, Z : 2 * Z] = wl

    gh, gl = split(g_ref[...])
    r_scr[...] = dot(wc_scr[...], jnp.concatenate([gh, gh], axis=1), NT) + dot(wc_scr[:, 0:Z], gl, NT)
    for ip in range(2):
        for ep in range(16):
            x0 = r_scr[64 * ep : 64 * ep + 32, 128 * ip : 128 * ip + 128]
            x1 = r_scr[64 * ep + 32 : 64 * ep + 64, 128 * ip : 128 * ip + 128]
            for k, y in enumerate(half_swap(x0, x1)):
                hi, lo = split(y)
                row = (2 * ip + k) * C
                goh_ref[row : row + C, 128 * ep : 128 * ep + 128] = hi
                gol_ref[row : row + C, 128 * ep : 128 * ep + 128] = lo


def grad_right_kernel(near_ref, far_ref, goh_ref, gol_ref, own_ref, other_ref, a_scr, ac_scr, t_scr):
    n = pl.program_id(0)

    @pl.when(n == 0)
    def _():
        load_left(near_ref, far_ref, a_scr)
        ah, al = split(a_scr[...])
        ac_scr[0:S, :] = ah
        ac_scr[S : 2 * S, :] = al

    r = dot(ac_scr[...], goh_ref[...])
    r = r[:S] + r[S:] + dot(ac_scr[0:S, :], gol_ref[...])
    t_scr[pl.ds(pl.multiple_of(n * 512, 512), 512), :] = (r * (1.0 / S)).T

    @pl.when(n == 3)
    def _():
        row = lax.axis_index("row") // 2
        y = lax.rem(row, 4)
        z = row // 4
        for m in range(16):
            block = jnp.concatenate([t_scr[pl.ds(4 * m + q, C, stride=TJ), :] for q in range(4)], axis=0)
            block = block.T
            for k in range(16):
                yy = lax.rem(k % 4 + 4 - y, 4)
                zz = lax.rem(k // 4 + 4 - z, 4)
                own_ref[yy, zz, :, 128 * m : 128 * m + 128] = block[4 * k : 4 * k + 4]
                other_ref[yy, zz, :, 128 * m : 128 * m + 128] = block[64 + 4 * k : 68 + 4 * k]


def outer_kernel(near_ref, far_ref, own_ref, other_ref, g_ref, oh_ref, ol_ref, bh_ref, bl_ref, gwo_ref, gwx_ref,
                 a_scr, at_scr, b_scr, t_scr, r_scr, gc_scr, w_scr):
    n = pl.program_id(0)

    @pl.when(n == 0)
    def _():
        load_left(near_ref, far_ref, a_scr)
        ath, atl = split(a_scr[...].T)
        at_scr[:, 0:S] = ath
        at_scr[:, S : 2 * S] = atl
        for k in range(16):
            b_scr[4 * k : 4 * k + 4, :] = own_ref[k]
            b_scr[64 + 4 * k : 68 + 4 * k, :] = other_ref[k]
        for m in range(16):
            t_scr[128 * m : 128 * m + 128, :] = b_scr[:, 128 * m : 128 * m + 128].T
        gh, gl = split(g_ref[...])
        gc_scr[:, 0:Z] = gh
        gc_scr[:, Z : 2 * Z] = gl

    for e in range(8):
        hi, lo = split(t_scr[pl.ds(8 * n + e, TJ, stride=C), :])
        bh_ref[TJ * e : TJ * e + TJ, :] = hi
        bl_ref[TJ * e : TJ * e + TJ, :] = lo
    for h in range(2):
        bh = bh_ref[256 * h : 256 * h + 256, :]
        bl = bl_ref[256 * h : 256 * h + 256, :]
        r_scr[h] = dot(at_scr[...], jnp.concatenate([bh, bh], axis=1), NT) + dot(at_scr[:, 0:S], bl, NT)
        for ep in range(2):
            for ip in range(8):
                x0 = r_scr[h, 64 * ip : 64 * ip + 32, 128 * ep : 128 * ep + 128]
                x1 = r_scr[h, 64 * ip + 32 : 64 * ip + 64, 128 * ep : 128 * ep + 128]
                for k, y in enumerate(half_swap(x0, x1)):
                    hi, lo = split(y)
                    row = (4 * h + 2 * ep + k) * C
                    oh_ref[row : row + C, 128 * ip : 128 * ip + 128] = hi
                    ol_ref[row : row + C, 128 * ip : 128 * ip + 128] = lo
    r = dot(oh_ref[...], gc_scr[...])
    rows = pl.ds(pl.multiple_of(n * 256, 256), 256)
    w_scr[rows, :] = (r[:, :Z] + r[:, Z:] + dot(ol_ref[...], gc_scr[:, 0:Z])) * (1.0 / S)

    @pl.when(n == 3)
    def _():
        core = core_index()
        bias = jnp.broadcast_to(jnp.sum(g_ref[...], axis=0, keepdims=True), (8, Z))
        for k in range(16):
            lo = w_scr[pl.ds(k, C, stride=C), :]
            hi = w_scr[pl.ds(16 + k, C, stride=C), :]
            gwo_ref[k, 0:C, :] = jnp.where(core == 0, lo, hi)
            gwx_ref[k, 0:C, :] = jnp.where(core == 0, hi, lo)
            gwo_ref[k, C : C + 8, :] = bias
            gwx_ref[k, C : C + 8, :] = bias


def finish_kernel(oh_ref, ol_ref, w_ref, b_ref, goh_ref, gol_ref, bh_ref, bl_ref, p_ref, gl_ref, wp_scr, wc_scr, acc_scr, s_scr):
    n = pl.program_id(0)

    @pl.when(n == 0)
    def _():
        load_weight(w_ref, wp_scr)
        wth, wtl = split(wp_scr[...].T)
        wc_scr[0:Z, :] = wth
        wc_scr[Z : 2 * Z, :] = wtl
        acc_scr[...] = jnp.zeros_like(acc_scr)

    r = dot(wc_scr[...], oh_ref[...])
    r = r[:Z] + r[Z:] + dot(wc_scr[0:Z, :], ol_ref[...])
    p_ref[...] = (r * (1.0 / S)).T + b_ref[...]
    bh = bh_ref[...]
    r = dot(goh_ref[...], jnp.concatenate([bh, bl_ref[...]], axis=1))
    acc_scr[...] += r[:, :S] + r[:, S:] + dot(gol_ref[...], bh)

    @pl.when(n == 3)
    def _():
        core = core_index()
        col = lax.axis_index("col")
        s_scr[...] = (acc_scr[...] * (1.0 / S)).T
        for q in range(8):
            own = s_scr[8 * q : 8 * q + 8, :]
            other = s_scr[64 + 8 * q : 72 + 8 * q, :]
            lo = jnp.where(core == 0, own, other)
            hi = jnp.where(core == 0, other, own)
            xx = lax.rem(q % 4 + 4 - lax.rem(col, 4), 4)
            zz = lax.rem(q // 4 + 2 - col // 4, 2)
            gl_ref[xx, zz, 0:8, :] = jnp.concatenate([lo[0:4], hi[0:4]], axis=0)
            gl_ref[xx, zz, 8:16, :] = jnp.concatenate([lo[4:8], hi[4:8]], axis=0)


def sum_spread_kernel(x_ref, out_ref):
    total = x_ref[0]
    for k in range(1, x_ref.shape[0]):
        total = total + x_ref[k]
    for k in range(out_ref.shape[0]):
        out_ref[k] = total


def sum_final_kernel(x_ref, out_ref, bias_ref):
    total = x_ref[0]
    for k in range(1, x_ref.shape[0]):
        total = total + x_ref[k]
    total = total * (1.0 / 512)
    for k in range(out_ref.shape[0]):
        out_ref[k] = total[:C]
    bias_ref[...] = total[C : C + 1]


def join_kernel(own_ref, other_ref, out_ref):
    core = core_index()
    for k in range(16):
        own = own_ref[k]
        other = other_ref[k]
        out_ref[C * k : C * k + C, :] = jnp.where(core == 0, own, other)
        out_ref[512 + C * k : 512 + C * k + C, :] = jnp.where(core == 0, other, own)


def whole(shape):
    return pl.BlockSpec(shape, lambda n: (0,) * len(shape))


def rows_of(shape):
    return pl.BlockSpec(shape, lambda n: (n, 0))


def cols_of(shape):
    return pl.BlockSpec(shape, lambda n: (0, n))


def call(kernel, ins, outs, scratch, flops, nbytes, steps=4):
    return pl.pallas_call(
        kernel,
        grid=(steps,),
        in_specs=ins,
        out_specs=[spec for _, _, spec in outs],
        out_shape=[pltpu.HBM(s, d) if d == BF16 else jax.ShapeDtypeStruct(s, d) for s, d, _ in outs],
        scratch_shapes=[pltpu.VMEM(s, d) for s, d in scratch],
        cost_estimate=pl.CostEstimate(flops=flops, bytes_accessed=nbytes, transcendentals=0),
        compiler_params=pltpu.CompilerParams(vmem_limit_bytes=40 << 20),
    )


LEFT = whole((4, 16, IC))
RIGHT = whole((16, 4, JE))
WHOLE_G = whole((IJ, Z))
WEIGHT = whole((CE, Z))
grad_outer_call = call(
    grad_outer_kernel,
    [rows_of((256, Z)), WEIGHT],
    [((IC, JE), BF16, rows_of((128, JE)))] * 2,
    [((CE, Z), F32), ((CE, 2 * Z), BF16), ((CE, 256), F32)],
    10**9, 5 << 20)
grad_right_call = call(
    grad_right_kernel,
    [LEFT, LEFT, cols_of((IC, 512)), cols_of((IC, 512))],
    [((4, 4, 4, JE), F32, whole((4, 4, 4, JE)))] * 2,
    [((S, IC), F32), ((2 * S, IC), BF16), ((JE, S), F32)],
    10**9, 5 << 20)
outer_call = call(
    outer_kernel,
    [LEFT, LEFT, RIGHT, RIGHT, WHOLE_G],
    [((CE, IJ), BF16, rows_of((256, IJ)))] * 2 + [((JE, S), BF16, rows_of((512, S)))] * 2
    + [((16, 40, Z), F32, whole((16, 40, Z)))] * 2,
    [((S, IC), F32), ((IC, 2 * S), BF16), ((S, JE), F32), ((JE, S), F32), ((2, IC, 256), F32), ((IJ, 2 * Z), BF16), ((CE, Z), F32)],
    2 * 10**9, 7 << 20)
finish_call = call(
    finish_kernel,
    [cols_of((CE, 256))] * 2 + [WEIGHT, whole((1, Z))] + [cols_of((IC, 512))] * 2 + [rows_of((512, S))] * 2,
    [((IJ, Z), F32, rows_of((256, Z))), ((4, 2, 16, IC), F32, whole((4, 2, 16, IC)))],
    [((CE, Z), F32), ((2 * Z, CE), BF16), ((IC, S), F32), ((S, IC), F32)],
    2 * 10**9, 9 << 20)
join_call = call(join_kernel, [whole((16, C, Z))] * 2, [((CE, Z), F32, WEIGHT)], [], 10**5, 1 << 20, 1)
spread_call = call(sum_spread_kernel, [whole((16, 40, Z))], [((8, 40, Z), F32, whole((8, 40, Z)))], [], 10**5, 1 << 19, 1)
final_call = call(
    sum_final_kernel,
    [whole((8, 40, Z))],
    [((16, C, Z), F32, whole((16, C, Z))), ((1, Z), F32, whole((1, Z)))],
    [], 10**5, 1 << 19, 1)


def rid(z, y, c):
    return (z * 4 + y) * 2 + c


CORE = [(r, r ^ 1) for r in range(32)]
YZ = [[rid(z, y, c) for z in range(4) for y in range(4)] for c in range(2)]
XY = [[rid(z, y, c) * 8 + h * 4 + x for y in range(4) for x in range(4)] for z in range(4) for h in range(2) for c in range(2)]
Z8 = [[rid(z, y, c) * 8 + h * 4 + x for z in range(4) for h in range(2)] for y in range(4) for x in range(4) for c in range(2)]
BOTH = ("row", "col")
R4 = range(4)
Y_PERMS = [[(rid(z, y, c), rid(z, (y + k) % 4, c)) for z in R4 for y in R4 for c in range(2)] for k in (1, 2, 3)]
Z_PERMS = [[(rid(z, y, c), rid((z + k) % 4, y, c)) for z in R4 for y in R4 for c in range(2)] for k in (1, 2, 3)]
X_PERMS = [[(h * 4 + x, h * 4 + (x + k) % 4) for h in range(2) for x in R4] for k in (1, 2, 3)]
H_PERM = [(q, q ^ 4) for q in range(8)]


def spread(x, n, axis, groups=None):
    copies = jnp.broadcast_to(x[None], (n,) + x.shape)
    return lax.all_to_all(copies, axis, 0, 0, axis_index_groups=groups)


def body(left, right, w_out, b_out, pair_grad):
    g = pair_grad.reshape(IJ, Z)
    right_own = spread(right, 16, "row", YZ)
    left_near = jnp.stack([left] + [lax.ppermute(left, "col", p) for p in X_PERMS])
    left_far = lax.ppermute(left_near, "col", H_PERM)
    goh, gol = grad_outer_call(g, w_out)
    right_other = lax.ppermute(right_own, "row", CORE)
    oh, ol, bh, bl, gw_own, gw_other = outer_call(left_near, left_far, right_own, right_other, g)
    gw = gw_own + lax.ppermute(gw_other, "row", CORE)
    gw = lax.all_to_all(gw, BOTH, 0, 0, axis_index_groups=XY)
    (gw,) = spread_call(gw)
    gw = lax.all_to_all(gw, BOTH, 0, 0, axis_index_groups=Z8)
    gw, grad_bias = final_call(gw)
    gw_own = lax.all_to_all(gw, BOTH, 0, 0, axis_index_groups=XY)
    gw_other = lax.ppermute(gw_own, "row", CORE)
    (grad_weight,) = join_call(gw_own, gw_other)
    gr_own, gr_other = grad_right_call(left_near, left_far, goh, gol)
    gr = gr_own + lax.ppermute(gr_other, "row", CORE)
    gr = gr[0] + sum(lax.ppermute(gr[k + 1], "row", p) for k, p in enumerate(Y_PERMS))
    grad_right = gr[0] + sum(lax.ppermute(gr[k + 1], "row", p) for k, p in enumerate(Z_PERMS))
    pair_out, gl = finish_call(oh, ol, w_out, b_out.reshape(1, Z), goh, gol, bh, bl)
    gl = gl[0] + sum(lax.ppermute(gl[k + 1], "col", p) for k, p in enumerate(X_PERMS))
    grad_left = gl[0] + lax.ppermute(gl[1], "col", H_PERM)
    return (pair_out.reshape(TI, TJ, Z), grad_left, grad_right, grad_weight, grad_bias.reshape(Z))


def solution(mesh):
    placed = (P("col", "row"), P("row", "col"), P(), P(), P("row", "col", None))
    return jax.shard_map(
        body,
        mesh=mesh,
        in_specs=placed,
        out_specs=(P("row", "col", None), P("col", "row"), P("row", "col"), P(), P()),
        check_vma=False,
    )
```

time: 771 us -> 111 us (0.14)
  the two profiles are of different devices: /device:TPU:32 before, /device:TPU:1 now
where the time goes in v2:
time: 111 us; the launch traced here: 110 us
  starting transfers between devices  54.3 us (49%)
  Pallas kernels  20.7 us (19%)
  waiting for transfers between devices  17.6 us (16%)
  local copies, waits for them, and re-layouts  13.8 us (12%)
  other arithmetic  3.03 us (3%)
    unnamed x26, local copies, waits for them, and re-layouts  12.1 us
    all_to_all x1, starting transfers between devices, spread(): return lax.all_to_all(copies, axis, 0, 0, axis_index_groups=groups)  11.7 us
    ppermute x6, starting transfers between devices, body(): lax.ppermute(gr[k + 1], 'row', p)  8.53 us
    pallas_call x1, Pallas kernels, body(): outer_call(left_near, left_far, right_own, right_other, g)  6.46 us
    all_to_all x1, starting transfers between devices, body(): gw = lax.all_to_all(gw, BOTH, 0, 0, axis_index_groups=Z8)  6.36 us
    all_to_all x1, waiting for transfers between devices, body(): gw_own = lax.all_to_all(gw, BOTH, 0, 0, axis_index_groups=XY)  6.34 us
    all_to_all x1, starting transfers between devices, body(): gw_own = lax.all_to_all(gw, BOTH, 0, 0, axis_index_groups=XY)  5.28 us
    all_to_all x1, waiting for transfers between devices, body(): gw = lax.all_to_all(gw, BOTH, 0, 0, axis_index_groups=Z8)  4.74 us
  transfers between devices with their start and end apart: 22, of which 7 were waited for; matrix products, arithmetic and copies ran while one was open for 2% of the time, Pallas kernels for 18%

profile of v2, /device:TPU:1, one launch (start us, length us, event | category | flops | bytes accessed | tf_op | source)
XLA Modules:
  0.0 110.4 jit_solution(16554871731323926220)
XLA Ops:
  0.6 1.7 %broadcast_in_dim.2 = f32[16,4,2048]{2,1,0:T(4,128)} broadcast(f32[4,2048]{1,0:T(4,128)} %param.6), dimensions={1,2} | broadcast | bytes 557056 | tf_op jit(solution)/shard_map/broadcast_in_dim | solution.py:306
  2.3 11.7 %all-to-all-start = ((f32[16,4,2048]{2,1,0:T(4,128)}), f32[16,4,2048]{2,1,0:T(4,128)S(1)}, u32[]{:S(2)}, u32[]{:S(2)}) async-start(f32[16,4,2048]{2,1,0:T(4,128)} %broadcast_in_dim.2), calls=%async_computation | async-start | bytes 1048576 | tf_op jit(solution)/shard_map/all_to_all | solution.py:307
  14.0 2.6 %collective-permute-start.2 = (f32[16,512]{1,0:T(8,128)}, f32[16,512]{1,0:T(8,128)S(1)}, u32[]{:S(2)}, u32[]{:S(2)}) collective-permute-start(f32[16,512]{1,0:T(8,128)} %param.5), channel_id=1, source_target_pairs={{0,3},{1,0},{2,1},{3,2},{4,7},{5,4},{6,5},{7,6},{8,11},{9,8},{10,9... | collective-permute-start | bytes 98312 | tf_op jit(solution)/shard_map/ppermute | solution.py:313
  16.6 0.5 collective-permute-start.1
  17.1 0.6 collective-permute-start
  17.7 0.2 collective-permute-done.2
  17.9 3.4 %collective-permute-done.1 = f32[16,512]{1,0:T(8,128)S(1)} collective-permute-done((f32[16,512]{1,0:T(8,128)}, f32[16,512]{1,0:T(8,128)S(1)}, u32[]{:S(2)}, u32[]{:S(2)}) %collective-permute-start.1) | collective-permute-done | bytes 32800 | tf_op jit(solution)/shard_map/ppermute | solution.py:313
  21.4 0.3 collective-permute-done
  21.6 0.8 pad_maximum_fusion.near_ref
  22.4 0.9 collective-permute-start.3
  23.3 1.0 copy-done.6
  24.4 1.0 copy-done.11
  25.4 4.1 %shard_map.93 = (bf16[512,2048]{1,0:T(8,128)(2,1)}, bf16[512,2048]{1,0:T(8,128)(2,1)}) custom-call(f32[1024,128]{1,0:T(8,128)S(1)} %bitcast.43, f32[1024,128]{1,0:T(8,128)S(1)} %copy-done.6), custom_call_target="tpu_custom_call" | custom-call | flops 1000000000 | bytes 5242880 | tf_op jit(solution)/shard_map/pallas_call | solution.py:315
  29.5 0.0 collective-permute-done.3.far_ref
  29.5 1.6 %copy-done = bf16[512,2048]{1,0:T(8,128)(2,1)S(1)} copy-done((bf16[512,2048]{1,0:T(8,128)(2,1)S(1)}, bf16[512,2048]{1,0:T(8,128)(2,1)}, u32[]{:S(2)}) %copy-start) | copy-done | bytes 2097176
  31.1 1.6 %copy-done.2 = bf16[512,2048]{1,0:T(8,128)(2,1)S(1)} copy-done((bf16[512,2048]{1,0:T(8,128)(2,1)S(1)}, bf16[512,2048]{1,0:T(8,128)(2,1)}, u32[]{:S(2)}) %copy-start.2) | copy-done | bytes 2097176
  32.7 3.1 %shard_map.95 = (f32[4,4,4,2048]{3,2,1,0:T(4,128)S(1)}, f32[4,4,4,2048]{3,2,1,0:T(4,128)S(1)}) custom-call(f32[4,16,512]{2,1,0:T(8,128)S(1)} %pad_maximum_fusion.near_ref, f32[4,16,512]{2,1,0:T(8,128)S(1)} %collective-permute-done.3.far_ref, bf16[512,2048]{1,0:T(8,128)(2,1)S(1)} %copy-done, bf16[512,2048]{1,0:T(8,128)(2,1)S(1)} %copy-done.2), custom_call_target="tpu_custom_call" | custom-call | flops 1000000000 | bytes 5242880 | tf_op jit(solution)/shard_map/pallas_call | solution.py:326
  35.9 0.0 copy-start.12
  35.9 2.6 %collective-permute-start.9 = (f32[4,4,4,2048]{3,2,1,0:T(4,128)S(1)}, f32[4,4,4,2048]{3,2,1,0:T(4,128)S(1)}, u32[]{:S(2)}, u32[]{:S(2)}) collective-permute-start(f32[4,4,4,2048]{3,2,1,0:T(4,128)S(1)} %get-tuple-element.28), channel_id=1, source_target_pairs={{0,8},{8,0},{16,24},{24,16},{32,40},{40,32},{48,56},{56,48},{64,72... | collective-permute-start | bytes 1572872 | tf_op jit(solution)/shard_map/ppermute | solution.py:327
  38.5 0.0 all-to-all-done.own_ref
  38.5 0.1 collective-permute-start.4
  38.6 1.4 %collective-permute-done.9 = f32[4,4,4,2048]{3,2,1,0:T(4,128)S(1)} collective-permute-done((f32[4,4,4,2048]{3,2,1,0:T(4,128)S(1)}, f32[4,4,4,2048]{3,2,1,0:T(4,128)S(1)}, u32[]{:S(2)}, u32[]{:S(2)}) %collective-permute-start.9) | collective-permute-done | bytes 524320 | tf_op jit(solution)/shard_map/ppermute | solution.py:327
  40.0 0.1 add.40
  40.2 2.9 %collective-permute-start.12 = (f32[4,4,2048]{2,1,0:T(4,128)S(1)}, f32[4,4,2048]{2,1,0:T(4,128)S(1)}, u32[]{:S(2)}, u32[]{:S(2)}) collective-permute-start(f32[4,4,2048]{2,1,0:T(4,128)S(1)} %get-tuple-element.34), channel_id=1, source_target_pairs={{0,48},{8,56},{16,0},{24,8},{32,16},{40,24},{48,32},{56,40},{64,11... | collective-permute-start | bytes 393224 | tf_op jit(solution)/shard_map/ppermute | solution.py:328
  43.1 0.0 collective-permute-start.10
  43.1 1.8 %collective-permute-start.11 = (f32[4,4,2048]{2,1,0:T(4,128)S(1)}, f32[4,4,2048]{2,1,0:T(4,128)S(1)}, u32[]{:S(2)}, u32[]{:S(2)}) collective-permute-start(f32[4,4,2048]{2,1,0:T(4,128)S(1)} %get-tuple-element.33), channel_id=1, source_target_pairs={{0,32},{8,40},{16,48},{24,56},{32,0},{40,8},{48,16},{56,24},{64,96... | collective-permute-start | bytes 393224 | tf_op jit(solution)/shard_map/ppermute | solution.py:328
  44.8 0.0 collective-permute-done.4.other_ref
  44.8 6.5 %shard_map.92 = (bf16[1024,1024]{1,0:T(8,128)(2,1)}, bf16[1024,1024]{1,0:T(8,128)(2,1)}, bf16[2048,128]{1,0:T(8,128)(2,1)}, bf16[2048,128]{1,0:T(8,128)(2,1)}, f...) custom-call(f32[4,16,512]{2,1,0:T(8,128)S(1)} %pad_maximum_fusion.near_ref, ...), custom_call_target="tpu_custom_call" | custom-call | flops 2000000000 | bytes 7340032 | tf_op jit(solution)/shard_map/pallas_call | solution.py:317
  51.3 1.3 %collective-permute-start.16 = (f32[16,40,128]{2,1,0:T(8,128)S(1)}, f32[16,40,128]{2,1,0:T(8,128)S(1)}, u32[]{:S(2)}, u32[]{:S(2)}) collective-permute-start(f32[16,40,128]{2,1,0:T(8,128)S(1)} %get-tuple-element.30), channel_id=1, source_target_pairs={{0,8},{8,0},{16,24},{24,16},{32,40},{40,32},{48,56},{56,48},{64,72... | collective-permute-start | bytes 983048 | tf_op jit(solution)/shard_map/ppermute | solution.py:318
  52.6 0.0 collective-permute-done.12
  52.6 0.0 collective-permute-done.10
  52.6 0.0 collective-permute-done.11
  52.6 0.1 fusion
  52.7 1.2 %collective-permute-done.16 = f32[16,40,128]{2,1,0:T(8,128)S(1)} collective-permute-done((f32[16,40,128]{2,1,0:T(8,128)S(1)}, f32[16,40,128]{2,1,0:T(8,128)S(1)}, u32[]{:S(2)}, u32[]{:S(2)}) %collective-permute-start.16) | collective-permute-done | bytes 327712 | tf_op jit(solution)/shard_map/ppermute | solution.py:318
  53.8 0.8 add.47
  54.6 3.8 %all-to-all-start.1 = ((f32[16,40,128]{2,1,0:T(8,128)}), f32[16,40,128]{2,1,0:T(8,128)S(1)}, u32[]{:S(2)}, u32[]{:S(2)}) async-start(f32[16,40,128]{2,1,0:T(8,128)} %add.47), calls=%async_computation.1 | async-start | bytes 655360 | tf_op jit(solution)/shard_map/all_to_all | solution.py:319
  58.5 1.6 %copy-done.3 = bf16[512,2048]{1,0:T(8,128)(2,1)S(1)} copy-done((bf16[512,2048]{1,0:T(8,128)(2,1)S(1)}, bf16[512,2048]{1,0:T(8,128)(2,1)}, u32[]{:S(2)}) %copy-start.3) | copy-done | bytes 2097176
  60.1 1.6 %copy-done.4 = bf16[1024,1024]{1,0:T(8,128)(2,1)S(1)} copy-done((bf16[1024,1024]{1,0:T(8,128)(2,1)S(1)}, bf16[1024,1024]{1,0:T(8,128)(2,1)}, u32[]{:S(2)}) %copy-start.4) | copy-done | bytes 2097176
  61.7 1.6 %copy-done.5 = bf16[1024,1024]{1,0:T(8,128)(2,1)S(1)} copy-done((bf16[1024,1024]{1,0:T(8,128)(2,1)S(1)}, bf16[1024,1024]{1,0:T(8,128)(2,1)}, u32[]{:S(2)}) %copy-start.5) | copy-done | bytes 2097176
  63.3 1.0 copy-done.8
  64.3 1.0 copy-done.9
  65.4 4.7 %shard_map.94 = (f32[1024,128]{1,0:T(8,128)}, f32[4,2,16,512]{3,2,1,0:T(8,128)S(1)}) custom-call(bf16[1024,1024]{1,0:T(8,128)(2,1)S(1)} %copy-done.4, bf16[1024,1024]{1,0:T(8,128)(2,1)S(1)} %copy-done.5, f32[1024,128]{1,0:T(8,128)S(1)} %copy-done.7, f32[1,128]{1,0:T(1,128)S(1)} %bitcast.42, bf16[512,2048]{1,0:T(8,128)(2,1)S(1)} %copy-done.1, ...), custom_call_target="tpu_custom_call" | custom-call | flops 2000000000 | bytes 9437184 | tf_op jit(solution)/shard_map/pallas_call | solution.py:330
  70.1 2.6 %collective-permute-start.7 = (f32[2,16,512]{2,1,0:T(8,128)S(1)}, f32[2,16,512]{2,1,0:T(8,128)S(1)}, u32[]{:S(2)}, u32[]{:S(2)}) collective-permute-start(f32[2,16,512]{2,1,0:T(8,128)S(1)} %get-tuple-element.37), channel_id=1, source_target_pairs={{0,3},{1,0},{2,1},{3,2},{4,7},{5,4},{6,5},{7,6},{8,11},{9,8},{10,9... | collective-permute-start | bytes 196616 | tf_op jit(solution)/shard_map/ppermute | solution.py:331
  72.7 0.0 collective-permute-start.5
  72.7 1.8 %collective-permute-start.6 = (f32[2,16,512]{2,1,0:T(8,128)S(1)}, f32[2,16,512]{2,1,0:T(8,128)S(1)}, u32[]{:S(2)}, u32[]{:S(2)}) collective-permute-start(f32[2,16,512]{2,1,0:T(8,128)S(1)} %get-tuple-element.36), channel_id=1, source_target_pairs={{0,2},{1,3},{2,0},{3,1},{4,6},{5,7},{6,4},{7,5},{8,10},{9,11},{10,... | collective-permute-start | bytes 196616 | tf_op jit(solution)/shard_map/ppermute | solution.py:331
  74.5 0.0 all-to-all-done.1.x_ref
  74.5 0.7 shard_map.96
  75.2 6.4 %all-to-all-start.2 = ((f32[8,40,128]{2,1,0:T(8,128)}), f32[8,40,128]{2,1,0:T(8,128)S(1)}, u32[]{:S(2)}, u32[]{:S(2)}) async-start(f32[8,40,128]{2,1,0:T(8,128)} %shard_map.96), calls=%async_computation.2 | async-start | bytes 327680 | tf_op jit(solution)/shard_map/all_to_all | solution.py:321
  81.6 3.6 %collective-permute-start.15 = (f32[4,2048]{1,0:T(4,128)S(1)}, f32[4,2048]{1,0:T(4,128)S(1)}, u32[]{:S(2)}, u32[]{:S(2)}) collective-permute-start(f32[4,2048]{1,0:T(4,128)S(1)} %get-tuple-element.40), channel_id=1, source_target_pairs={{0,192},{8,200},{16,208},{24,216},{32,224},{40,232},{48,240},{56,2... | collective-permute-start | bytes 98312 | tf_op jit(solution)/shard_map/ppermute | solution.py:329
  85.2 0.0 collective-permute-start.13
  85.2 4.7 %all-to-all-done.2.x_ref = f32[8,40,128]{2,1,0:T(8,128)S(1)} async-done(((f32[8,40,128]{2,1,0:T(8,128)}), f32[8,40,128]{2,1,0:T(8,128)S(1)}, u32[]{:S(2)}, u32[]{:S(2)}) %all-to-all-start.2) | async-done | bytes 163872 | tf_op jit(solution)/shard_map/all_to_all | solution.py:321
  90.0 0.7 shard_map.97
  90.7 5.3 %all-to-all-start.3 = ((f32[16,32,128]{2,1,0:T(8,128)}), f32[16,32,128]{2,1,0:T(8,128)S(1)}, u32[]{:S(2)}, u32[]{:S(2)}) async-start(f32[16,32,128]{2,1,0:T(8,128)} %get-tuple-element.31), calls=%async_computation.3 | async-start | bytes 524288 | tf_op jit(solution)/shard_map/all_to_all | solution.py:323
  96.0 0.0 collective-permute-done.7
  96.0 0.3 collective-permute-start.14
  96.3 0.9 collective-permute-start.8
  97.2 6.3 %all-to-all-done.3.own_ref = f32[16,32,128]{2,1,0:T(8,128)S(1)} async-done(((f32[16,32,128]{2,1,0:T(8,128)}), f32[16,32,128]{2,1,0:T(8,128)S(1)}, u32[]{:S(2)}, u32[]{:S(2)}) %all-to-all-start.3) | async-done | bytes 262176 | tf_op jit(solution)/shard_map/all_to_all | solution.py:323
  103.5 4.7 %collective-permute-start.17 = (f32[16,32,128]{2,1,0:T(8,128)S(1)}, f32[16,32,128]{2,1,0:T(8,128)S(1)}, u32[]{:S(2)}, u32[]{:S(2)}) collective-permute-start(f32[16,32,128]{2,1,0:T(8,128)S(1)} %all-to-all-done.3.own_ref), channel_id=1, source_target_pairs={{0,8},{8,0},{16,24},{24,16},{32,40},{40,32},{48,56},{56,48},{64,72... | collective-permute-start | bytes 786440 | tf_op jit(solution)/shard_map/ppermute | solution.py:324
  108.2 0.0 collective-permute-done.15
  108.2 0.0 collective-permute-done.13
  108.2 0.6 fusion.1
  108.9 0.6 fusion.2
  109.5 0.0 collective-permute-done.17.other_ref
  109.5 0.8 shard_map.98
  (25 shorter events, 0.1 us)
Async XLA Ops:
  2.3 36.2 %all-to-all-start = ((f32[16,4,2048]{2,1,0:T(4,128)}), f32[16,4,2048]{2,1,0:T(4,128)S(1)}, u32[]{:S(2)}, u32[]{:S(2)}) async-start(f32[16,4,2048]{2,1,0:T(4,128)} %broadcast_in_dim.2), calls=%async_computation | async-start | bytes 1048576 | tf_op jit(solution)/shard_map/all_to_all | solution.py:307
  14.0 3.9 %collective-permute-start.2 = (f32[16,512]{1,0:T(8,128)}, f32[16,512]{1,0:T(8,128)S(1)}, u32[]{:S(2)}, u32[]{:S(2)}) collective-permute-start(f32[16,512]{1,0:T(8,128)} %param.5), channel_id=1, source_target_pairs={{0,3},{1,0},{2,1},{3,2},{4,7},{5,4},{6,5},{7,6},{8,11},{9,8},{10,9... | collective-permute-start | bytes 98312 | tf_op jit(solution)/shard_map/ppermute | solution.py:313
  16.6 4.8 %collective-permute-start.1 = (f32[16,512]{1,0:T(8,128)}, f32[16,512]{1,0:T(8,128)S(1)}, u32[]{:S(2)}, u32[]{:S(2)}) collective-permute-start(f32[16,512]{1,0:T(8,128)} %param.5), channel_id=1, source_target_pairs={{0,2},{1,3},{2,0},{3,1},{4,6},{5,7},{6,4},{7,5},{8,10},{9,11},{10,... | collective-permute-start | bytes 98312 | tf_op jit(solution)/shard_map/ppermute | solution.py:313
  17.1 4.5 %collective-permute-start = (f32[16,512]{1,0:T(8,128)}, f32[16,512]{1,0:T(8,128)S(1)}, u32[]{:S(2)}, u32[]{:S(2)}) collective-permute-start(f32[16,512]{1,0:T(8,128)} %param.5), channel_id=1, source_target_pairs={{0,1},{1,2},{2,3},{3,0},{4,5},{5,6},{6,7},{7,4},{8,9},{9,10},{10,1... | collective-permute-start | bytes 98312 | tf_op jit(solution)/shard_map/ppermute | solution.py:313
  22.4 7.2 %collective-permute-start.3 = (f32[4,16,512]{2,1,0:T(8,128)S(1)}, f32[4,16,512]{2,1,0:T(8,128)S(1)}, u32[]{:S(2)}, u32[]{:S(2)}) collective-permute-start(f32[4,16,512]{2,1,0:T(8,128)S(1)} %pad_maximum_fusion.near_ref), channel_id=1, source_target_pairs={{0,4},{1,5},{2,6},{3,7},{4,0},{5,1},{6,2},{7,3},{8,12},{9,13},{10,... | collective-permute-start | bytes 393224 | tf_op jit(solution)/shard_map/ppermute | solution.py:314
  23.3 1.0 copy-start.6
  24.4 1.0 copy-start.11
  29.5 1.6 %copy-start = (bf16[512,2048]{1,0:T(8,128)(2,1)S(1)}, bf16[512,2048]{1,0:T(8,128)(2,1)}, u32[]{:S(2)}) copy-start(bf16[512,2048]{1,0:T(8,128)(2,1)} %get-tuple-element.21.goh_ref) | copy-start | bytes 6291460
  31.1 1.6 %copy-start.2 = (bf16[512,2048]{1,0:T(8,128)(2,1)S(1)}, bf16[512,2048]{1,0:T(8,128)(2,1)}, u32[]{:S(2)}) copy-start(bf16[512,2048]{1,0:T(8,128)(2,1)} %get-tuple-element.22.gol_ref) | copy-start | bytes 6291460
  35.9 9.0 %copy-start.12 = (f32[16,64,128]{2,1,0:T(8,128)S(1)}, f32[16,64,128]{2,1,0:T(8,128)}, u32[]{:S(2)}) copy-start(f32[16,64,128]{2,1,0:T(8,128)} %param.9) | copy-start | bytes 1572868
  35.9 4.2 %collective-permute-start.9 = (f32[4,4,4,2048]{3,2,1,0:T(4,128)S(1)}, f32[4,4,4,2048]{3,2,1,0:T(4,128)S(1)}, u32[]{:S(2)}, u32[]{:S(2)}) collective-permute-start(f32[4,4,4,2048]{3,2,1,0:T(4,128)S(1)} %get-tuple-element.28), channel_id=1, source_target_pairs={{0,8},{8,0},{16,24},{24,16},{32,40},{40,32},{48,56},{56,48},{64,72... | collective-permute-start | bytes 1572872 | tf_op jit(solution)/shard_map/ppermute | solution.py:327
  38.5 6.3 %collective-permute-start.4 = (f32[16,4,2048]{2,1,0:T(4,128)S(1)}, f32[16,4,2048]{2,1,0:T(4,128)S(1)}, u32[]{:S(2)}, u32[]{:S(2)}) collective-permute-start(f32[16,4,2048]{2,1,0:T(4,128)S(1)} %all-to-all-done.own_ref), channel_id=1, source_target_pairs={{0,8},{8,0},{16,24},{24,16},{32,40},{40,32},{48,56},{56,48},{64,72... | collective-permute-start | bytes 1572872 | tf_op jit(solution)/shard_map/ppermute | solution.py:316
  40.2 12.4 %collective-permute-start.12 = (f32[4,4,2048]{2,1,0:T(4,128)S(1)}, f32[4,4,2048]{2,1,0:T(4,128)S(1)}, u32[]{:S(2)}, u32[]{:S(2)}) collective-permute-start(f32[4,4,2048]{2,1,0:T(4,128)S(1)} %get-tuple-element.34), channel_id=1, source_target_pairs={{0,48},{8,56},{16,0},{24,8},{32,16},{40,24},{48,32},{56,40},{64,11... | collective-permute-start | bytes 393224 | tf_op jit(solution)/shard_map/ppermute | solution.py:328
  43.1 9.5 %collective-permute-start.10 = (f32[4,4,2048]{2,1,0:T(4,128)S(1)}, f32[4,4,2048]{2,1,0:T(4,128)S(1)}, u32[]{:S(2)}, u32[]{:S(2)}) collective-permute-start(f32[4,4,2048]{2,1,0:T(4,128)S(1)} %get-tuple-element.35), channel_id=1, source_target_pairs={{0,16},{8,24},{16,32},{24,40},{32,48},{40,56},{48,0},{56,8},{64,80... | collective-permute-start | bytes 393224 | tf_op jit(solution)/shard_map/ppermute | solution.py:328
  43.1 9.5 %collective-permute-start.11 = (f32[4,4,2048]{2,1,0:T(4,128)S(1)}, f32[4,4,2048]{2,1,0:T(4,128)S(1)}, u32[]{:S(2)}, u32[]{:S(2)}) collective-permute-start(f32[4,4,2048]{2,1,0:T(4,128)S(1)} %get-tuple-element.33), channel_id=1, source_target_pairs={{0,32},{8,40},{16,48},{24,56},{32,0},{40,8},{48,16},{56,24},{64,96... | collective-permute-start | bytes 393224 | tf_op jit(solution)/shard_map/ppermute | solution.py:328
  44.8 13.6 %copy-start.7 = (f32[1024,128]{1,0:T(8,128)S(1)}, f32[1024,128]{1,0:T(8,128)}, u32[]{:S(2)}) copy-start(f32[1024,128]{1,0:T(8,128)} %w_ref.3) | copy-start | bytes 1572868
  51.3 7.2 %copy-start.1 = (bf16[512,2048]{1,0:T(8,128)(2,1)S(1)}, bf16[512,2048]{1,0:T(8,128)(2,1)}, u32[]{:S(2)}) copy-start(bf16[512,2048]{1,0:T(8,128)(2,1)} %get-tuple-element.21.goh_ref) | copy-start | bytes 6291460
  51.3 7.2 %copy-start.10 = (f32[128]{0:T(128)S(1)}, f32[128]{0:T(128)}, u32[]{:S(2)}) copy-start(f32[128]{0:T(128)} %param.8) | copy-start | bytes 1540
  51.3 2.5 %collective-permute-start.16 = (f32[16,40,128]{2,1,0:T(8,128)S(1)}, f32[16,40,128]{2,1,0:T(8,128)S(1)}, u32[]{:S(2)}, u32[]{:S(2)}) collective-permute-start(f32[16,40,128]{2,1,0:T(8,128)S(1)} %get-tuple-element.30), channel_id=1, source_target_pairs={{0,8},{8,0},{16,24},{24,16},{32,40},{40,32},{48,56},{56,48},{64,72... | collective-permute-start | bytes 983048 | tf_op jit(solution)/shard_map/ppermute | solution.py:318
  54.6 19.9 %all-to-all-start.1 = ((f32[16,40,128]{2,1,0:T(8,128)}), f32[16,40,128]{2,1,0:T(8,128)S(1)}, u32[]{:S(2)}, u32[]{:S(2)}) async-start(f32[16,40,128]{2,1,0:T(8,128)} %add.47), calls=%async_computation.1 | async-start | bytes 655360 | tf_op jit(solution)/shard_map/all_to_all | solution.py:319
  58.5 1.6 %copy-start.3 = (bf16[512,2048]{1,0:T(8,128)(2,1)S(1)}, bf16[512,2048]{1,0:T(8,128)(2,1)}, u32[]{:S(2)}) copy-start(bf16[512,2048]{1,0:T(8,128)(2,1)} %get-tuple-element.22.gol_ref) | copy-start | bytes 6291460
  60.1 1.6 %copy-start.4 = (bf16[1024,1024]{1,0:T(8,128)(2,1)S(1)}, bf16[1024,1024]{1,0:T(8,128)(2,1)}, u32[]{:S(2)}) copy-start(bf16[1024,1024]{1,0:T(8,128)(2,1)} %get-tuple-element.19.oh_ref) | copy-start | bytes 6291460
  61.7 1.6 %copy-start.5 = (bf16[1024,1024]{1,0:T(8,128)(2,1)S(1)}, bf16[1024,1024]{1,0:T(8,128)(2,1)}, u32[]{:S(2)}) copy-start(bf16[1024,1024]{1,0:T(8,128)(2,1)} %get-tuple-element.20.ol_ref) | copy-start | bytes 6291460
  63.3 1.0 copy-start.8
  64.3 1.0 copy-start.9
  70.1 25.9 %collective-permute-start.7 = (f32[2,16,512]{2,1,0:T(8,128)S(1)}, f32[2,16,512]{2,1,0:T(8,128)S(1)}, u32[]{:S(2)}, u32[]{:S(2)}) collective-permute-start(f32[2,16,512]{2,1,0:T(8,128)S(1)} %get-tuple-element.37), channel_id=1, source_target_pairs={{0,3},{1,0},{2,1},{3,2},{4,7},{5,4},{6,5},{7,6},{8,11},{9,8},{10,9... | collective-permute-start | bytes 196616 | tf_op jit(solution)/shard_map/ppermute | solution.py:331
  72.7 23.5 %collective-permute-start.5 = (f32[2,16,512]{2,1,0:T(8,128)S(1)}, f32[2,16,512]{2,1,0:T(8,128)S(1)}, u32[]{:S(2)}, u32[]{:S(2)}) collective-permute-start(f32[2,16,512]{2,1,0:T(8,128)S(1)} %get-tuple-element.38), channel_id=1, source_target_pairs={{0,1},{1,2},{2,3},{3,0},{4,5},{5,6},{6,7},{7,4},{8,9},{9,10},{10,1... | collective-permute-start | bytes 196616 | tf_op jit(solution)/shard_map/ppermute | solution.py:331
  72.7 23.5 %collective-permute-start.6 = (f32[2,16,512]{2,1,0:T(8,128)S(1)}, f32[2,16,512]{2,1,0:T(8,128)S(1)}, u32[]{:S(2)}, u32[]{:S(2)}) collective-permute-start(f32[2,16,512]{2,1,0:T(8,128)S(1)} %get-tuple-element.36), channel_id=1, source_target_pairs={{0,2},{1,3},{2,0},{3,1},{4,6},{5,7},{6,4},{7,5},{8,10},{9,11},{10,... | collective-permute-start | bytes 196616 | tf_op jit(solution)/shard_map/ppermute | solution.py:331
  75.2 14.8 %all-to-all-start.2 = ((f32[8,40,128]{2,1,0:T(8,128)}), f32[8,40,128]{2,1,0:T(8,128)S(1)}, u32[]{:S(2)}, u32[]{:S(2)}) async-start(f32[8,40,128]{2,1,0:T(8,128)} %shard_map.96), calls=%async_computation.2 | async-start | bytes 327680 | tf_op jit(solution)/shard_map/all_to_all | solution.py:321
  81.6 26.7 %collective-permute-start.15 = (f32[4,2048]{1,0:T(4,128)S(1)}, f32[4,2048]{1,0:T(4,128)S(1)}, u32[]{:S(2)}, u32[]{:S(2)}) collective-permute-start(f32[4,2048]{1,0:T(4,128)S(1)} %get-tuple-element.40), channel_id=1, source_target_pairs={{0,192},{8,200},{16,208},{24,216},{32,224},{40,232},{48,240},{56,2... | collective-permute-start | bytes 98312 | tf_op jit(solution)/shard_map/ppermute | solution.py:329
  85.2 23.0 %collective-permute-start.13 = (f32[4,2048]{1,0:T(4,128)S(1)}, f32[4,2048]{1,0:T(4,128)S(1)}, u32[]{:S(2)}, u32[]{:S(2)}) collective-permute-start(f32[4,2048]{1,0:T(4,128)S(1)} %get-tuple-element.41), channel_id=1, source_target_pairs={{0,64},{8,72},{16,80},{24,88},{32,96},{40,104},{48,112},{56,120},{... | collective-permute-start | bytes 98312 | tf_op jit(solution)/shard_map/ppermute | solution.py:329
  90.7 12.8 %all-to-all-start.3 = ((f32[16,32,128]{2,1,0:T(8,128)}), f32[16,32,128]{2,1,0:T(8,128)S(1)}, u32[]{:S(2)}, u32[]{:S(2)}) async-start(f32[16,32,128]{2,1,0:T(8,128)} %get-tuple-element.31), calls=%async_computation.3 | async-start | bytes 524288 | tf_op jit(solution)/shard_map/all_to_all | solution.py:323
  96.0 12.2 %collective-permute-start.14 = (f32[4,2048]{1,0:T(4,128)S(1)}, f32[4,2048]{1,0:T(4,128)S(1)}, u32[]{:S(2)}, u32[]{:S(2)}) collective-permute-start(f32[4,2048]{1,0:T(4,128)S(1)} %get-tuple-element.39), channel_id=1, source_target_pairs={{0,128},{8,136},{16,144},{24,152},{32,160},{40,168},{48,176},{56,1... | collective-permute-start | bytes 98312 | tf_op jit(solution)/shard_map/ppermute | solution.py:329
  96.3 12.6 %collective-permute-start.8 = (f32[16,512]{1,0:T(8,128)S(1)}, f32[16,512]{1,0:T(8,128)S(1)}, u32[]{:S(2)}, u32[]{:S(2)}) collective-permute-start(f32[16,512]{1,0:T(8,128)S(1)} %slice_bitcast_fusion.11), channel_id=1, source_target_pairs={{0,4},{1,5},{2,6},{3,7},{4,0},{5,1},{6,2},{7,3},{8,12},{9,13},{10,... | collective-permute-start | bytes 98312 | tf_op jit(solution)/shard_map/ppermute | solution.py:332
  103.5 6.0 %collective-permute-start.17 = (f32[16,32,128]{2,1,0:T(8,128)S(1)}, f32[16,32,128]{2,1,0:T(8,128)S(1)}, u32[]{:S(2)}, u32[]{:S(2)}) collective-permute-start(f32[16,32,128]{2,1,0:T(8,128)S(1)} %all-to-all-done.3.own_ref), channel_id=1, source_target_pairs={{0,8},{8,0},{16,24},{24,16},{32,40},{40,32},{48,56},{56,48},{64,72... | collective-permute-start | bytes 786440 | tf_op jit(solution)/shard_map/ppermute | solution.py:324

commit v3 on v2

--- a/solution.py
+++ b/solution.py
@@ -4,6 +4,7 @@
 from jax.experimental import pallas as pl
 from jax.experimental.pallas import tpu as pltpu
 from jax.sharding import PartitionSpec as P
+
 
 C = 32
 Z = 128
@@ -41,13 +42,13 @@
     return lax.rem(lax.axis_index("row"), 2)
 
 
-def load_left(near_ref, far_ref, a_scr):
+def load_left(piece_refs, a_scr):
     core = core_index()
     col = lax.axis_index("col")
-    for ref, half in ((near_ref, col // 4), (far_ref, 1 - col // 4)):
-        for p in range(4):
+    for p, ref in enumerate(piece_refs):
+        for h, half in ((0, col // 4), (1, 1 - col // 4)):
             q = half * 4 + lax.rem(col + 4 - p, 4)
-            x = ref[p]
+            x = ref[h]
             lo = jnp.concatenate([x[0:4], x[8:12]], axis=0)
             hi = jnp.concatenate([x[4:8], x[12:16]], axis=0)
             a_scr[pl.ds(pl.multiple_of(q * 8, 8), 8), :] = jnp.where(core == 0, lo, hi)
@@ -80,12 +81,12 @@
                 gol_ref[row : row + C, 128 * ep : 128 * ep + 128] = lo
 
 
-def grad_right_kernel(near_ref, far_ref, goh_ref, gol_ref, own_ref, other_ref, a_scr, ac_scr, t_scr):
+def grad_right_kernel(l0_ref, l1_ref, l2_ref, l3_ref, goh_ref, gol_ref, own_ref, other_ref, a_scr, ac_scr, t_scr):
     n = pl.program_id(0)
 
     @pl.when(n == 0)
     def _():
-        load_left(near_ref, far_ref, a_scr)
+        load_left((l0_ref, l1_ref, l2_ref, l3_ref), a_scr)
         ah, al = split(a_scr[...])
         ac_scr[0:S, :] = ah
         ac_scr[S : 2 * S, :] = al
@@ -109,13 +110,13 @@
                 other_ref[yy, zz, :, 128 * m : 128 * m + 128] = block[64 + 4 * k : 68 + 4 * k]
 
 
-def outer_kernel(near_ref, far_ref, own_ref, other_ref, g_ref, oh_ref, ol_ref, bh_ref, bl_ref, gwo_ref, gwx_ref,
+def outer_kernel(l0_ref, l1_ref, l2_ref, l3_ref, own_ref, other_ref, g_ref, oh_ref, ol_ref, bh_ref, bl_ref, gwo_ref, gwx_ref,
                  a_scr, at_scr, b_scr, t_scr, r_scr, gc_scr, w_scr):
     n = pl.program_id(0)
 
     @pl.when(n == 0)
     def _():
-        load_left(near_ref, far_ref, a_scr)
+        load_left((l0_ref, l1_ref, l2_ref, l3_ref), a_scr)
         ath, atl = split(a_scr[...].T)
         at_scr[:, 0:S] = ath
         at_scr[:, S : 2 * S] = atl
@@ -162,20 +163,26 @@
             gwx_ref[k, C : C + 8, :] = bias
 
 
-def finish_kernel(oh_ref, ol_ref, w_ref, b_ref, goh_ref, gol_ref, bh_ref, bl_ref, p_ref, gl_ref, wp_scr, wc_scr, acc_scr, s_scr):
-    n = pl.program_id(0)
-
-    @pl.when(n == 0)
+def pair_kernel(oh_ref, ol_ref, w_ref, b_ref, p_ref, wp_scr, wc_scr):
+    @pl.when(pl.program_id(0) == 0)
     def _():
         load_weight(w_ref, wp_scr)
         wth, wtl = split(wp_scr[...].T)
         wc_scr[0:Z, :] = wth
         wc_scr[Z : 2 * Z, :] = wtl
-        acc_scr[...] = jnp.zeros_like(acc_scr)
 
     r = dot(wc_scr[...], oh_ref[...])
     r = r[:Z] + r[Z:] + dot(wc_scr[0:Z, :], ol_ref[...])
     p_ref[...] = (r * (1.0 / S)).T + b_ref[...]
+
+
+def grad_left_kernel(goh_ref, gol_ref, bh_ref, bl_ref, gl_ref, acc_scr, s_scr):
+    n = pl.program_id(0)
+
+    @pl.when(n == 0)
+    def _():
+        acc_scr[...] = jnp.zeros_like(acc_scr)
+
     bh = bh_ref[...]
     r = dot(goh_ref[...], jnp.concatenate([bh, bl_ref[...]], axis=1))
     acc_scr[...] += r[:, :S] + r[:, S:] + dot(gol_ref[...], bh)
@@ -196,6 +203,11 @@
             gl_ref[xx, zz, 8:16, :] = jnp.concatenate([lo[4:8], hi[4:8]], axis=0)
 
 
+def copies_kernel(x_ref, out_ref):
+    for k in range(out_ref.shape[0]):
+        out_ref[k] = x_ref[...]
+
+
 def sum_spread_kernel(x_ref, out_ref):
     total = x_ref[0]
     for k in range(1, x_ref.shape[0]):
@@ -214,13 +226,15 @@
     bias_ref[...] = total[C : C + 1]
 
 
-def join_kernel(own_ref, other_ref, out_ref):
+def join_kernel(own_ref, other_ref, r0_ref, r1_ref, r2_ref, r3_ref, l0_ref, l1_ref, w_ref, gr_ref, gl_ref):
     core = core_index()
     for k in range(16):
         own = own_ref[k]
         other = other_ref[k]
-        out_ref[C * k : C * k + C, :] = jnp.where(core == 0, own, other)
-        out_ref[512 + C * k : 512 + C * k + C, :] = jnp.where(core == 0, other, own)
+        w_ref[C * k : C * k + C, :] = jnp.where(core == 0, own, other)
+        w_ref[512 + C * k : 512 + C * k + C, :] = jnp.where(core == 0, other, own)
+    gr_ref[...] = (r0_ref[0] + r1_ref[...]) + (r2_ref[...] + r3_ref[...])
+    gl_ref[...] = l0_ref[0] + l1_ref[...]
 
 
 def whole(shape):
@@ -235,7 +249,7 @@
     return pl.BlockSpec(shape, lambda n: (0, n))
 
 
-def call(kernel, ins, outs, scratch, flops, nbytes, steps=4):
+def call(kernel, ins, outs, scratch, flops, nbytes, steps=4, limit=40):
     return pl.pallas_call(
         kernel,
         grid=(steps,),
@@ -244,11 +258,11 @@
         out_shape=[pltpu.HBM(s, d) if d == BF16 else jax.ShapeDtypeStruct(s, d) for s, d, _ in outs],
         scratch_shapes=[pltpu.VMEM(s, d) for s, d in scratch],
         cost_estimate=pl.CostEstimate(flops=flops, bytes_accessed=nbytes, transcendentals=0),
-        compiler_params=pltpu.CompilerParams(vmem_limit_bytes=40 << 20),
+        compiler_params=pltpu.CompilerParams(vmem_limit_bytes=limit << 20),
     )
 
 
-LEFT = whole((4, 16, IC))
+LEFT = whole((2, 16, IC))
 RIGHT = whole((16, 4, JE))
 WHOLE_G = whole((IJ, Z))
 WEIGHT = whole((CE, Z))
@@ -260,30 +274,41 @@
     10**9, 5 << 20)
 grad_right_call = call(
     grad_right_kernel,
-    [LEFT, LEFT, cols_of((IC, 512)), cols_of((IC, 512))],
+    [LEFT, LEFT, LEFT, LEFT, cols_of((IC, 512)), cols_of((IC, 512))],
     [((4, 4, 4, JE), F32, whole((4, 4, 4, JE)))] * 2,
     [((S, IC), F32), ((2 * S, IC), BF16), ((JE, S), F32)],
     10**9, 5 << 20)
 outer_call = call(
     outer_kernel,
-    [LEFT, LEFT, RIGHT, RIGHT, WHOLE_G],
+    [LEFT, LEFT, LEFT, LEFT, RIGHT, RIGHT, WHOLE_G],
     [((CE, IJ), BF16, rows_of((256, IJ)))] * 2 + [((JE, S), BF16, rows_of((512, S)))] * 2
     + [((16, 40, Z), F32, whole((16, 40, Z)))] * 2,
     [((S, IC), F32), ((IC, 2 * S), BF16), ((S, JE), F32), ((JE, S), F32), ((2, IC, 256), F32), ((IJ, 2 * Z), BF16), ((CE, Z), F32)],
     2 * 10**9, 7 << 20)
-finish_call = call(
-    finish_kernel,
-    [cols_of((CE, 256))] * 2 + [WEIGHT, whole((1, Z))] + [cols_of((IC, 512))] * 2 + [rows_of((512, S))] * 2,
-    [((IJ, Z), F32, rows_of((256, Z))), ((4, 2, 16, IC), F32, whole((4, 2, 16, IC)))],
-    [((CE, Z), F32), ((2 * Z, CE), BF16), ((IC, S), F32), ((S, IC), F32)],
-    2 * 10**9, 9 << 20)
-join_call = call(join_kernel, [whole((16, C, Z))] * 2, [((CE, Z), F32, WEIGHT)], [], 10**5, 1 << 20, 1)
-spread_call = call(sum_spread_kernel, [whole((16, 40, Z))], [((8, 40, Z), F32, whole((8, 40, Z)))], [], 10**5, 1 << 19, 1)
+pair_call = call(
+    pair_kernel,
+    [cols_of((CE, 256))] * 2 + [WEIGHT, whole((1, Z))],
+    [((IJ, Z), F32, rows_of((256, Z)))],
+    [((CE, Z), F32), ((2 * Z, CE), BF16)],
+    10**9, 5 << 20)
+grad_left_call = call(
+    grad_left_kernel,
+    [cols_of((IC, 512))] * 2 + [rows_of((512, S))] * 2,
+    [((4, 2, 16, IC), F32, whole((4, 2, 16, IC)))],
+    [((IC, S), F32), ((S, IC), F32)],
+    10**9, 6 << 20)
+join_call = call(
+    join_kernel,
+    [whole((16, C, Z))] * 2 + [whole((4, 4, JE))] + [whole((4, JE))] * 3 + [whole((2, 16, IC)), whole((16, IC))],
+    [((CE, Z), F32, WEIGHT), ((4, JE), F32, whole((4, JE))), ((16, IC), F32, whole((16, IC)))],
+    [], 10**5, 1 << 20, 1, 8)
+copies_call = call(copies_kernel, [whole((4, JE))], [((16, 4, JE), F32, RIGHT)], [], 10**5, 1 << 19, 1, 8)
+spread_call = call(sum_spread_kernel, [whole((16, 40, Z))], [((8, 40, Z), F32, whole((8, 40, Z)))], [], 10**5, 1 << 19, 1, 8)
 final_call = call(
     sum_final_kernel,
     [whole((8, 40, Z))],
     [((16, C, Z), F32, whole((16, C, Z))), ((1, Z), F32, whole((1, Z)))],
-    [], 10**5, 1 << 19, 1)
+    [], 10**5, 1 << 19, 1, 8)
 
 
 def rid(z, y, c):
@@ -302,34 +327,39 @@
 H_PERM = [(q, q ^ 4) for q in range(8)]
 
 
-def spread(x, n, axis, groups=None):
-    copies = jnp.broadcast_to(x[None], (n,) + x.shape)
-    return lax.all_to_all(copies, axis, 0, 0, axis_index_groups=groups)
+def in_hbm(*xs):
+    return [pltpu.with_memory_space_constraint(x, pltpu.HBM) for x in xs]
 
 
 def body(left, right, w_out, b_out, pair_grad):
+    tie = lax.optimization_barrier
     g = pair_grad.reshape(IJ, Z)
-    right_own = spread(right, 16, "row", YZ)
-    left_near = jnp.stack([left] + [lax.ppermute(left, "col", p) for p in X_PERMS])
-    left_far = lax.ppermute(left_near, "col", H_PERM)
-    goh, gol = grad_outer_call(g, w_out)
+    left_far = lax.ppermute(left, "col", H_PERM)
+    (copies,) = copies_call(right)
+    right_own = lax.all_to_all(copies, "row", 0, 0, axis_index_groups=YZ)
+    left_pair = jnp.stack([left, left_far])
+    pieces = [left_pair] + [lax.ppermute(left_pair, "col", p) for p in X_PERMS]
+    goh, gol = grad_outer_call(*in_hbm(g, w_out))
     right_other = lax.ppermute(right_own, "row", CORE)
-    oh, ol, bh, bl, gw_own, gw_other = outer_call(left_near, left_far, right_own, right_other, g)
+    oh, ol, bh, bl, gw_own, gw_other = outer_call(*pieces, right_own, right_other, g)
     gw = gw_own + lax.ppermute(gw_other, "row", CORE)
+    gw, goh, gol = tie((gw, goh, gol))
     gw = lax.all_to_all(gw, BOTH, 0, 0, axis_index_groups=XY)
+    gr_own, gr_other = grad_right_call(*pieces, *in_hbm(goh, gol))
+    gr = gr_own + lax.ppermute(gr_other, "row", CORE)
+    (gl,) = grad_left_call(*in_hbm(goh, gol, bh, bl))
     (gw,) = spread_call(gw)
+    gw, oh, ol = tie((gw, oh, ol))
+    gr = gr[0] + sum(lax.ppermute(gr[k + 1], "row", p) for k, p in enumerate(Y_PERMS))
+    gl = gl[0] + sum(lax.ppermute(gl[k + 1], "col", p) for k, p in enumerate(X_PERMS))
     gw = lax.all_to_all(gw, BOTH, 0, 0, axis_index_groups=Z8)
+    (pair_out,) = pair_call(*in_hbm(oh, ol, w_out), b_out.reshape(1, Z))
     gw, grad_bias = final_call(gw)
+    gr_parts = [lax.ppermute(gr[k + 1], "row", p) for k, p in enumerate(Z_PERMS)]
+    gl_part = lax.ppermute(gl[1], "col", H_PERM)
     gw_own = lax.all_to_all(gw, BOTH, 0, 0, axis_index_groups=XY)
     gw_other = lax.ppermute(gw_own, "row", CORE)
-    (grad_weight,) = join_call(gw_own, gw_other)
-    gr_own, gr_other = grad_right_call(left_near, left_far, goh, gol)
-    gr = gr_own + lax.ppermute(gr_other, "row", CORE)
-    gr = gr[0] + sum(lax.ppermute(gr[k + 1], "row", p) for k, p in enumerate(Y_PERMS))
-    grad_right = gr[0] + sum(lax.ppermute(gr[k + 1], "row", p) for k, p in enumerate(Z_PERMS))
-    pair_out, gl = finish_call(oh, ol, w_out, b_out.reshape(1, Z), goh, gol, bh, bl)
-    gl = gl[0] + sum(lax.ppermute(gl[k + 1], "col", p) for k, p in enumerate(X_PERMS))
-    grad_left = gl[0] + lax.ppermute(gl[1], "col", H_PERM)
+    grad_weight, grad_right, grad_left = join_call(gw_own, gw_other, gr, *gr_parts, gl, gl_part)
     return (pair_out.reshape(TI, TJ, Z), grad_left, grad_right, grad_weight, grad_bias.reshape(Z))
 
 

time: 111 us -> 124 us (1.12)
  the two profiles are of different devices: /device:TPU:1 before, /device:TPU:32 now
where the time goes in v3:
time: 124 us; the launch traced here: 122 us
  starting transfers between devices  41.4 us (33%)
  Pallas kernels  28.7 us (23%)
  blocking collectives  27.6 us (22%)
  waiting for transfers between devices  20 us (16%)
  local copies, waits for them, and re-layouts  1.85 us (1%)
  other arithmetic  1.79 us (1%)
    all_to_all x1, blocking collectives, body(): right_own = lax.all_to_all(copies, 'row', 0, 0, axis_index_groups=YZ)  27.6 us
    ppermute x6, starting transfers between devices, body(): lax.ppermute(gr[k + 1], 'row', p)  11.7 us
    all_to_all x1, waiting for transfers between devices, body(): gw_own = lax.all_to_all(gw, BOTH, 0, 0, axis_index_groups=XY)  8.59 us
    all_to_all x1, starting transfers between devices, body(): gw_own = lax.all_to_all(gw, BOTH, 0, 0, axis_index_groups=XY)  6.46 us
    pallas_call x1, Pallas kernels, body(): outer_call(*pieces, right_own, right_other, g)  6.41 us
    ppermute x3, starting transfers between devices, body(): lax.ppermute(gl[k + 1], 'col', p)  6.13 us
    ppermute x3, starting transfers between devices, body(): pieces = [left_pair] + [lax.ppermute(left_pair, 'col', p) for p in X_PERMS]  5.65 us
    pallas_call x1, Pallas kernels, body(): goh, gol = grad_outer_call(*in_hbm(g, w_out))  5.63 us
  transfers between devices with their start and end apart: 21, of which 9 were waited for; matrix products, arithmetic and copies ran while one was open for 1% of the time, Pallas kernels for 14%

profile of v3, /device:TPU:32, one launch (start us, length us, event | category | flops | bytes accessed | tf_op | source)
XLA Modules:
  0.0 122.1 jit_solution(8104038552865536054)
XLA Ops:
  0.6 0.0 copy-start
  0.6 0.7 copy-done
  1.4 27.6 %all_to_all.20.own_ref = f32[16,4,2048]{2,1,0:T(4,128)S(1)} all-to-all(f32[16,4,2048]{2,1,0:T(4,128)S(1)} %shard_map.92), channel_id=1, replica_groups={{0,16,32,48,64,80,96,112,128,144,160,176,192,208,224,240},{8,24,40,56,7..., dimensions={0} | all-to-all | bytes 1048576 | tf_op jit(solution)/shard_map/all_to_all | solution.py:339
  29.0 0.0 collective-permute-start.4
  29.0 0.9 collective-permute-start
  29.9 3.2 %collective-permute-done = f32[16,512]{1,0:T(8,128)S(1)} collective-permute-done((f32[16,512]{1,0:T(8,128)}, f32[16,512]{1,0:T(8,128)S(1)}, u32[]{:S(2)}, u32[]{:S(2)}) %collective-permute-start) | collective-permute-done | bytes 32800 | tf_op jit(solution)/shard_map/ppermute | solution.py:337
  33.1 0.8 pad_maximum_fusion.l0_ref
  33.9 1.5 %collective-permute-start.1 = (f32[2,16,512]{2,1,0:T(8,128)S(1)}, f32[2,16,512]{2,1,0:T(8,128)S(1)}, u32[]{:S(2)}, u32[]{:S(2)}) collective-permute-start(f32[2,16,512]{2,1,0:T(8,128)S(1)} %pad_maximum_fusion.l0_ref), channel_id=1, source_target_pairs={{0,1},{1,2},{2,3},{3,0},{4,5},{5,6},{6,7},{7,4},{8,9},{9,10},{10,1... | collective-permute-start | bytes 196616 | tf_op jit(solution)/shard_map/ppermute | solution.py:341
  35.4 2.7 %collective-permute-start.2 = (f32[2,16,512]{2,1,0:T(8,128)S(1)}, f32[2,16,512]{2,1,0:T(8,128)S(1)}, u32[]{:S(2)}, u32[]{:S(2)}) collective-permute-start(f32[2,16,512]{2,1,0:T(8,128)S(1)} %pad_maximum_fusion.l0_ref), channel_id=1, source_target_pairs={{0,2},{1,3},{2,0},{3,1},{4,6},{5,7},{6,4},{7,5},{8,10},{9,11},{10,... | collective-permute-start | bytes 196616 | tf_op jit(solution)/shard_map/ppermute | solution.py:341
  38.1 1.4 %collective-permute-start.3 = (f32[2,16,512]{2,1,0:T(8,128)S(1)}, f32[2,16,512]{2,1,0:T(8,128)S(1)}, u32[]{:S(2)}, u32[]{:S(2)}) collective-permute-start(f32[2,16,512]{2,1,0:T(8,128)S(1)} %pad_maximum_fusion.l0_ref), channel_id=1, source_target_pairs={{0,3},{1,0},{2,1},{3,2},{4,7},{5,4},{6,5},{7,6},{8,11},{9,8},{10,9... | collective-permute-start | bytes 196616 | tf_op jit(solution)/shard_map/ppermute | solution.py:341
  39.5 0.5 collective-permute-done.1.l1_ref
  40.1 1.1 collective-permute-done.2.l2_ref
  41.1 1.2 %collective-permute-done.3.l3_ref = f32[2,16,512]{2,1,0:T(8,128)S(1)} collective-permute-done((f32[2,16,512]{2,1,0:T(8,128)S(1)}, f32[2,16,512]{2,1,0:T(8,128)S(1)}, u32[]{:S(2)}, u32[]{:S(2)}) %collective-permute-start.3) | collective-permute-done | bytes 65568 | tf_op jit(solution)/shard_map/ppermute | solution.py:341
  42.4 0.0 collective-permute-done.4.other_ref
  42.4 0.0 copy-start.2
  42.4 1.0 copy-done.2
  43.4 6.4 %shard_map.93 = (bf16[1024,1024]{1,0:T(8,128)(2,1)}, bf16[1024,1024]{1,0:T(8,128)(2,1)}, bf16[2048,128]{1,0:T(8,128)(2,1)}, bf16[2048,128]{1,0:T(8,128)(2,1)}, f...) custom-call(f32[2,16,512]{2,1,0:T(8,128)S(1)} %pad_maximum_fusion.l0_ref, ...), custom_call_target="tpu_custom_call" | custom-call | flops 2000000000 | bytes 7340032 | tf_op jit(solution)/shard_map/pallas_call | solution.py:344
  49.8 0.0 collective-permute-start.5
  49.8 5.6 %shard_map.94 = (bf16[512,2048]{1,0:T(8,128)(2,1)}, bf16[512,2048]{1,0:T(8,128)(2,1)}) custom-call(f32[1024,128]{1,0:T(8,128)} %bitcast.35, f32[1024,128]{1,0:T(8,128)} %w_ref.3), custom_call_target="tpu_custom_call" | custom-call | flops 1000000000 | bytes 5242880 | tf_op jit(solution)/shard_map/pallas_call | solution.py:342
  55.5 0.0 collective-permute-done.5
  55.5 0.8 add.24
  56.3 4.8 %shard_map.98 = (f32[4,4,4,2048]{3,2,1,0:T(4,128)S(1)}, f32[4,4,4,2048]{3,2,1,0:T(4,128)S(1)}) custom-call(f32[2,16,512]{2,1,0:T(8,128)S(1)} %pad_maximum_fusion.l0_ref, f32[2,16,512]{2,1,0:T(8,128)S(1)} %collective-permute-done.1.l1_ref, f32[2,16,512]{2,1,0:T(8,128)S(1)} %collective-permute-done.2.l2_ref, f32[2,16,512]{2,1,0:T(8,128)S(1)} %collective-permute-done.3.l3_ref, ...), custom_call_target="tpu_custom_call" | custom-call | flops 1000000000 | bytes 5242880 | tf_op jit(solution)/shard_map/pallas_call | solution.py:348
  61.0 0.6 collective-permute-start.7
  61.6 5.2 %all-to-all-start.1 = ((f32[16,40,128]{2,1,0:T(8,128)}), f32[16,40,128]{2,1,0:T(8,128)S(1)}, u32[]{:S(2)}, u32[]{:S(2)}) async-start(f32[16,40,128]{2,1,0:T(8,128)} %add.24), calls=%async_computation.1 | async-start | bytes 655360 | tf_op jit(solution)/shard_map/all_to_all | solution.py:347
  66.8 4.2 %shard_map.99 = f32[4,2,16,512]{3,2,1,0:T(8,128)S(1)} custom-call(bf16[512,2048]{1,0:T(8,128)(2,1)} %get-tuple-element.37.goh_ref, bf16[512,2048]{1,0:T(8,128)(2,1)} %get-tuple-element.38.gol_ref, bf16[2048,128]{1,0:T(8,128)(2,1)} %get-tuple-element.41.bh_ref, bf16[2048,128]{1,0:T(8,128)(2,1)} %get-tuple-element.42.bl_ref), custom_call_target="tpu_custom_call" | custom-call | flops 1000000000 | bytes 6291456 | tf_op jit(solution)/shard_map/pallas_call | solution.py:350
  71.0 2.0 %collective-permute-start.14 = (f32[2,16,512]{2,1,0:T(8,128)S(1)}, f32[2,16,512]{2,1,0:T(8,128)S(1)}, u32[]{:S(2)}, u32[]{:S(2)}) collective-permute-start(f32[2,16,512]{2,1,0:T(8,128)S(1)} %get-tuple-element.52), channel_id=1, source_target_pairs={{0,1},{1,2},{2,3},{3,0},{4,5},{5,6},{6,7},{7,4},{8,9},{9,10},{10,1... | collective-permute-start | bytes 196616 | tf_op jit(solution)/shard_map/ppermute | solution.py:354
  73.0 2.7 %collective-permute-start.15 = (f32[2,16,512]{2,1,0:T(8,128)S(1)}, f32[2,16,512]{2,1,0:T(8,128)S(1)}, u32[]{:S(2)}, u32[]{:S(2)}) collective-permute-start(f32[2,16,512]{2,1,0:T(8,128)S(1)} %get-tuple-element.50), channel_id=1, source_target_pairs={{0,2},{1,3},{2,0},{3,1},{4,6},{5,7},{6,4},{7,5},{8,10},{9,11},{10,... | collective-permute-start | bytes 196616 | tf_op jit(solution)/shard_map/ppermute | solution.py:354
  75.7 1.5 %collective-permute-start.16 = (f32[2,16,512]{2,1,0:T(8,128)S(1)}, f32[2,16,512]{2,1,0:T(8,128)S(1)}, u32[]{:S(2)}, u32[]{:S(2)}) collective-permute-start(f32[2,16,512]{2,1,0:T(8,128)S(1)} %get-tuple-element.51), channel_id=1, source_target_pairs={{0,3},{1,0},{2,1},{3,2},{4,7},{5,4},{6,5},{7,6},{8,11},{9,8},{10,9... | collective-permute-start | bytes 196616 | tf_op jit(solution)/shard_map/ppermute | solution.py:354
  77.2 0.1 collective-permute-done.14
  77.3 1.5 %collective-permute-done.15 = f32[2,16,512]{2,1,0:T(8,128)S(1)} collective-permute-done((f32[2,16,512]{2,1,0:T(8,128)S(1)}, f32[2,16,512]{2,1,0:T(8,128)S(1)}, u32[]{:S(2)}, u32[]{:S(2)}) %collective-permute-start.15) | collective-permute-done | bytes 65568 | tf_op jit(solution)/shard_map/ppermute | solution.py:354
  78.8 1.2 collective-permute-done.16
  80.0 0.0 all-to-all-done.1.x_ref
  80.0 0.7 shard_map.95
  80.7 0.0 copy-start.1
  80.7 4.8 %all-to-all-start.2 = ((f32[8,40,128]{2,1,0:T(8,128)}), f32[8,40,128]{2,1,0:T(8,128)S(1)}, u32[]{:S(2)}, u32[]{:S(2)}) async-start(f32[8,40,128]{2,1,0:T(8,128)} %shard_map.95), calls=%async_computation.2 | async-start | bytes 327680 | tf_op jit(solution)/shard_map/all_to_all | solution.py:355
  85.5 0.0 collective-permute-done.7
  85.5 0.1 add.25
  85.7 2.9 %collective-permute-start.10 = (f32[4,4,2048]{2,1,0:T(4,128)S(1)}, f32[4,4,2048]{2,1,0:T(4,128)S(1)}, u32[]{:S(2)}, u32[]{:S(2)}) collective-permute-start(f32[4,4,2048]{2,1,0:T(4,128)S(1)} %get-tuple-element.48), channel_id=1, source_target_pairs={{0,48},{8,56},{16,0},{24,8},{32,16},{40,24},{48,32},{56,40},{64,11... | collective-permute-start | bytes 393224 | tf_op jit(solution)/shard_map/ppermute | solution.py:353
  88.6 0.0 collective-permute-start.8
  88.6 2.3 %collective-permute-start.9 = (f32[4,4,2048]{2,1,0:T(4,128)S(1)}, f32[4,4,2048]{2,1,0:T(4,128)S(1)}, u32[]{:S(2)}, u32[]{:S(2)}) collective-permute-start(f32[4,4,2048]{2,1,0:T(4,128)S(1)} %get-tuple-element.47), channel_id=1, source_target_pairs={{0,32},{8,40},{16,48},{24,56},{32,0},{40,8},{48,16},{56,24},{64,96... | collective-permute-start | bytes 393224 | tf_op jit(solution)/shard_map/ppermute | solution.py:353
  90.9 0.0 collective-permute-start.17
  90.9 2.5 %all-to-all-done.2.x_ref = f32[8,40,128]{2,1,0:T(8,128)S(1)} async-done(((f32[8,40,128]{2,1,0:T(8,128)}), f32[8,40,128]{2,1,0:T(8,128)S(1)}, u32[]{:S(2)}, u32[]{:S(2)}) %all-to-all-start.2) | async-done | bytes 163872 | tf_op jit(solution)/shard_map/all_to_all | solution.py:355
  93.5 0.7 shard_map.97
  94.2 6.5 %all-to-all-start.3 = ((f32[16,32,128]{2,1,0:T(8,128)}), f32[16,32,128]{2,1,0:T(8,128)S(1)}, u32[]{:S(2)}, u32[]{:S(2)}) async-start(f32[16,32,128]{2,1,0:T(8,128)} %get-tuple-element.36), calls=%async_computation.3 | async-start | bytes 524288 | tf_op jit(solution)/shard_map/all_to_all | solution.py:360
  100.7 0.0 collective-permute-done.10
  100.7 0.0 collective-permute-done.8
  100.7 0.0 collective-permute-done.9
  100.7 0.1 fusion.r0_ref
  100.8 8.6 %all-to-all-done.3.own_ref = f32[16,32,128]{2,1,0:T(8,128)S(1)} async-done(((f32[16,32,128]{2,1,0:T(8,128)}), f32[16,32,128]{2,1,0:T(8,128)S(1)}, u32[]{:S(2)}, u32[]{:S(2)}) %all-to-all-start.3) | async-done | bytes 262176 | tf_op jit(solution)/shard_map/all_to_all | solution.py:360
  109.4 0.0 collective-permute-start.6
  109.4 0.3 collective-permute-start.11
  109.7 4.0 %collective-permute-start.12 = (f32[4,2048]{1,0:T(4,128)S(1)}, f32[4,2048]{1,0:T(4,128)S(1)}, u32[]{:S(2)}, u32[]{:S(2)}) collective-permute-start(f32[4,2048]{1,0:T(4,128)S(1)} %get-tuple-element.54), channel_id=1, source_target_pairs={{0,128},{8,136},{16,144},{24,152},{32,160},{40,168},{48,176},{56,1... | collective-permute-start | bytes 98312 | tf_op jit(solution)/shard_map/ppermute | solution.py:358
  113.7 2.1 %collective-permute-start.13 = (f32[4,2048]{1,0:T(4,128)S(1)}, f32[4,2048]{1,0:T(4,128)S(1)}, u32[]{:S(2)}, u32[]{:S(2)}) collective-permute-start(f32[4,2048]{1,0:T(4,128)S(1)} %get-tuple-element.53), channel_id=1, source_target_pairs={{0,192},{8,200},{16,208},{24,216},{32,224},{40,232},{48,240},{56,2... | collective-permute-start | bytes 98312 | tf_op jit(solution)/shard_map/ppermute | solution.py:358
  115.8 0.0 copy-done.1
  115.8 5.4 %shard_map.96 = f32[1024,128]{1,0:T(8,128)} custom-call(bf16[1024,1024]{1,0:T(8,128)(2,1)} %get-tuple-element.33.oh_ref, bf16[1024,1024]{1,0:T(8,128)(2,1)} %get-tuple-element.34.ol_ref, f32[1024,128]{1,0:T(8,128)} %w_ref.3, f32[1,128]{1,0:T(1,128)S(1)} %bitcast.34), custom_call_target="tpu_custom_call" | custom-call | flops 1000000000 | bytes 5242880 | tf_op jit(solution)/shard_map/pallas_call | solution.py:356
  121.2 0.0 collective-permute-done.17.l1_ref
  121.2 0.0 collective-permute-done.11.r1_ref
  121.2 0.0 collective-permute-done.12.r2_ref
  121.2 0.0 collective-permute-done.13.r3_ref
  121.2 0.0 collective-permute-done.6.other_ref
  121.2 0.8 shard_map.100
  (6 shorter events, 0.1 us)
Async XLA Ops:
  0.6 0.8 copy-start
  29.0 13.4 %collective-permute-start.4 = (f32[16,4,2048]{2,1,0:T(4,128)S(1)}, f32[16,4,2048]{2,1,0:T(4,128)S(1)}, u32[]{:S(2)}, u32[]{:S(2)}) collective-permute-start(f32[16,4,2048]{2,1,0:T(4,128)S(1)} %all_to_all.20.own_ref), channel_id=1, source_target_pairs={{0,8},{8,0},{16,24},{24,16},{32,40},{40,32},{48,56},{56,48},{64,72... | collective-permute-start | bytes 1572872 | tf_op jit(solution)/shard_map/ppermute | solution.py:343
  29.0 4.1 %collective-permute-start = (f32[16,512]{1,0:T(8,128)}, f32[16,512]{1,0:T(8,128)S(1)}, u32[]{:S(2)}, u32[]{:S(2)}) collective-permute-start(f32[16,512]{1,0:T(8,128)} %param.5), channel_id=1, source_target_pairs={{0,4},{1,5},{2,6},{3,7},{4,0},{5,1},{6,2},{7,3},{8,12},{9,13},{10,... | collective-permute-start | bytes 98312 | tf_op jit(solution)/shard_map/ppermute | solution.py:337
  33.9 6.2 %collective-permute-start.1 = (f32[2,16,512]{2,1,0:T(8,128)S(1)}, f32[2,16,512]{2,1,0:T(8,128)S(1)}, u32[]{:S(2)}, u32[]{:S(2)}) collective-permute-start(f32[2,16,512]{2,1,0:T(8,128)S(1)} %pad_maximum_fusion.l0_ref), channel_id=1, source_target_pairs={{0,1},{1,2},{2,3},{3,0},{4,5},{5,6},{6,7},{7,4},{8,9},{9,10},{10,1... | collective-permute-start | bytes 196616 | tf_op jit(solution)/shard_map/ppermute | solution.py:341
  35.4 5.8 %collective-permute-start.2 = (f32[2,16,512]{2,1,0:T(8,128)S(1)}, f32[2,16,512]{2,1,0:T(8,128)S(1)}, u32[]{:S(2)}, u32[]{:S(2)}) collective-permute-start(f32[2,16,512]{2,1,0:T(8,128)S(1)} %pad_maximum_fusion.l0_ref), channel_id=1, source_target_pairs={{0,2},{1,3},{2,0},{3,1},{4,6},{5,7},{6,4},{7,5},{8,10},{9,11},{10,... | collective-permute-start | bytes 196616 | tf_op jit(solution)/shard_map/ppermute | solution.py:341
  38.1 4.3 %collective-permute-start.3 = (f32[2,16,512]{2,1,0:T(8,128)S(1)}, f32[2,16,512]{2,1,0:T(8,128)S(1)}, u32[]{:S(2)}, u32[]{:S(2)}) collective-permute-start(f32[2,16,512]{2,1,0:T(8,128)S(1)} %pad_maximum_fusion.l0_ref), channel_id=1, source_target_pairs={{0,3},{1,0},{2,1},{3,2},{4,7},{5,4},{6,5},{7,6},{8,11},{9,8},{10,9... | collective-permute-start | bytes 196616 | tf_op jit(solution)/shard_map/ppermute | solution.py:341
  42.4 1.0 copy-start.2
  49.8 5.6 %collective-permute-start.5 = (f32[16,40,128]{2,1,0:T(8,128)S(1)}, f32[16,40,128]{2,1,0:T(8,128)S(1)}, u32[]{:S(2)}, u32[]{:S(2)}) collective-permute-start(f32[16,40,128]{2,1,0:T(8,128)S(1)} %get-tuple-element.27), channel_id=1, source_target_pairs={{0,8},{8,0},{16,24},{24,16},{32,40},{40,32},{48,56},{56,48},{64,72... | collective-permute-start | bytes 983048 | tf_op jit(solution)/shard_map/ppermute | solution.py:345
  61.0 24.4 %collective-permute-start.7 = (f32[4,4,4,2048]{3,2,1,0:T(4,128)S(1)}, f32[4,4,4,2048]{3,2,1,0:T(4,128)S(1)}, u32[]{:S(2)}, u32[]{:S(2)}) collective-permute-start(f32[4,4,4,2048]{3,2,1,0:T(4,128)S(1)} %get-tuple-element.40), channel_id=1, source_target_pairs={{0,8},{8,0},{16,24},{24,16},{32,40},{40,32},{48,56},{56,48},{64,72... | collective-permute-start | bytes 1572872 | tf_op jit(solution)/shard_map/ppermute | solution.py:349
  61.6 18.4 %all-to-all-start.1 = ((f32[16,40,128]{2,1,0:T(8,128)}), f32[16,40,128]{2,1,0:T(8,128)S(1)}, u32[]{:S(2)}, u32[]{:S(2)}) async-start(f32[16,40,128]{2,1,0:T(8,128)} %add.24), calls=%async_computation.1 | async-start | bytes 655360 | tf_op jit(solution)/shard_map/all_to_all | solution.py:347
  71.0 6.3 %collective-permute-start.14 = (f32[2,16,512]{2,1,0:T(8,128)S(1)}, f32[2,16,512]{2,1,0:T(8,128)S(1)}, u32[]{:S(2)}, u32[]{:S(2)}) collective-permute-start(f32[2,16,512]{2,1,0:T(8,128)S(1)} %get-tuple-element.52), channel_id=1, source_target_pairs={{0,1},{1,2},{2,3},{3,0},{4,5},{5,6},{6,7},{7,4},{8,9},{9,10},{10,1... | collective-permute-start | bytes 196616 | tf_op jit(solution)/shard_map/ppermute | solution.py:354
  73.0 5.8 %collective-permute-start.15 = (f32[2,16,512]{2,1,0:T(8,128)S(1)}, f32[2,16,512]{2,1,0:T(8,128)S(1)}, u32[]{:S(2)}, u32[]{:S(2)}) collective-permute-start(f32[2,16,512]{2,1,0:T(8,128)S(1)} %get-tuple-element.50), channel_id=1, source_target_pairs={{0,2},{1,3},{2,0},{3,1},{4,6},{5,7},{6,4},{7,5},{8,10},{9,11},{10,... | collective-permute-start | bytes 196616 | tf_op jit(solution)/shard_map/ppermute | solution.py:354
  75.7 4.3 %collective-permute-start.16 = (f32[2,16,512]{2,1,0:T(8,128)S(1)}, f32[2,16,512]{2,1,0:T(8,128)S(1)}, u32[]{:S(2)}, u32[]{:S(2)}) collective-permute-start(f32[2,16,512]{2,1,0:T(8,128)S(1)} %get-tuple-element.51), channel_id=1, source_target_pairs={{0,3},{1,0},{2,1},{3,2},{4,7},{5,4},{6,5},{7,6},{8,11},{9,8},{10,9... | collective-permute-start | bytes 196616 | tf_op jit(solution)/shard_map/ppermute | solution.py:354
  80.7 35.1 %copy-start.1 = (f32[128]{0:T(128)S(1)}, f32[128]{0:T(128)}, u32[]{:S(2)}) copy-start(f32[128]{0:T(128)} %param.8) | copy-start | bytes 1540
  80.7 12.8 %all-to-all-start.2 = ((f32[8,40,128]{2,1,0:T(8,128)}), f32[8,40,128]{2,1,0:T(8,128)S(1)}, u32[]{:S(2)}, u32[]{:S(2)}) async-start(f32[8,40,128]{2,1,0:T(8,128)} %shard_map.95), calls=%async_computation.2 | async-start | bytes 327680 | tf_op jit(solution)/shard_map/all_to_all | solution.py:355
  85.7 15.0 %collective-permute-start.10 = (f32[4,4,2048]{2,1,0:T(4,128)S(1)}, f32[4,4,2048]{2,1,0:T(4,128)S(1)}, u32[]{:S(2)}, u32[]{:S(2)}) collective-permute-start(f32[4,4,2048]{2,1,0:T(4,128)S(1)} %get-tuple-element.48), channel_id=1, source_target_pairs={{0,48},{8,56},{16,0},{24,8},{32,16},{40,24},{48,32},{56,40},{64,11... | collective-permute-start | bytes 393224 | tf_op jit(solution)/shard_map/ppermute | solution.py:353
  88.6 12.1 %collective-permute-start.8 = (f32[4,4,2048]{2,1,0:T(4,128)S(1)}, f32[4,4,2048]{2,1,0:T(4,128)S(1)}, u32[]{:S(2)}, u32[]{:S(2)}) collective-permute-start(f32[4,4,2048]{2,1,0:T(4,128)S(1)} %get-tuple-element.49), channel_id=1, source_target_pairs={{0,16},{8,24},{16,32},{24,40},{32,48},{40,56},{48,0},{56,8},{64,80... | collective-permute-start | bytes 393224 | tf_op jit(solution)/shard_map/ppermute | solution.py:353
  88.6 12.1 %collective-permute-start.9 = (f32[4,4,2048]{2,1,0:T(4,128)S(1)}, f32[4,4,2048]{2,1,0:T(4,128)S(1)}, u32[]{:S(2)}, u32[]{:S(2)}) collective-permute-start(f32[4,4,2048]{2,1,0:T(4,128)S(1)} %get-tuple-element.47), channel_id=1, source_target_pairs={{0,32},{8,40},{16,48},{24,56},{32,0},{40,8},{48,16},{56,24},{64,96... | collective-permute-start | bytes 393224 | tf_op jit(solution)/shard_map/ppermute | solution.py:353
  90.9 30.3 %collective-permute-start.17 = (f32[16,512]{1,0:T(8,128)S(1)}, f32[16,512]{1,0:T(8,128)S(1)}, u32[]{:S(2)}, u32[]{:S(2)}) collective-permute-start(f32[16,512]{1,0:T(8,128)S(1)} %slice_bitcast_fusion.8), channel_id=1, source_target_pairs={{0,4},{1,5},{2,6},{3,7},{4,0},{5,1},{6,2},{7,3},{8,12},{9,13},{10,... | collective-permute-start | bytes 98312 | tf_op jit(solution)/shard_map/ppermute | solution.py:359
  94.2 15.2 %all-to-all-start.3 = ((f32[16,32,128]{2,1,0:T(8,128)}), f32[16,32,128]{2,1,0:T(8,128)S(1)}, u32[]{:S(2)}, u32[]{:S(2)}) async-start(f32[16,32,128]{2,1,0:T(8,128)} %get-tuple-element.36), calls=%async_computation.3 | async-start | bytes 524288 | tf_op jit(solution)/shard_map/all_to_all | solution.py:360
  109.4 11.9 %collective-permute-start.6 = (f32[16,32,128]{2,1,0:T(8,128)S(1)}, f32[16,32,128]{2,1,0:T(8,128)S(1)}, u32[]{:S(2)}, u32[]{:S(2)}) collective-permute-start(f32[16,32,128]{2,1,0:T(8,128)S(1)} %all-to-all-done.3.own_ref), channel_id=1, source_target_pairs={{0,8},{8,0},{16,24},{24,16},{32,40},{40,32},{48,56},{56,48},{64,72... | collective-permute-start | bytes 786440 | tf_op jit(solution)/shard_map/ppermute | solution.py:361
  109.4 11.8 %collective-permute-start.11 = (f32[4,2048]{1,0:T(4,128)S(1)}, f32[4,2048]{1,0:T(4,128)S(1)}, u32[]{:S(2)}, u32[]{:S(2)}) collective-permute-start(f32[4,2048]{1,0:T(4,128)S(1)} %get-tuple-element.55), channel_id=1, source_target_pairs={{0,64},{8,72},{16,80},{24,88},{32,96},{40,104},{48,112},{56,120},{... | collective-permute-start | bytes 98312 | tf_op jit(solution)/shard_map/ppermute | solution.py:358
  109.7 11.5 %collective-permute-start.12 = (f32[4,2048]{1,0:T(4,128)S(1)}, f32[4,2048]{1,0:T(4,128)S(1)}, u32[]{:S(2)}, u32[]{:S(2)}) collective-permute-start(f32[4,2048]{1,0:T(4,128)S(1)} %get-tuple-element.54), channel_id=1, source_target_pairs={{0,128},{8,136},{16,144},{24,152},{32,160},{40,168},{48,176},{56,1... | collective-permute-start | bytes 98312 | tf_op jit(solution)/shard_map/ppermute | solution.py:358
  113.7 7.5 %collective-permute-start.13 = (f32[4,2048]{1,0:T(4,128)S(1)}, f32[4,2048]{1,0:T(4,128)S(1)}, u32[]{:S(2)}, u32[]{:S(2)}) collective-permute-start(f32[4,2048]{1,0:T(4,128)S(1)} %get-tuple-element.53), channel_id=1, source_target_pairs={{0,192},{8,200},{16,208},{24,216},{32,224},{40,232},{48,240},{56,2... | collective-permute-start | bytes 98312 | tf_op jit(solution)/shard_map/ppermute | solution.py:358

commit v4 on v3

--- a/solution.py
+++ b/solution.py
@@ -81,7 +81,7 @@
                 gol_ref[row : row + C, 128 * ep : 128 * ep + 128] = lo
 
 
-def grad_right_kernel(l0_ref, l1_ref, l2_ref, l3_ref, goh_ref, gol_ref, own_ref, other_ref, a_scr, ac_scr, t_scr):
+def grad_right_kernel(l0_ref, l1_ref, l2_ref, l3_ref, goh_ref, gol_ref, own_ref, other_ref, a_scr, ac_scr, acc_scr, t_scr):
     n = pl.program_id(0)
 
     @pl.when(n == 0)
@@ -91,11 +91,21 @@
         ac_scr[0:S, :] = ah
         ac_scr[S : 2 * S, :] = al
 
-    r = dot(ac_scr[...], goh_ref[...])
-    r = r[:S] + r[S:] + dot(ac_scr[0:S, :], gol_ref[...])
-    t_scr[pl.ds(pl.multiple_of(n * 512, 512), 512), :] = (r * (1.0 / S)).T
-
-    @pl.when(n == 3)
+    k = pl.ds(pl.multiple_of(n * 256, 256), 256)
+    for q in range(4):
+        cols = slice(512 * q, 512 * q + 512)
+        r = dot(ac_scr[:, k], goh_ref[:, cols])
+        r = r[:S] + r[S:] + dot(ac_scr[0:S, k], gol_ref[:, cols])
+
+        @pl.when(n == 0)
+        def _():
+            acc_scr[:, cols] = r
+
+        @pl.when(n == 1)
+        def _():
+            t_scr[cols, :] = ((acc_scr[:, cols] + r) * (1.0 / S)).T
+
+    @pl.when(n == 1)
     def _():
         row = lax.axis_index("row") // 2
         y = lax.rem(row, 4)
@@ -163,35 +173,47 @@
             gwx_ref[k, C : C + 8, :] = bias
 
 
-def pair_kernel(oh_ref, ol_ref, w_ref, b_ref, p_ref, wp_scr, wc_scr):
-    @pl.when(pl.program_id(0) == 0)
+def pair_kernel(oh_ref, ol_ref, w_ref, b_ref, p_ref, wp_scr, wc_scr, acc_scr):
+    n = pl.program_id(0)
+
+    @pl.when(n == 0)
     def _():
         load_weight(w_ref, wp_scr)
         wth, wtl = split(wp_scr[...].T)
         wc_scr[0:Z, :] = wth
         wc_scr[Z : 2 * Z, :] = wtl
 
-    r = dot(wc_scr[...], oh_ref[...])
-    r = r[:Z] + r[Z:] + dot(wc_scr[0:Z, :], ol_ref[...])
-    p_ref[...] = (r * (1.0 / S)).T + b_ref[...]
-
-
-def grad_left_kernel(goh_ref, gol_ref, bh_ref, bl_ref, gl_ref, acc_scr, s_scr):
+    k = pl.ds(pl.multiple_of(n * 256, 256), 256)
+    for q in range(4):
+        cols = slice(256 * q, 256 * q + 256)
+        r = dot(wc_scr[:, k], oh_ref[:, cols])
+        r = r[:Z] + r[Z:] + dot(wc_scr[0:Z, k], ol_ref[:, cols])
+
+        @pl.when(n == 0)
+        def _():
+            acc_scr[:, cols] = r
+
+        @pl.when((n > 0) & (n < 3))
+        def _():
+            acc_scr[:, cols] += r
+
+        @pl.when(n == 3)
+        def _():
+            p_ref[cols, :] = ((acc_scr[:, cols] + r) * (1.0 / S)).T + b_ref[...]
+
+
+def grad_left_kernel(goh_ref, gol_ref, bh_ref, bl_ref, gl_ref, s_scr):
     n = pl.program_id(0)
-
-    @pl.when(n == 0)
-    def _():
-        acc_scr[...] = jnp.zeros_like(acc_scr)
 
     bh = bh_ref[...]
     r = dot(goh_ref[...], jnp.concatenate([bh, bl_ref[...]], axis=1))
-    acc_scr[...] += r[:, :S] + r[:, S:] + dot(gol_ref[...], bh)
-
-    @pl.when(n == 3)
+    r = (r[:, :S] + r[:, S:] + dot(gol_ref[...], bh)) * (1.0 / S)
+    s_scr[:, pl.ds(pl.multiple_of(n * 256, 256), 256)] = r.T
+
+    @pl.when(n == 1)
     def _():
         core = core_index()
         col = lax.axis_index("col")
-        s_scr[...] = (acc_scr[...] * (1.0 / S)).T
         for q in range(8):
             own = s_scr[8 * q : 8 * q + 8, :]
             other = s_scr[64 + 8 * q : 72 + 8 * q, :]
@@ -243,10 +265,6 @@
 
 def rows_of(shape):
     return pl.BlockSpec(shape, lambda n: (n, 0))
-
-
-def cols_of(shape):
-    return pl.BlockSpec(shape, lambda n: (0, n))
 
 
 def call(kernel, ins, outs, scratch, flops, nbytes, steps=4, limit=40):
@@ -274,10 +292,10 @@
     10**9, 5 << 20)
 grad_right_call = call(
     grad_right_kernel,
-    [LEFT, LEFT, LEFT, LEFT, cols_of((IC, 512)), cols_of((IC, 512))],
+    [LEFT, LEFT, LEFT, LEFT, rows_of((256, JE)), rows_of((256, JE))],
     [((4, 4, 4, JE), F32, whole((4, 4, 4, JE)))] * 2,
-    [((S, IC), F32), ((2 * S, IC), BF16), ((JE, S), F32)],
-    10**9, 5 << 20)
+    [((S, IC), F32), ((2 * S, IC), BF16), ((S, JE), F32), ((JE, S), F32)],
+    10**9, 5 << 20, 2)
 outer_call = call(
     outer_kernel,
     [LEFT, LEFT, LEFT, LEFT, RIGHT, RIGHT, WHOLE_G],
@@ -287,16 +305,16 @@
     2 * 10**9, 7 << 20)
 pair_call = call(
     pair_kernel,
-    [cols_of((CE, 256))] * 2 + [WEIGHT, whole((1, Z))],
-    [((IJ, Z), F32, rows_of((256, Z)))],
-    [((CE, Z), F32), ((2 * Z, CE), BF16)],
+    [rows_of((256, IJ))] * 2 + [WEIGHT, whole((1, Z))],
+    [((IJ, Z), F32, whole((IJ, Z)))],
+    [((CE, Z), F32), ((2 * Z, CE), BF16), ((Z, IJ), F32)],
     10**9, 5 << 20)
 grad_left_call = call(
     grad_left_kernel,
-    [cols_of((IC, 512))] * 2 + [rows_of((512, S))] * 2,
+    [rows_of((256, JE))] * 2 + [whole((JE, S))] * 2,
     [((4, 2, 16, IC), F32, whole((4, 2, 16, IC)))],
-    [((IC, S), F32), ((S, IC), F32)],
-    10**9, 6 << 20)
+    [((S, IC), F32)],
+    10**9, 6 << 20, 2)
 join_call = call(
     join_kernel,
     [whole((16, C, Z))] * 2 + [whole((4, 4, JE))] + [whole((4, JE))] * 3 + [whole((2, 16, IC)), whole((16, IC))],
@@ -340,12 +358,12 @@
     left_pair = jnp.stack([left, left_far])
     pieces = [left_pair] + [lax.ppermute(left_pair, "col", p) for p in X_PERMS]
     goh, gol = grad_outer_call(*in_hbm(g, w_out))
+    gr_own, gr_other = grad_right_call(*pieces, *in_hbm(goh, gol))
     right_other = lax.ppermute(right_own, "row", CORE)
     oh, ol, bh, bl, gw_own, gw_other = outer_call(*pieces, right_own, right_other, g)
     gw = gw_own + lax.ppermute(gw_other, "row", CORE)
-    gw, goh, gol = tie((gw, goh, gol))
+    gw, goh, gol, bh, bl = tie((gw, goh, gol, bh, bl))
     gw = lax.all_to_all(gw, BOTH, 0, 0, axis_index_groups=XY)
-    gr_own, gr_other = grad_right_call(*pieces, *in_hbm(goh, gol))
     gr = gr_own + lax.ppermute(gr_other, "row", CORE)
     (gl,) = grad_left_call(*in_hbm(goh, gol, bh, bl))
     (gw,) = spread_call(gw)

time: 124 us -> 113 us (0.911)
  the two profiles are of different devices: /device:TPU:32 before, /device:TPU:1 now
where the time goes in v4:
time: 113 us; the launch traced here: 112 us
  starting transfers between devices  54.3 us (48%)
  Pallas kernels  31 us (27%)
  waiting for transfers between devices  23 us (20%)
  other arithmetic  1.8 us (2%)
    ppermute x6, starting transfers between devices, body(): lax.ppermute(gr[k + 1], 'row', p)  12.5 us
    all_to_all x1, starting transfers between devices, body(): right_own = lax.all_to_all(copies, 'row', 0, 0, axis_index_groups=YZ)  11.7 us
    ppermute x1, waiting for transfers between devices, body(): left_far = lax.ppermute(left, 'col', H_PERM)  10.4 us
    pallas_call x1, Pallas kernels, body(): pair_out, = pair_call(*in_hbm(oh, ol, w_out), b_out.reshape(1, Z))  7.28 us
    all_to_all x1, waiting for transfers between devices, body(): gw = lax.all_to_all(gw, BOTH, 0, 0, axis_index_groups=XY)  6.72 us
    pallas_call x1, Pallas kernels, body(): outer_call(*pieces, right_own, right_other, g)  6.41 us
    all_to_all x1, starting transfers between devices, body(): gw = lax.all_to_all(gw, BOTH, 0, 0, axis_index_groups=Z8)  5.9 us
    pallas_call x1, Pallas kernels, body(): goh, gol = grad_outer_call(*in_hbm(g, w_out))  5.61 us
  transfers between devices with their start and end apart: 22, of which 8 were waited for; matrix products, arithmetic and copies ran while one was open for 2% of the time, Pallas kernels for 20%

profile of v4, /device:TPU:1, one launch (start us, length us, event | category | flops | bytes accessed | tf_op | source)
XLA Modules:
  0.0 111.8 jit_solution(15214806866679994270)
XLA Ops:
  0.6 0.0 copy-start
  0.6 0.7 copy-done
  1.4 0.8 shard_map.92
  2.2 11.7 %all-to-all-start = ((f32[16,4,2048]{2,1,0:T(4,128)}), f32[16,4,2048]{2,1,0:T(4,128)S(1)}, u32[]{:S(2)}, u32[]{:S(2)}) async-start(f32[16,4,2048]{2,1,0:T(4,128)} %shard_map.92), calls=%async_computation | async-start | bytes 1048576 | tf_op jit(solution)/shard_map/all_to_all | solution.py:357
  14.0 0.8 collective-permute-start
  14.8 10.4 %collective-permute-done = f32[16,512]{1,0:T(8,128)S(1)} collective-permute-done((f32[16,512]{1,0:T(8,128)}, f32[16,512]{1,0:T(8,128)S(1)}, u32[]{:S(2)}, u32[]{:S(2)}) %collective-permute-start) | collective-permute-done | bytes 32800 | tf_op jit(solution)/shard_map/ppermute | solution.py:355
  25.2 0.8 pad_maximum_fusion.l0_ref
  25.9 1.2 %collective-permute-start.1 = (f32[2,16,512]{2,1,0:T(8,128)S(1)}, f32[2,16,512]{2,1,0:T(8,128)S(1)}, u32[]{:S(2)}, u32[]{:S(2)}) collective-permute-start(f32[2,16,512]{2,1,0:T(8,128)S(1)} %pad_maximum_fusion.l0_ref), channel_id=1, source_target_pairs={{0,1},{1,2},{2,3},{3,0},{4,5},{5,6},{6,7},{7,4},{8,9},{9,10},{10,1... | collective-permute-start | bytes 196616 | tf_op jit(solution)/shard_map/ppermute | solution.py:359
  27.2 2.5 %collective-permute-start.2 = (f32[2,16,512]{2,1,0:T(8,128)S(1)}, f32[2,16,512]{2,1,0:T(8,128)S(1)}, u32[]{:S(2)}, u32[]{:S(2)}) collective-permute-start(f32[2,16,512]{2,1,0:T(8,128)S(1)} %pad_maximum_fusion.l0_ref), channel_id=1, source_target_pairs={{0,2},{1,3},{2,0},{3,1},{4,6},{5,7},{6,4},{7,5},{8,10},{9,11},{10,... | collective-permute-start | bytes 196616 | tf_op jit(solution)/shard_map/ppermute | solution.py:359
  29.6 1.2 %collective-permute-start.3 = (f32[2,16,512]{2,1,0:T(8,128)S(1)}, f32[2,16,512]{2,1,0:T(8,128)S(1)}, u32[]{:S(2)}, u32[]{:S(2)}) collective-permute-start(f32[2,16,512]{2,1,0:T(8,128)S(1)} %pad_maximum_fusion.l0_ref), channel_id=1, source_target_pairs={{0,3},{1,0},{2,1},{3,2},{4,7},{5,4},{6,5},{7,6},{8,11},{9,8},{10,9... | collective-permute-start | bytes 196616 | tf_op jit(solution)/shard_map/ppermute | solution.py:359
  30.8 5.6 %shard_map.94 = (bf16[512,2048]{1,0:T(8,128)(2,1)}, bf16[512,2048]{1,0:T(8,128)(2,1)}) custom-call(f32[1024,128]{1,0:T(8,128)} %bitcast.35, f32[1024,128]{1,0:T(8,128)} %w_ref.3), custom_call_target="tpu_custom_call" | custom-call | flops 1000000000 | bytes 5242880 | tf_op jit(solution)/shard_map/pallas_call | solution.py:360
  36.4 0.0 collective-permute-done.1.l1_ref
  36.4 0.0 collective-permute-done.2.l2_ref
  36.4 0.0 collective-permute-done.3.l3_ref
  36.4 0.0 copy-start.2
  36.4 5.2 %shard_map.98 = (f32[4,4,4,2048]{3,2,1,0:T(4,128)S(1)}, f32[4,4,4,2048]{3,2,1,0:T(4,128)S(1)}) custom-call(f32[2,16,512]{2,1,0:T(8,128)S(1)} %pad_maximum_fusion.l0_ref, f32[2,16,512]{2,1,0:T(8,128)S(1)} %collective-permute-done.1.l1_ref, f32[2,16,512]{2,1,0:T(8,128)S(1)} %collective-permute-done.2.l2_ref, f32[2,16,512]{2,1,0:T(8,128)S(1)} %collective-permute-done.3.l3_ref, ...), custom_call_target="tpu_custom_call" | custom-call | flops 1000000000 | bytes 5242880 | tf_op jit(solution)/shard_map/pallas_call | solution.py:361
  41.6 3.6 %collective-permute-start.7 = (f32[4,4,4,2048]{3,2,1,0:T(4,128)S(1)}, f32[4,4,4,2048]{3,2,1,0:T(4,128)S(1)}, u32[]{:S(2)}, u32[]{:S(2)}) collective-permute-start(f32[4,4,4,2048]{3,2,1,0:T(4,128)S(1)} %get-tuple-element.42), channel_id=1, source_target_pairs={{0,8},{8,0},{16,24},{24,16},{32,40},{40,32},{48,56},{56,48},{64,72... | collective-permute-start | bytes 1572872 | tf_op jit(solution)/shard_map/ppermute | solution.py:367
  45.2 0.0 all-to-all-done.own_ref
  45.2 0.1 collective-permute-start.4
  45.3 1.4 %collective-permute-done.7 = f32[4,4,4,2048]{3,2,1,0:T(4,128)S(1)} collective-permute-done((f32[4,4,4,2048]{3,2,1,0:T(4,128)S(1)}, f32[4,4,4,2048]{3,2,1,0:T(4,128)S(1)}, u32[]{:S(2)}, u32[]{:S(2)}) %collective-permute-start.7) | collective-permute-done | bytes 524320 | tf_op jit(solution)/shard_map/ppermute | solution.py:367
  46.7 0.2 add.25
  46.9 0.6 collective-permute-done.4.other_ref
  47.4 0.0 copy-done.2
  47.4 6.4 %shard_map.93 = (bf16[1024,1024]{1,0:T(8,128)(2,1)}, bf16[1024,1024]{1,0:T(8,128)(2,1)}, bf16[2048,128]{1,0:T(8,128)(2,1)}, bf16[2048,128]{1,0:T(8,128)(2,1)}, f...) custom-call(f32[2,16,512]{2,1,0:T(8,128)S(1)} %pad_maximum_fusion.l0_ref, ...), custom_call_target="tpu_custom_call" | custom-call | flops 2000000000 | bytes 7340032 | tf_op jit(solution)/shard_map/pallas_call | solution.py:363
  53.9 0.4 collective-permute-start.5
  54.3 3.3 %collective-permute-start.10 = (f32[4,4,2048]{2,1,0:T(4,128)S(1)}, f32[4,4,2048]{2,1,0:T(4,128)S(1)}, u32[]{:S(2)}, u32[]{:S(2)}) collective-permute-start(f32[4,4,2048]{2,1,0:T(4,128)S(1)} %get-tuple-element.52), channel_id=1, source_target_pairs={{0,48},{8,56},{16,0},{24,8},{32,16},{40,24},{48,32},{56,40},{64,11... | collective-permute-start | bytes 393224 | tf_op jit(solution)/shard_map/ppermute | solution.py:371
  57.6 0.0 collective-permute-start.8
  57.6 1.8 %collective-permute-start.9 = (f32[4,4,2048]{2,1,0:T(4,128)S(1)}, f32[4,4,2048]{2,1,0:T(4,128)S(1)}, u32[]{:S(2)}, u32[]{:S(2)}) collective-permute-start(f32[4,4,2048]{2,1,0:T(4,128)S(1)} %get-tuple-element.51), channel_id=1, source_target_pairs={{0,32},{8,40},{16,48},{24,56},{32,0},{40,8},{48,16},{56,24},{64,96... | collective-permute-start | bytes 393224 | tf_op jit(solution)/shard_map/ppermute | solution.py:371
  59.3 0.0 collective-permute-done.5
  59.4 0.8 add.24
  60.1 3.5 %all-to-all-start.1 = ((f32[16,40,128]{2,1,0:T(8,128)}), f32[16,40,128]{2,1,0:T(8,128)S(1)}, u32[]{:S(2)}, u32[]{:S(2)}) async-start(f32[16,40,128]{2,1,0:T(8,128)} %add.24), calls=%async_computation.1 | async-start | bytes 655360 | tf_op jit(solution)/shard_map/all_to_all | solution.py:366
  63.7 0.0 collective-permute-done.10
  63.7 0.6 collective-permute-done.8
  64.3 1.0 collective-permute-done.9
  65.4 0.1 fusion.r0_ref
  65.4 6.7 %all-to-all-done.1.x_ref = f32[16,40,128]{2,1,0:T(8,128)S(1)} async-done(((f32[16,40,128]{2,1,0:T(8,128)}), f32[16,40,128]{2,1,0:T(8,128)S(1)}, u32[]{:S(2)}, u32[]{:S(2)}) %all-to-all-start.1) | async-done | bytes 327712 | tf_op jit(solution)/shard_map/all_to_all | solution.py:366
  72.2 0.7 shard_map.95
  72.9 5.9 %all-to-all-start.2 = ((f32[8,40,128]{2,1,0:T(8,128)}), f32[8,40,128]{2,1,0:T(8,128)S(1)}, u32[]{:S(2)}, u32[]{:S(2)}) async-start(f32[8,40,128]{2,1,0:T(8,128)} %shard_map.95), calls=%async_computation.2 | async-start | bytes 327680 | tf_op jit(solution)/shard_map/all_to_all | solution.py:373
  78.8 0.0 copy-start.1
  78.8 3.5 %shard_map.99 = f32[4,2,16,512]{3,2,1,0:T(8,128)S(1)} custom-call(bf16[512,2048]{1,0:T(8,128)(2,1)} %get-tuple-element.43.goh_ref, bf16[512,2048]{1,0:T(8,128)(2,1)} %get-tuple-element.44.gol_ref, bf16[2048,128]{1,0:T(8,128)(2,1)} %get-tuple-element.45.bh_ref, bf16[2048,128]{1,0:T(8,128)(2,1)} %get-tuple-element.46.bl_ref), custom_call_target="tpu_custom_call" | custom-call | flops 1000000000 | bytes 6291456 | tf_op jit(solution)/shard_map/pallas_call | solution.py:368
  82.3 0.4 collective-permute-start.14
  82.7 0.8 collective-permute-start.15
  83.4 1.7 %collective-permute-start.16 = (f32[2,16,512]{2,1,0:T(8,128)S(1)}, f32[2,16,512]{2,1,0:T(8,128)S(1)}, u32[]{:S(2)}, u32[]{:S(2)}) collective-permute-start(f32[2,16,512]{2,1,0:T(8,128)S(1)} %get-tuple-element.55), channel_id=1, source_target_pairs={{0,3},{1,0},{2,1},{3,2},{4,7},{5,4},{6,5},{7,6},{8,11},{9,8},{10,9... | collective-permute-start | bytes 196616 | tf_op jit(solution)/shard_map/ppermute | solution.py:372
  85.2 2.0 %all-to-all-done.2.x_ref = f32[8,40,128]{2,1,0:T(8,128)S(1)} async-done(((f32[8,40,128]{2,1,0:T(8,128)}), f32[8,40,128]{2,1,0:T(8,128)S(1)}, u32[]{:S(2)}, u32[]{:S(2)}) %all-to-all-start.2) | async-done | bytes 163872 | tf_op jit(solution)/shard_map/all_to_all | solution.py:373
  87.1 0.7 shard_map.97
  87.9 3.5 %all-to-all-start.3 = ((f32[16,32,128]{2,1,0:T(8,128)}), f32[16,32,128]{2,1,0:T(8,128)S(1)}, u32[]{:S(2)}, u32[]{:S(2)}) async-start(f32[16,32,128]{2,1,0:T(8,128)} %get-tuple-element.40), calls=%async_computation.3 | async-start | bytes 524288 | tf_op jit(solution)/shard_map/all_to_all | solution.py:378
  91.4 0.8 collective-permute-start.11
  92.2 3.3 %collective-permute-start.12 = (f32[4,2048]{1,0:T(4,128)S(1)}, f32[4,2048]{1,0:T(4,128)S(1)}, u32[]{:S(2)}, u32[]{:S(2)}) collective-permute-start(f32[4,2048]{1,0:T(4,128)S(1)} %get-tuple-element.58), channel_id=1, source_target_pairs={{0,128},{8,136},{16,144},{24,152},{32,160},{40,168},{48,176},{56,1... | collective-permute-start | bytes 98312 | tf_op jit(solution)/shard_map/ppermute | solution.py:376
  95.5 0.0 collective-permute-done.14
  95.5 3.3 %collective-permute-start.13 = (f32[4,2048]{1,0:T(4,128)S(1)}, f32[4,2048]{1,0:T(4,128)S(1)}, u32[]{:S(2)}, u32[]{:S(2)}) collective-permute-start(f32[4,2048]{1,0:T(4,128)S(1)} %get-tuple-element.57), channel_id=1, source_target_pairs={{0,192},{8,200},{16,208},{24,216},{32,224},{40,232},{48,240},{56,2... | collective-permute-start | bytes 98312 | tf_op jit(solution)/shard_map/ppermute | solution.py:376
  98.8 0.0 collective-permute-done.15
  98.8 0.0 collective-permute-done.16
  98.9 0.2 all-to-all-done.3.own_ref
  99.0 4.3 %collective-permute-start.6 = (f32[16,32,128]{2,1,0:T(8,128)S(1)}, f32[16,32,128]{2,1,0:T(8,128)S(1)}, u32[]{:S(2)}, u32[]{:S(2)}) collective-permute-start(f32[16,32,128]{2,1,0:T(8,128)S(1)} %all-to-all-done.3.own_ref), channel_id=1, source_target_pairs={{0,8},{8,0},{16,24},{24,16},{32,40},{40,32},{48,56},{56,48},{64,72... | collective-permute-start | bytes 786440 | tf_op jit(solution)/shard_map/ppermute | solution.py:379
  103.3 0.3 collective-permute-start.17
  103.6 0.0 copy-done.1
  103.6 7.3 %shard_map.96 = f32[1024,128]{1,0:T(8,128)} custom-call(bf16[1024,1024]{1,0:T(8,128)(2,1)} %get-tuple-element.37.oh_ref, bf16[1024,1024]{1,0:T(8,128)(2,1)} %get-tuple-element.38.ol_ref, f32[1024,128]{1,0:T(8,128)} %w_ref.3, f32[1,128]{1,0:T(1,128)S(1)} %bitcast.34), custom_call_target="tpu_custom_call" | custom-call | flops 1000000000 | bytes 5242880 | tf_op jit(solution)/shard_map/pallas_call | solution.py:374
  110.9 0.0 collective-permute-done.11.r1_ref
  110.9 0.0 collective-permute-done.12.r2_ref
  110.9 0.0 collective-permute-done.13.r3_ref
  110.9 0.0 collective-permute-done.17.l1_ref
  110.9 0.0 collective-permute-done.6.other_ref
  110.9 0.9 shard_map.100
  (5 shorter events, 0.1 us)
Async XLA Ops:
  0.6 0.8 copy-start
  2.2 42.9 %all-to-all-start = ((f32[16,4,2048]{2,1,0:T(4,128)}), f32[16,4,2048]{2,1,0:T(4,128)S(1)}, u32[]{:S(2)}, u32[]{:S(2)}) async-start(f32[16,4,2048]{2,1,0:T(4,128)} %shard_map.92), calls=%async_computation | async-start | bytes 1048576 | tf_op jit(solution)/shard_map/all_to_all | solution.py:357
  14.0 11.2 %collective-permute-start = (f32[16,512]{1,0:T(8,128)}, f32[16,512]{1,0:T(8,128)S(1)}, u32[]{:S(2)}, u32[]{:S(2)}) collective-permute-start(f32[16,512]{1,0:T(8,128)} %param.5), channel_id=1, source_target_pairs={{0,4},{1,5},{2,6},{3,7},{4,0},{5,1},{6,2},{7,3},{8,12},{9,13},{10,... | collective-permute-start | bytes 98312 | tf_op jit(solution)/shard_map/ppermute | solution.py:355
  25.9 10.4 %collective-permute-start.1 = (f32[2,16,512]{2,1,0:T(8,128)S(1)}, f32[2,16,512]{2,1,0:T(8,128)S(1)}, u32[]{:S(2)}, u32[]{:S(2)}) collective-permute-start(f32[2,16,512]{2,1,0:T(8,128)S(1)} %pad_maximum_fusion.l0_ref), channel_id=1, source_target_pairs={{0,1},{1,2},{2,3},{3,0},{4,5},{5,6},{6,7},{7,4},{8,9},{9,10},{10,1... | collective-permute-start | bytes 196616 | tf_op jit(solution)/shard_map/ppermute | solution.py:359
  27.2 9.2 %collective-permute-start.2 = (f32[2,16,512]{2,1,0:T(8,128)S(1)}, f32[2,16,512]{2,1,0:T(8,128)S(1)}, u32[]{:S(2)}, u32[]{:S(2)}) collective-permute-start(f32[2,16,512]{2,1,0:T(8,128)S(1)} %pad_maximum_fusion.l0_ref), channel_id=1, source_target_pairs={{0,2},{1,3},{2,0},{3,1},{4,6},{5,7},{6,4},{7,5},{8,10},{9,11},{10,... | collective-permute-start | bytes 196616 | tf_op jit(solution)/shard_map/ppermute | solution.py:359
  29.6 6.8 %collective-permute-start.3 = (f32[2,16,512]{2,1,0:T(8,128)S(1)}, f32[2,16,512]{2,1,0:T(8,128)S(1)}, u32[]{:S(2)}, u32[]{:S(2)}) collective-permute-start(f32[2,16,512]{2,1,0:T(8,128)S(1)} %pad_maximum_fusion.l0_ref), channel_id=1, source_target_pairs={{0,3},{1,0},{2,1},{3,2},{4,7},{5,4},{6,5},{7,6},{8,11},{9,8},{10,9... | collective-permute-start | bytes 196616 | tf_op jit(solution)/shard_map/ppermute | solution.py:359
  36.4 11.1 %copy-start.2 = (f32[16,64,128]{2,1,0:T(8,128)S(1)}, f32[16,64,128]{2,1,0:T(8,128)}, u32[]{:S(2)}) copy-start(f32[16,64,128]{2,1,0:T(8,128)} %param.9) | copy-start | bytes 1572868
  41.6 5.1 %collective-permute-start.7 = (f32[4,4,4,2048]{3,2,1,0:T(4,128)S(1)}, f32[4,4,4,2048]{3,2,1,0:T(4,128)S(1)}, u32[]{:S(2)}, u32[]{:S(2)}) collective-permute-start(f32[4,4,4,2048]{3,2,1,0:T(4,128)S(1)} %get-tuple-element.42), channel_id=1, source_target_pairs={{0,8},{8,0},{16,24},{24,16},{32,40},{40,32},{48,56},{56,48},{64,72... | collective-permute-start | bytes 1572872 | tf_op jit(solution)/shard_map/ppermute | solution.py:367
  45.2 2.3 %collective-permute-start.4 = (f32[16,4,2048]{2,1,0:T(4,128)S(1)}, f32[16,4,2048]{2,1,0:T(4,128)S(1)}, u32[]{:S(2)}, u32[]{:S(2)}) collective-permute-start(f32[16,4,2048]{2,1,0:T(4,128)S(1)} %all-to-all-done.own_ref), channel_id=1, source_target_pairs={{0,8},{8,0},{16,24},{24,16},{32,40},{40,32},{48,56},{56,48},{64,72... | collective-permute-start | bytes 1572872 | tf_op jit(solution)/shard_map/ppermute | solution.py:362
  53.9 5.5 %collective-permute-start.5 = (f32[16,40,128]{2,1,0:T(8,128)S(1)}, f32[16,40,128]{2,1,0:T(8,128)S(1)}, u32[]{:S(2)}, u32[]{:S(2)}) collective-permute-start(f32[16,40,128]{2,1,0:T(8,128)S(1)} %get-tuple-element.29), channel_id=1, source_target_pairs={{0,8},{8,0},{16,24},{24,16},{32,40},{40,32},{48,56},{56,48},{64,72... | collective-permute-start | bytes 983048 | tf_op jit(solution)/shard_map/ppermute | solution.py:364
  54.3 9.4 %collective-permute-start.10 = (f32[4,4,2048]{2,1,0:T(4,128)S(1)}, f32[4,4,2048]{2,1,0:T(4,128)S(1)}, u32[]{:S(2)}, u32[]{:S(2)}) collective-permute-start(f32[4,4,2048]{2,1,0:T(4,128)S(1)} %get-tuple-element.52), channel_id=1, source_target_pairs={{0,48},{8,56},{16,0},{24,8},{32,16},{40,24},{48,32},{56,40},{64,11... | collective-permute-start | bytes 393224 | tf_op jit(solution)/shard_map/ppermute | solution.py:371
  57.6 6.7 %collective-permute-start.8 = (f32[4,4,2048]{2,1,0:T(4,128)S(1)}, f32[4,4,2048]{2,1,0:T(4,128)S(1)}, u32[]{:S(2)}, u32[]{:S(2)}) collective-permute-start(f32[4,4,2048]{2,1,0:T(4,128)S(1)} %get-tuple-element.53), channel_id=1, source_target_pairs={{0,16},{8,24},{16,32},{24,40},{32,48},{40,56},{48,0},{56,8},{64,80... | collective-permute-start | bytes 393224 | tf_op jit(solution)/shard_map/ppermute | solution.py:371
  57.6 7.8 %collective-permute-start.9 = (f32[4,4,2048]{2,1,0:T(4,128)S(1)}, f32[4,4,2048]{2,1,0:T(4,128)S(1)}, u32[]{:S(2)}, u32[]{:S(2)}) collective-permute-start(f32[4,4,2048]{2,1,0:T(4,128)S(1)} %get-tuple-element.51), channel_id=1, source_target_pairs={{0,32},{8,40},{16,48},{24,56},{32,0},{40,8},{48,16},{56,24},{64,96... | collective-permute-start | bytes 393224 | tf_op jit(solution)/shard_map/ppermute | solution.py:371
  60.1 12.0 %all-to-all-start.1 = ((f32[16,40,128]{2,1,0:T(8,128)}), f32[16,40,128]{2,1,0:T(8,128)S(1)}, u32[]{:S(2)}, u32[]{:S(2)}) async-start(f32[16,40,128]{2,1,0:T(8,128)} %add.24), calls=%async_computation.1 | async-start | bytes 655360 | tf_op jit(solution)/shard_map/all_to_all | solution.py:366
  72.9 14.3 %all-to-all-start.2 = ((f32[8,40,128]{2,1,0:T(8,128)}), f32[8,40,128]{2,1,0:T(8,128)S(1)}, u32[]{:S(2)}, u32[]{:S(2)}) async-start(f32[8,40,128]{2,1,0:T(8,128)} %shard_map.95), calls=%async_computation.2 | async-start | bytes 327680 | tf_op jit(solution)/shard_map/all_to_all | solution.py:373
  78.8 24.8 %copy-start.1 = (f32[128]{0:T(128)S(1)}, f32[128]{0:T(128)}, u32[]{:S(2)}) copy-start(f32[128]{0:T(128)} %param.8) | copy-start | bytes 1540
  82.3 13.3 %collective-permute-start.14 = (f32[2,16,512]{2,1,0:T(8,128)S(1)}, f32[2,16,512]{2,1,0:T(8,128)S(1)}, u32[]{:S(2)}, u32[]{:S(2)}) collective-permute-start(f32[2,16,512]{2,1,0:T(8,128)S(1)} %get-tuple-element.56), channel_id=1, source_target_pairs={{0,1},{1,2},{2,3},{3,0},{4,5},{5,6},{6,7},{7,4},{8,9},{9,10},{10,1... | collective-permute-start | bytes 196616 | tf_op jit(solution)/shard_map/ppermute | solution.py:372
  82.7 16.2 %collective-permute-start.15 = (f32[2,16,512]{2,1,0:T(8,128)S(1)}, f32[2,16,512]{2,1,0:T(8,128)S(1)}, u32[]{:S(2)}, u32[]{:S(2)}) collective-permute-start(f32[2,16,512]{2,1,0:T(8,128)S(1)} %get-tuple-element.54), channel_id=1, source_target_pairs={{0,2},{1,3},{2,0},{3,1},{4,6},{5,7},{6,4},{7,5},{8,10},{9,11},{10,... | collective-permute-start | bytes 196616 | tf_op jit(solution)/shard_map/ppermute | solution.py:372
  83.4 15.4 %collective-permute-start.16 = (f32[2,16,512]{2,1,0:T(8,128)S(1)}, f32[2,16,512]{2,1,0:T(8,128)S(1)}, u32[]{:S(2)}, u32[]{:S(2)}) collective-permute-start(f32[2,16,512]{2,1,0:T(8,128)S(1)} %get-tuple-element.55), channel_id=1, source_target_pairs={{0,3},{1,0},{2,1},{3,2},{4,7},{5,4},{6,5},{7,6},{8,11},{9,8},{10,9... | collective-permute-start | bytes 196616 | tf_op jit(solution)/shard_map/ppermute | solution.py:372
  87.9 11.1 %all-to-all-start.3 = ((f32[16,32,128]{2,1,0:T(8,128)}), f32[16,32,128]{2,1,0:T(8,128)S(1)}, u32[]{:S(2)}, u32[]{:S(2)}) async-start(f32[16,32,128]{2,1,0:T(8,128)} %get-tuple-element.40), calls=%async_computation.3 | async-start | bytes 524288 | tf_op jit(solution)/shard_map/all_to_all | solution.py:378
  91.4 19.4 %collective-permute-start.11 = (f32[4,2048]{1,0:T(4,128)S(1)}, f32[4,2048]{1,0:T(4,128)S(1)}, u32[]{:S(2)}, u32[]{:S(2)}) collective-permute-start(f32[4,2048]{1,0:T(4,128)S(1)} %get-tuple-element.59), channel_id=1, source_target_pairs={{0,64},{8,72},{16,80},{24,88},{32,96},{40,104},{48,112},{56,120},{... | collective-permute-start | bytes 98312 | tf_op jit(solution)/shard_map/ppermute | solution.py:376
  92.2 18.6 %collective-permute-start.12 = (f32[4,2048]{1,0:T(4,128)S(1)}, f32[4,2048]{1,0:T(4,128)S(1)}, u32[]{:S(2)}, u32[]{:S(2)}) collective-permute-start(f32[4,2048]{1,0:T(4,128)S(1)} %get-tuple-element.58), channel_id=1, source_target_pairs={{0,128},{8,136},{16,144},{24,152},{32,160},{40,168},{48,176},{56,1... | collective-permute-start | bytes 98312 | tf_op jit(solution)/shard_map/ppermute | solution.py:376
  95.5 15.4 %collective-permute-start.13 = (f32[4,2048]{1,0:T(4,128)S(1)}, f32[4,2048]{1,0:T(4,128)S(1)}, u32[]{:S(2)}, u32[]{:S(2)}) collective-permute-start(f32[4,2048]{1,0:T(4,128)S(1)} %get-tuple-element.57), channel_id=1, source_target_pairs={{0,192},{8,200},{16,208},{24,216},{32,224},{40,232},{48,240},{56,2... | collective-permute-start | bytes 98312 | tf_op jit(solution)/shard_map/ppermute | solution.py:376
  99.0 11.9 %collective-permute-start.6 = (f32[16,32,128]{2,1,0:T(8,128)S(1)}, f32[16,32,128]{2,1,0:T(8,128)S(1)}, u32[]{:S(2)}, u32[]{:S(2)}) collective-permute-start(f32[16,32,128]{2,1,0:T(8,128)S(1)} %all-to-all-done.3.own_ref), channel_id=1, source_target_pairs={{0,8},{8,0},{16,24},{24,16},{32,40},{40,32},{48,56},{56,48},{64,72... | collective-permute-start | bytes 786440 | tf_op jit(solution)/shard_map/ppermute | solution.py:379
  103.3 7.6 %collective-permute-start.17 = (f32[16,512]{1,0:T(8,128)S(1)}, f32[16,512]{1,0:T(8,128)S(1)}, u32[]{:S(2)}, u32[]{:S(2)}) collective-permute-start(f32[16,512]{1,0:T(8,128)S(1)} %slice_bitcast_fusion.8), channel_id=1, source_target_pairs={{0,4},{1,5},{2,6},{3,7},{4,0},{5,1},{6,2},{7,3},{8,12},{9,13},{10,... | collective-permute-start | bytes 98312 | tf_op jit(solution)/shard_map/ppermute | solution.py:377

commit v5 on v4

--- a/solution.py
+++ b/solution.py
@@ -60,64 +60,71 @@
         wp_scr[C * e : C * e + C, :] = w_ref[pl.ds(e, C, stride=C), :]
 
 
-def grad_outer_kernel(g_ref, w_ref, goh_ref, gol_ref, wp_scr, wc_scr, r_scr):
-    @pl.when(pl.program_id(0) == 0)
-    def _():
-        load_weight(w_ref, wp_scr)
-        wh, wl = split(wp_scr[...])
-        wc_scr[:, 0:Z] = wh
-        wc_scr[:, Z : 2 * Z] = wl
-
-    gh, gl = split(g_ref[...])
-    r_scr[...] = dot(wc_scr[...], jnp.concatenate([gh, gh], axis=1), NT) + dot(wc_scr[:, 0:Z], gl, NT)
-    for ip in range(2):
-        for ep in range(16):
-            x0 = r_scr[64 * ep : 64 * ep + 32, 128 * ip : 128 * ip + 128]
-            x1 = r_scr[64 * ep + 32 : 64 * ep + 64, 128 * ip : 128 * ip + 128]
-            for k, y in enumerate(half_swap(x0, x1)):
-                hi, lo = split(y)
-                row = (2 * ip + k) * C
-                goh_ref[row : row + C, 128 * ep : 128 * ep + 128] = hi
-                gol_ref[row : row + C, 128 * ep : 128 * ep + 128] = lo
-
-
-def grad_right_kernel(l0_ref, l1_ref, l2_ref, l3_ref, goh_ref, gol_ref, own_ref, other_ref, a_scr, ac_scr, acc_scr, t_scr):
-    n = pl.program_id(0)
-
-    @pl.when(n == 0)
-    def _():
-        load_left((l0_ref, l1_ref, l2_ref, l3_ref), a_scr)
-        ah, al = split(a_scr[...])
-        ac_scr[0:S, :] = ah
-        ac_scr[S : 2 * S, :] = al
-
-    k = pl.ds(pl.multiple_of(n * 256, 256), 256)
-    for q in range(4):
-        cols = slice(512 * q, 512 * q + 512)
-        r = dot(ac_scr[:, k], goh_ref[:, cols])
-        r = r[:S] + r[S:] + dot(ac_scr[0:S, k], gol_ref[:, cols])
-
-        @pl.when(n == 0)
-        def _():
-            acc_scr[:, cols] = r
-
-        @pl.when(n == 1)
-        def _():
-            t_scr[cols, :] = ((acc_scr[:, cols] + r) * (1.0 / S)).T
-
-    @pl.when(n == 1)
-    def _():
-        row = lax.axis_index("row") // 2
-        y = lax.rem(row, 4)
-        z = row // 4
-        for m in range(16):
-            block = jnp.concatenate([t_scr[pl.ds(4 * m + q, C, stride=TJ), :] for q in range(4)], axis=0)
-            block = block.T
-            for k in range(16):
-                yy = lax.rem(k % 4 + 4 - y, 4)
-                zz = lax.rem(k // 4 + 4 - z, 4)
-                own_ref[yy, zz, :, 128 * m : 128 * m + 128] = block[4 * k : 4 * k + 4]
-                other_ref[yy, zz, :, 128 * m : 128 * m + 128] = block[64 + 4 * k : 68 + 4 * k]
+def slot_of(k):
+    return jnp.where(k == 0, 0, jnp.where(k == 3, 1, k + 1))
+
+
+def grads_kernel(l0_ref, l1_ref, l2_ref, l3_ref, g_hbm, w_hbm, goh_hbm, gol_hbm, own_ref, other_ref,
+                 a_scr, ac_scr, g_scr, w_scr, wp_scr, wc_scr, r_scr, goh_scr, gol_scr, t_scr, in_sem, out_sem):
+    get_w = pltpu.make_async_copy(w_hbm, w_scr, in_sem.at[0])
+    get_g = pltpu.make_async_copy(g_hbm, g_scr, in_sem.at[1])
+    get_w.start()
+    get_g.start()
+    load_left((l0_ref, l1_ref, l2_ref, l3_ref), a_scr)
+    ah, al = split(a_scr[...])
+    ac_scr[0:S, :] = ah
+    ac_scr[S : 2 * S, :] = al
+    get_w.wait()
+    load_weight(w_scr, wp_scr)
+    wh, wl = split(wp_scr[...])
+    wc_scr[:, 0:Z] = wh
+    wc_scr[:, Z : 2 * Z] = wl
+    get_g.wait()
+
+    def puts(n):
+        rows = pl.ds(pl.multiple_of(n * 128, 128), 128)
+        return (
+            pltpu.make_async_copy(goh_scr.at[rows, :], goh_hbm.at[rows, :], out_sem.at[0, n]),
+            pltpu.make_async_copy(gol_scr.at[rows, :], gol_hbm.at[rows, :], out_sem.at[1, n]),
+        )
+
+    @pl.loop(0, 4)
+    def _(n):
+        gh, gl = split(g_scr[pl.ds(pl.multiple_of(n * 256, 256), 256), :])
+        r_scr[...] = dot(wc_scr[...], jnp.concatenate([gh, gh], axis=1), NT) + dot(wc_scr[:, 0:Z], gl, NT)
+        for ip in range(2):
+            for ep in range(16):
+                x0 = r_scr[64 * ep : 64 * ep + 32, 128 * ip : 128 * ip + 128]
+                x1 = r_scr[64 * ep + 32 : 64 * ep + 64, 128 * ip : 128 * ip + 128]
+                for k, y in enumerate(half_swap(x0, x1)):
+                    hi, lo = split(y)
+                    rows = pl.ds(pl.multiple_of((4 * n + 2 * ip + k) * C, C), C)
+                    goh_scr[rows, 128 * ep : 128 * ep + 128] = hi
+                    gol_scr[rows, 128 * ep : 128 * ep + 128] = lo
+        for put in puts(n):
+            put.start()
+
+    @pl.loop(0, 8)
+    def _(n):
+        cols = pl.ds(pl.multiple_of(n * 256, 256), 256)
+        r = dot(ac_scr[...], goh_scr[:, cols])
+        r = r[:S] + r[S:] + dot(ac_scr[0:S, :], gol_scr[:, cols])
+        t_scr[cols, :] = (r * (1.0 / S)).T
+
+    row = lax.axis_index("row") // 2
+    y = lax.rem(row, 4)
+    z = row // 4
+    for m in range(16):
+        block = jnp.concatenate([t_scr[pl.ds(4 * m + q, C, stride=TJ), :] for q in range(4)], axis=0)
+        block = block.T
+        for k in range(16):
+            yy = slot_of((k % 4) ^ y)
+            zz = slot_of((k // 4) ^ z)
+            own_ref[yy, zz, :, 128 * m : 128 * m + 128] = block[4 * k : 4 * k + 4]
+            other_ref[yy, zz, :, 128 * m : 128 * m + 128] = block[64 + 4 * k : 68 + 4 * k]
+    for n in range(4):
+        for put in puts(n):
+            put.wait()
 
 
 def outer_kernel(l0_ref, l1_ref, l2_ref, l3_ref, own_ref, other_ref, g_ref, oh_ref, ol_ref, bh_ref, bl_ref, gwo_ref, gwx_ref,
@@ -173,33 +180,35 @@
             gwx_ref[k, C : C + 8, :] = bias
 
 
-def pair_kernel(oh_ref, ol_ref, w_ref, b_ref, p_ref, wp_scr, wc_scr, acc_scr):
-    n = pl.program_id(0)
-
-    @pl.when(n == 0)
-    def _():
-        load_weight(w_ref, wp_scr)
-        wth, wtl = split(wp_scr[...].T)
-        wc_scr[0:Z, :] = wth
-        wc_scr[Z : 2 * Z, :] = wtl
-
-    k = pl.ds(pl.multiple_of(n * 256, 256), 256)
-    for q in range(4):
-        cols = slice(256 * q, 256 * q + 256)
-        r = dot(wc_scr[:, k], oh_ref[:, cols])
-        r = r[:Z] + r[Z:] + dot(wc_scr[0:Z, k], ol_ref[:, cols])
-
-        @pl.when(n == 0)
-        def _():
-            acc_scr[:, cols] = r
-
-        @pl.when((n > 0) & (n < 3))
-        def _():
-            acc_scr[:, cols] += r
-
-        @pl.when(n == 3)
-        def _():
-            p_ref[cols, :] = ((acc_scr[:, cols] + r) * (1.0 / S)).T + b_ref[...]
+def pair_kernel(oh_hbm, ol_hbm, w_hbm, b_ref, p_hbm, oh_scr, ol_scr, w_scr, wp_scr, wc_scr, p_scr, in_sem, out_sem):
+    get_w = pltpu.make_async_copy(w_hbm, w_scr, in_sem.at[0])
+    get_h = pltpu.make_async_copy(oh_hbm, oh_scr, in_sem.at[1])
+    get_l = pltpu.make_async_copy(ol_hbm, ol_scr, in_sem.at[2])
+    get_w.start()
+    get_h.start()
+    get_l.start()
+    get_w.wait()
+    load_weight(w_scr, wp_scr)
+    wth, wtl = split(wp_scr[...].T)
+    wc_scr[0:Z, :] = wth
+    wc_scr[Z : 2 * Z, :] = wtl
+    get_h.wait()
+    get_l.wait()
+
+    def put(n):
+        rows = pl.ds(pl.multiple_of(n * 256, 256), 256)
+        return pltpu.make_async_copy(p_scr.at[rows, :], p_hbm.at[rows, :], out_sem.at[n])
+
+    @pl.loop(0, 4)
+    def _(n):
+        cols = pl.ds(pl.multiple_of(n * 256, 256), 256)
+        r = dot(wc_scr[...], oh_scr[:, cols])
+        r = r[:Z] + r[Z:] + dot(wc_scr[0:Z, :], ol_scr[:, cols])
+        p_scr[cols, :] = (r * (1.0 / S)).T + b_ref[...]
+        put(n).start()
+
+    for n in range(4):
+        put(n).wait()
 
 
 def grad_left_kernel(goh_ref, gol_ref, bh_ref, bl_ref, gl_ref, s_scr):
@@ -219,7 +228,7 @@
             other = s_scr[64 + 8 * q : 72 + 8 * q, :]
             lo = jnp.where(core == 0, own, other)
             hi = jnp.where(core == 0, other, own)
-            xx = lax.rem(q % 4 + 4 - lax.rem(col, 4), 4)
+            xx = slot_of((q % 4) ^ lax.rem(col, 4))
             zz = lax.rem(q // 4 + 2 - col // 4, 2)
             gl_ref[xx, zz, 0:8, :] = jnp.concatenate([lo[0:4], hi[0:4]], axis=0)
             gl_ref[xx, zz, 8:16, :] = jnp.concatenate([lo[4:8], hi[4:8]], axis=0)
@@ -248,14 +257,14 @@
     bias_ref[...] = total[C : C + 1]
 
 
-def join_kernel(own_ref, other_ref, r0_ref, r1_ref, r2_ref, r3_ref, l0_ref, l1_ref, w_ref, gr_ref, gl_ref):
+def join_kernel(own_ref, other_ref, r0_ref, r1_ref, l0_ref, l1_ref, w_ref, gr_ref, gl_ref):
     core = core_index()
     for k in range(16):
         own = own_ref[k]
         other = other_ref[k]
         w_ref[C * k : C * k + C, :] = jnp.where(core == 0, own, other)
         w_ref[512 + C * k : 512 + C * k + C, :] = jnp.where(core == 0, other, own)
-    gr_ref[...] = (r0_ref[0] + r1_ref[...]) + (r2_ref[...] + r3_ref[...])
+    gr_ref[...] = r0_ref[0] + r1_ref[...]
     gl_ref[...] = l0_ref[0] + l1_ref[...]
 
 
@@ -284,18 +293,32 @@
 RIGHT = whole((16, 4, JE))
 WHOLE_G = whole((IJ, Z))
 WEIGHT = whole((CE, Z))
-grad_outer_call = call(
-    grad_outer_kernel,
-    [rows_of((256, Z)), WEIGHT],
-    [((IC, JE), BF16, rows_of((128, JE)))] * 2,
-    [((CE, Z), F32), ((CE, 2 * Z), BF16), ((CE, 256), F32)],
-    10**9, 5 << 20)
-grad_right_call = call(
-    grad_right_kernel,
-    [LEFT, LEFT, LEFT, LEFT, rows_of((256, JE)), rows_of((256, JE))],
-    [((4, 4, 4, JE), F32, whole((4, 4, 4, JE)))] * 2,
-    [((S, IC), F32), ((2 * S, IC), BF16), ((S, JE), F32), ((JE, S), F32)],
-    10**9, 5 << 20, 2)
+ANY = pl.BlockSpec(memory_space=pl.ANY)
+VM = pl.BlockSpec(memory_space=pltpu.VMEM)
+DMA = pltpu.SemaphoreType.DMA
+
+
+def flat_call(kernel, ins, outs, scratch, sems, flops, nbytes):
+    return pl.pallas_call(
+        kernel,
+        in_specs=ins,
+        out_specs=[spec for _, spec in outs],
+        out_shape=[shape for shape, _ in outs],
+        scratch_shapes=[pltpu.VMEM(s, d) for s, d in scratch] + [DMA(s) for s in sems],
+        cost_estimate=pl.CostEstimate(flops=flops, bytes_accessed=nbytes, transcendentals=0),
+        compiler_params=pltpu.CompilerParams(vmem_limit_bytes=40 << 20),
+    )
+
+
+GR_PART = (jax.ShapeDtypeStruct((4, 4, 4, JE), F32), VM)
+grads_call = flat_call(
+    grads_kernel,
+    [VM] * 4 + [ANY] * 2,
+    [(pltpu.HBM((IC, JE), BF16), ANY)] * 2 + [GR_PART] * 2,
+    [((S, IC), F32), ((2 * S, IC), BF16), ((IJ, Z), F32), ((CE, Z), F32), ((CE, Z), F32), ((CE, 2 * Z), BF16),
+     ((CE, 256), F32), ((IC, JE), BF16), ((IC, JE), BF16), ((JE, S), F32)],
+    [(2,), (2, 4)],
+    2 * 10**9, 6 << 20)
 outer_call = call(
     outer_kernel,
     [LEFT, LEFT, LEFT, LEFT, RIGHT, RIGHT, WHOLE_G],
@@ -303,11 +326,12 @@
     + [((16, 40, Z), F32, whole((16, 40, Z)))] * 2,
     [((S, IC), F32), ((IC, 2 * S), BF16), ((S, JE), F32), ((JE, S), F32), ((2, IC, 256), F32), ((IJ, 2 * Z), BF16), ((CE, Z), F32)],
     2 * 10**9, 7 << 20)
-pair_call = call(
+pair_call = flat_call(
     pair_kernel,
-    [rows_of((256, IJ))] * 2 + [WEIGHT, whole((1, Z))],
-    [((IJ, Z), F32, whole((IJ, Z)))],
-    [((CE, Z), F32), ((2 * Z, CE), BF16), ((Z, IJ), F32)],
+    [ANY] * 3 + [VM],
+    [(pltpu.HBM((IJ, Z), F32), ANY)],
+    [((CE, IJ), BF16), ((CE, IJ), BF16), ((CE, Z), F32), ((CE, Z), F32), ((2 * Z, CE), BF16), ((IJ, Z), F32)],
+    [(3,), (4,)],
     10**9, 5 << 20)
 grad_left_call = call(
     grad_left_kernel,
@@ -317,7 +341,7 @@
     10**9, 6 << 20, 2)
 join_call = call(
     join_kernel,
-    [whole((16, C, Z))] * 2 + [whole((4, 4, JE))] + [whole((4, JE))] * 3 + [whole((2, 16, IC)), whole((16, IC))],
+    [whole((16, C, Z))] * 2 + [whole((2, 4, JE)), whole((4, JE)), whole((2, 16, IC)), whole((16, IC))],
     [((CE, Z), F32, WEIGHT), ((4, JE), F32, whole((4, JE))), ((16, IC), F32, whole((16, IC)))],
     [], 10**5, 1 << 20, 1, 8)
 copies_call = call(copies_kernel, [whole((4, JE))], [((16, 4, JE), F32, RIGHT)], [], 10**5, 1 << 19, 1, 8)
@@ -339,8 +363,9 @@
 Z8 = [[rid(z, y, c) * 8 + h * 4 + x for z in range(4) for h in range(2)] for y in range(4) for x in range(4) for c in range(2)]
 BOTH = ("row", "col")
 R4 = range(4)
-Y_PERMS = [[(rid(z, y, c), rid(z, (y + k) % 4, c)) for z in R4 for y in R4 for c in range(2)] for k in (1, 2, 3)]
-Z_PERMS = [[(rid(z, y, c), rid((z + k) % 4, y, c)) for z in R4 for y in R4 for c in range(2)] for k in (1, 2, 3)]
+Y_FLIP = {k: [(rid(z, y, c), rid(z, y ^ k, c)) for z in R4 for y in R4 for c in range(2)] for k in (1, 3)}
+Z_FLIP = {k: [(rid(z, y, c), rid(z ^ k, y, c)) for z in R4 for y in R4 for c in range(2)] for k in (1, 3)}
+X_FLIP = {k: [(q, q ^ k) for q in range(8)] for k in (1, 3)}
 X_PERMS = [[(h * 4 + x, h * 4 + (x + k) % 4) for h in range(2) for x in R4] for k in (1, 2, 3)]
 H_PERM = [(q, q ^ 4) for q in range(8)]
 
@@ -353,12 +378,11 @@
     tie = lax.optimization_barrier
     g = pair_grad.reshape(IJ, Z)
     left_far = lax.ppermute(left, "col", H_PERM)
-    (copies,) = copies_call(right)
+    (copies,) = copies_call(*in_hbm(right))
     right_own = lax.all_to_all(copies, "row", 0, 0, axis_index_groups=YZ)
     left_pair = jnp.stack([left, left_far])
     pieces = [left_pair] + [lax.ppermute(left_pair, "col", p) for p in X_PERMS]
-    goh, gol = grad_outer_call(*in_hbm(g, w_out))
-    gr_own, gr_other = grad_right_call(*pieces, *in_hbm(goh, gol))
+    goh, gol, gr_own, gr_other = grads_call(*pieces, *in_hbm(g, w_out))
     right_other = lax.ppermute(right_own, "row", CORE)
     oh, ol, bh, bl, gw_own, gw_other = outer_call(*pieces, right_own, right_other, g)
     gw = gw_own + lax.ppermute(gw_other, "row", CORE)
@@ -368,16 +392,19 @@
     (gl,) = grad_left_call(*in_hbm(goh, gol, bh, bl))
     (gw,) = spread_call(gw)
     gw, oh, ol = tie((gw, oh, ol))
-    gr = gr[0] + sum(lax.ppermute(gr[k + 1], "row", p) for k, p in enumerate(Y_PERMS))
-    gl = gl[0] + sum(lax.ppermute(gl[k + 1], "col", p) for k, p in enumerate(X_PERMS))
+    gr = gr[:2] + lax.ppermute(gr[2:], "row", Y_FLIP[1])
+    gr = gr[0] + lax.ppermute(gr[1], "row", Y_FLIP[3])
+    gl = gl[:2] + lax.ppermute(gl[2:], "col", X_FLIP[1])
+    gl = gl[0] + lax.ppermute(gl[1], "col", X_FLIP[3])
     gw = lax.all_to_all(gw, BOTH, 0, 0, axis_index_groups=Z8)
     (pair_out,) = pair_call(*in_hbm(oh, ol, w_out), b_out.reshape(1, Z))
     gw, grad_bias = final_call(gw)
-    gr_parts = [lax.ppermute(gr[k + 1], "row", p) for k, p in enumerate(Z_PERMS)]
+    gr = gr[:2] + lax.ppermute(gr[2:], "row", Z_FLIP[1])
+    gr_part = lax.ppermute(gr[1], "row", Z_FLIP[3])
     gl_part = lax.ppermute(gl[1], "col", H_PERM)
     gw_own = lax.all_to_all(gw, BOTH, 0, 0, axis_index_groups=XY)
     gw_other = lax.ppermute(gw_own, "row", CORE)
-    grad_weight, grad_right, grad_left = join_call(gw_own, gw_other, gr, *gr_parts, gl, gl_part)
+    grad_weight, grad_right, grad_left = join_call(gw_own, gw_other, gr, gr_part, gl, gl_part)
     return (pair_out.reshape(TI, TJ, Z), grad_left, grad_right, grad_weight, grad_bias.reshape(Z))
 
 

time: 113 us -> 110 us (0.973)
  waiting for transfers between devices: 23 us -> 30.1 us
  Pallas kernels: 31 us -> 26.6 us
  starting transfers between devices: 54.3 us -> 50.2 us
    ppermute x1, waiting for transfers between devices: 10.4 us -> 1.51 us  [body(): left_far = lax.ppermute(left, 'col', H_PERM)]
    ppermute x9 -> x6, starting transfers between devices: 15.4 us -> 7.31 us  [the longest x1 2.94 us: body(): gr = gr[0] + lax.ppermute(gr[1], 'row', Y_FLIP[3])]
    all_to_all x1, waiting for transfers between devices: 0.18 us -> 7.36 us  [body(): gw_own = lax.all_to_all(gw, BOTH, 0, 0, axis_index_groups=XY)]
    all_to_all x1, waiting for transfers between devices: 1.99 us -> 8.17 us  [body(): gw = lax.all_to_all(gw, BOTH, 0, 0, axis_index_groups=Z8)]
    ppermute x1, starting transfers between devices: 0.11 us -> 3.91 us  [body(): right_other = lax.ppermute(right_own, 'row', CORE)]
    pallas_call x1, Pallas kernels: 7.28 us -> 4.98 us  [body(): pair_out, = pair_call(*in_hbm(oh, ol, w_out), b_out.reshape(1, Z))]
    pallas_call x4 -> x3, Pallas kernels: 12.4 us -> 10.2 us  [the longest x1 7.81 us: body(): goh, gol, gr_own, gr_other = grads_call(*pieces, *in_hbm(g, w_out))]
    all_to_all x1, waiting for transfers between devices: 6.72 us -> 8.83 us  [body(): gw = lax.all_to_all(gw, BOTH, 0, 0, axis_index_groups=XY)]
  transfers between devices with their start and end apart: 22 -> 19, of which waited for: 8 -> 6; matrix products, arithmetic and copies ran while one was open for 2% -> 1% of each run, Pallas kernels for 20% -> 23%
where the time goes in v5:
time: 110 us
  starting transfers between devices  50.2 us (46%)
  waiting for transfers between devices  30.1 us (27%)
  Pallas kernels  26.6 us (24%)
  other arithmetic  1.86 us (2%)
    all_to_all x1, starting transfers between devices, body(): right_own = lax.all_to_all(copies, 'row', 0, 0, axis_index_groups=YZ)  10.7 us
    all_to_all x1, waiting for transfers between devices, body(): gw = lax.all_to_all(gw, BOTH, 0, 0, axis_index_groups=XY)  8.83 us
    all_to_all x1, waiting for transfers between devices, body(): gw = lax.all_to_all(gw, BOTH, 0, 0, axis_index_groups=Z8)  8.17 us
    pallas_call x1, Pallas kernels, body(): goh, gol, gr_own, gr_other = grads_call(*pieces, *in_hbm(g, w_out))  7.81 us
    all_to_all x1, waiting for transfers between devices, body(): gw_own = lax.all_to_all(gw, BOTH, 0, 0, axis_index_groups=XY)  7.36 us
    pallas_call x1, Pallas kernels, body(): outer_call(*pieces, right_own, right_other, g)  6.46 us
    all_to_all x1, starting transfers between devices, body(): gw = lax.all_to_all(gw, BOTH, 0, 0, axis_index_groups=Z8)  5.12 us
    pallas_call x1, Pallas kernels, body(): pair_out, = pair_call(*in_hbm(oh, ol, w_out), b_out.reshape(1, Z))  4.98 us
  transfers between devices with their start and end apart: 19, of which 6 were waited for; matrix products, arithmetic and copies ran while one was open for 1% of the time, Pallas kernels for 23%

profile of v5, /device:TPU:1, one launch (start us, length us, event | category | flops | bytes accessed | tf_op | source)
XLA Modules:
  0.0 109.7 jit_solution(1142185120720577672)
XLA Ops:
  0.6 2.5 %collective-permute-start = (f32[16,512]{1,0:T(8,128)}, f32[16,512]{1,0:T(8,128)S(1)}, u32[]{:S(2)}, u32[]{:S(2)}) collective-permute-start(f32[16,512]{1,0:T(8,128)} %param.5), channel_id=1, source_target_pairs={{0,4},{1,5},{2,6},{3,7},{4,0},{5,1},{6,2},{7,3},{8,12},{9,13},{10,... | collective-permute-start | bytes 98312 | tf_op jit(solution)/shard_map/ppermute | solution.py:380
  3.2 1.5 %collective-permute-done = f32[16,512]{1,0:T(8,128)S(1)} collective-permute-done((f32[16,512]{1,0:T(8,128)}, f32[16,512]{1,0:T(8,128)S(1)}, u32[]{:S(2)}, u32[]{:S(2)}) %collective-permute-start) | collective-permute-done | bytes 32800 | tf_op jit(solution)/shard_map/ppermute | solution.py:380
  4.7 0.8 pad_maximum_fusion.l0_ref
  5.5 1.2 %collective-permute-start.1 = (f32[2,16,512]{2,1,0:T(8,128)S(1)}, f32[2,16,512]{2,1,0:T(8,128)S(1)}, u32[]{:S(2)}, u32[]{:S(2)}) collective-permute-start(f32[2,16,512]{2,1,0:T(8,128)S(1)} %pad_maximum_fusion.l0_ref), channel_id=1, source_target_pairs={{0,1},{1,2},{2,3},{3,0},{4,5},{5,6},{6,7},{7,4},{8,9},{9,10},{10,1... | collective-permute-start | bytes 196616 | tf_op jit(solution)/shard_map/ppermute | solution.py:384
  6.7 2.5 %collective-permute-start.2 = (f32[2,16,512]{2,1,0:T(8,128)S(1)}, f32[2,16,512]{2,1,0:T(8,128)S(1)}, u32[]{:S(2)}, u32[]{:S(2)}) collective-permute-start(f32[2,16,512]{2,1,0:T(8,128)S(1)} %pad_maximum_fusion.l0_ref), channel_id=1, source_target_pairs={{0,2},{1,3},{2,0},{3,1},{4,6},{5,7},{6,4},{7,5},{8,10},{9,11},{10,... | collective-permute-start | bytes 196616 | tf_op jit(solution)/shard_map/ppermute | solution.py:384
  9.1 1.2 %collective-permute-start.3 = (f32[2,16,512]{2,1,0:T(8,128)S(1)}, f32[2,16,512]{2,1,0:T(8,128)S(1)}, u32[]{:S(2)}, u32[]{:S(2)}) collective-permute-start(f32[2,16,512]{2,1,0:T(8,128)S(1)} %pad_maximum_fusion.l0_ref), channel_id=1, source_target_pairs={{0,3},{1,0},{2,1},{3,2},{4,7},{5,4},{6,5},{7,6},{8,11},{9,8},{10,9... | collective-permute-start | bytes 196616 | tf_op jit(solution)/shard_map/ppermute | solution.py:384
  10.3 1.6 %shard_map.92 = f32[16,4,2048]{2,1,0:T(4,128)} custom-call(f32[4,2048]{1,0:T(4,128)} %x_ref.1), custom_call_target="tpu_custom_call" | custom-call | flops 100000 | bytes 524288 | tf_op jit(solution)/shard_map/pallas_call | solution.py:381
  11.9 10.7 %all-to-all-start = ((f32[16,4,2048]{2,1,0:T(4,128)}), f32[16,4,2048]{2,1,0:T(4,128)S(1)}, u32[]{:S(2)}, u32[]{:S(2)}) async-start(f32[16,4,2048]{2,1,0:T(4,128)} %shard_map.92), calls=%async_computation | async-start | bytes 1048576 | tf_op jit(solution)/shard_map/all_to_all | solution.py:382
  22.6 0.0 collective-permute-done.1.l1_ref
  22.6 0.0 collective-permute-done.2.l2_ref
  22.6 0.0 collective-permute-done.3.l3_ref
  22.6 7.8 %shard_map.94 = (bf16[512,2048]{1,0:T(8,128)(2,1)}, bf16[512,2048]{1,0:T(8,128)(2,1)}, f32[4,4,4,2048]{3,2,1,0:T(4,128)S(1)}, f32[4,4,4,2048]{3,2,1,0:T(4,128)S(1)}) custom-call(f32[2,16,512]{2,1,0:T(8,128)S(1)} %pad_maximum_fusion.l0_ref, f32[2,16,512]{2,1,0:T(8,128)S(1)} %collective-permute-done.1.l1_ref, f32[2,16,512]{2,1,0:T(8,128)S(1)} %collective-permute-done.2.l2_ref, ...), custom_call_target="tpu_custom_call" | custom-call | flops 2000000000 | bytes 6291456 | tf_op jit(solution)/shard_map/pallas_call | solution.py:385
  30.5 0.0 copy-start.1
  30.5 3.0 %collective-permute-start.7 = (f32[4,4,4,2048]{3,2,1,0:T(4,128)S(1)}, f32[4,4,4,2048]{3,2,1,0:T(4,128)S(1)}, u32[]{:S(2)}, u32[]{:S(2)}) collective-permute-start(f32[4,4,4,2048]{3,2,1,0:T(4,128)S(1)} %get-tuple-element.42), channel_id=1, source_target_pairs={{0,8},{8,0},{16,24},{24,16},{32,40},{40,32},{48,56},{56,48},{64,72... | collective-permute-start | bytes 1572872 | tf_op jit(solution)/shard_map/ppermute | solution.py:391
  33.5 1.5 %collective-permute-done.7 = f32[4,4,4,2048]{3,2,1,0:T(4,128)S(1)} collective-permute-done((f32[4,4,4,2048]{3,2,1,0:T(4,128)S(1)}, f32[4,4,4,2048]{3,2,1,0:T(4,128)S(1)}, u32[]{:S(2)}, u32[]{:S(2)}) %collective-permute-start.7) | collective-permute-done | bytes 524320 | tf_op jit(solution)/shard_map/ppermute | solution.py:391
  35.0 0.1 add.22
  35.2 1.7 %collective-permute-start.8 = (f32[2,4,4,2048]{3,2,1,0:T(4,128)S(1)}, f32[2,4,4,2048]{3,2,1,0:T(4,128)S(1)}, u32[]{:S(2)}, u32[]{:S(2)}) collective-permute-start(f32[2,4,4,2048]{3,2,1,0:T(4,128)S(1)} %slice.49), channel_id=1, source_target_pairs={{0,16},{8,24},{16,0},{24,8},{32,48},{40,56},{48,32},{56,40},{64,80... | collective-permute-start | bytes 786440 | tf_op jit(solution)/shard_map/ppermute | solution.py:395
  36.9 0.0 all-to-all-done.own_ref
  36.9 3.9 %collective-permute-start.4 = (f32[16,4,2048]{2,1,0:T(4,128)S(1)}, f32[16,4,2048]{2,1,0:T(4,128)S(1)}, u32[]{:S(2)}, u32[]{:S(2)}) collective-permute-start(f32[16,4,2048]{2,1,0:T(4,128)S(1)} %all-to-all-done.own_ref), channel_id=1, source_target_pairs={{0,8},{8,0},{16,24},{24,16},{32,40},{40,32},{48,56},{56,48},{64,72... | collective-permute-start | bytes 1572872 | tf_op jit(solution)/shard_map/ppermute | solution.py:386
  40.8 2.6 %collective-permute-done.8 = f32[2,4,4,2048]{3,2,1,0:T(4,128)S(1)} collective-permute-done((f32[2,4,4,2048]{3,2,1,0:T(4,128)S(1)}, f32[2,4,4,2048]{3,2,1,0:T(4,128)S(1)}, u32[]{:S(2)}, u32[]{:S(2)}) %collective-permute-start.8) | collective-permute-done | bytes 262176 | tf_op jit(solution)/shard_map/ppermute | solution.py:395
  43.5 0.1 slice_add_fusion
  43.6 2.9 %collective-permute-start.9 = (f32[4,4,2048]{2,1,0:T(4,128)S(1)}, f32[4,4,2048]{2,1,0:T(4,128)S(1)}, u32[]{:S(2)}, u32[]{:S(2)}) collective-permute-start(f32[4,4,2048]{2,1,0:T(4,128)S(1)} %slice_bitcast_fusion), channel_id=1, source_target_pairs={{0,48},{8,56},{16,32},{24,40},{32,16},{40,24},{48,0},{56,8},{64,11... | collective-permute-start | bytes 393224 | tf_op jit(solution)/shard_map/ppermute | solution.py:396
  46.5 0.0 collective-permute-done.4.other_ref
  46.5 0.0 copy-done.1
  46.5 6.5 %shard_map.93 = (bf16[1024,1024]{1,0:T(8,128)(2,1)}, bf16[1024,1024]{1,0:T(8,128)(2,1)}, bf16[2048,128]{1,0:T(8,128)(2,1)}, bf16[2048,128]{1,0:T(8,128)(2,1)}, f...) custom-call(f32[2,16,512]{2,1,0:T(8,128)S(1)} %pad_maximum_fusion.l0_ref, ...), custom_call_target="tpu_custom_call" | custom-call | flops 2000000000 | bytes 7340032 | tf_op jit(solution)/shard_map/pallas_call | solution.py:387
  53.0 1.2 %collective-permute-start.5 = (f32[16,40,128]{2,1,0:T(8,128)S(1)}, f32[16,40,128]{2,1,0:T(8,128)S(1)}, u32[]{:S(2)}, u32[]{:S(2)}) collective-permute-start(f32[16,40,128]{2,1,0:T(8,128)S(1)} %get-tuple-element.29), channel_id=1, source_target_pairs={{0,8},{8,0},{16,24},{24,16},{32,40},{40,32},{48,56},{56,48},{64,72... | collective-permute-start | bytes 983048 | tf_op jit(solution)/shard_map/ppermute | solution.py:388
  54.1 0.0 collective-permute-done.9
  54.2 2.0 %collective-permute-start.10 = (f32[2,4,2048]{2,1,0:T(4,128)S(1)}, f32[2,4,2048]{2,1,0:T(4,128)S(1)}, u32[]{:S(2)}, u32[]{:S(2)}) collective-permute-start(f32[2,4,2048]{2,1,0:T(4,128)S(1)} %slice.53), channel_id=1, source_target_pairs={{0,64},{8,72},{16,80},{24,88},{32,96},{40,104},{48,112},{56,120},{... | collective-permute-start | bytes 196616 | tf_op jit(solution)/shard_map/ppermute | solution.py:402
  56.2 0.0 collective-permute-done.5
  56.2 0.8 add.21
  57.0 3.5 %shard_map.98 = f32[4,2,16,512]{3,2,1,0:T(8,128)S(1)} custom-call(bf16[512,2048]{1,0:T(8,128)(2,1)} %get-tuple-element.43.goh_ref, bf16[512,2048]{1,0:T(8,128)(2,1)} %get-tuple-element.44.gol_ref, bf16[2048,128]{1,0:T(8,128)(2,1)} %get-tuple-element.45.bh_ref, bf16[2048,128]{1,0:T(8,128)(2,1)} %get-tuple-element.46.bl_ref), custom_call_target="tpu_custom_call" | custom-call | flops 1000000000 | bytes 6291456 | tf_op jit(solution)/shard_map/pallas_call | solution.py:392
  60.5 0.0 copy-start
  60.5 0.4 collective-permute-start.12
  60.9 3.7 %all-to-all-start.1 = ((f32[16,40,128]{2,1,0:T(8,128)}), f32[16,40,128]{2,1,0:T(8,128)S(1)}, u32[]{:S(2)}, u32[]{:S(2)}) async-start(f32[16,40,128]{2,1,0:T(8,128)} %add.21), calls=%async_computation.1 | async-start | bytes 655360 | tf_op jit(solution)/shard_map/all_to_all | solution.py:390
  64.7 0.0 collective-permute-done.10
  64.7 8.8 %all-to-all-done.1.x_ref = f32[16,40,128]{2,1,0:T(8,128)S(1)} async-done(((f32[16,40,128]{2,1,0:T(8,128)}), f32[16,40,128]{2,1,0:T(8,128)S(1)}, u32[]{:S(2)}, u32[]{:S(2)}) %all-to-all-start.1) | async-done | bytes 327712 | tf_op jit(solution)/shard_map/all_to_all | solution.py:390
  73.5 0.7 shard_map.95
  74.2 5.1 %all-to-all-start.2 = ((f32[8,40,128]{2,1,0:T(8,128)}), f32[8,40,128]{2,1,0:T(8,128)S(1)}, u32[]{:S(2)}, u32[]{:S(2)}) async-start(f32[8,40,128]{2,1,0:T(8,128)} %shard_map.95), calls=%async_computation.2 | async-start | bytes 327680 | tf_op jit(solution)/shard_map/all_to_all | solution.py:399
  79.3 0.0 collective-permute-done.12
  79.4 0.1 collective-permute-start.13
  79.5 8.2 %all-to-all-done.2.x_ref = f32[8,40,128]{2,1,0:T(8,128)S(1)} async-done(((f32[8,40,128]{2,1,0:T(8,128)}), f32[8,40,128]{2,1,0:T(8,128)S(1)}, u32[]{:S(2)}, u32[]{:S(2)}) %all-to-all-start.2) | async-done | bytes 163872 | tf_op jit(solution)/shard_map/all_to_all | solution.py:399
  87.7 0.7 shard_map.97
  88.4 3.5 %all-to-all-start.3 = ((f32[16,32,128]{2,1,0:T(8,128)}), f32[16,32,128]{2,1,0:T(8,128)S(1)}, u32[]{:S(2)}, u32[]{:S(2)}) async-start(f32[16,32,128]{2,1,0:T(8,128)} %get-tuple-element.40), calls=%async_computation.3 | async-start | bytes 524288 | tf_op jit(solution)/shard_map/all_to_all | solution.py:405
  92.0 0.1 collective-permute-start.11
  92.1 0.0 collective-permute-done.13
  92.1 7.4 %all-to-all-done.3.own_ref = f32[16,32,128]{2,1,0:T(8,128)S(1)} async-done(((f32[16,32,128]{2,1,0:T(8,128)}), f32[16,32,128]{2,1,0:T(8,128)S(1)}, u32[]{:S(2)}, u32[]{:S(2)}) %all-to-all-start.3) | async-done | bytes 262176 | tf_op jit(solution)/shard_map/all_to_all | solution.py:405
  99.5 4.0 %collective-permute-start.6 = (f32[16,32,128]{2,1,0:T(8,128)S(1)}, f32[16,32,128]{2,1,0:T(8,128)S(1)}, u32[]{:S(2)}, u32[]{:S(2)}) collective-permute-start(f32[16,32,128]{2,1,0:T(8,128)S(1)} %all-to-all-done.3.own_ref), channel_id=1, source_target_pairs={{0,8},{8,0},{16,24},{24,16},{32,40},{40,32},{48,56},{56,48},{64,72... | collective-permute-start | bytes 786440 | tf_op jit(solution)/shard_map/ppermute | solution.py:406
  103.5 0.3 collective-permute-start.14
  103.8 0.0 copy-done
  103.8 5.0 %shard_map.96 = f32[1024,128]{1,0:T(8,128)} custom-call(bf16[1024,1024]{1,0:T(8,128)(2,1)} %get-tuple-element.37.oh_hbm, bf16[1024,1024]{1,0:T(8,128)(2,1)} %get-tuple-element.38.ol_hbm, f32[1024,128]{1,0:T(8,128)} %w_hbm.3, f32[1,128]{1,0:T(1,128)S(1)} %bitcast.22), custom_call_target="tpu_custom_call" | custom-call | flops 1000000000 | bytes 5242880 | tf_op jit(solution)/shard_map/pallas_call | solution.py:400
  108.8 0.0 collective-permute-done.11.r1_ref
  108.8 0.0 collective-permute-done.14.l1_ref
  108.8 0.0 collective-permute-done.6.other_ref
  108.8 0.8 shard_map.99
  (11 shorter events, 0.2 us)
Async XLA Ops:
  0.6 4.1 %collective-permute-start = (f32[16,512]{1,0:T(8,128)}, f32[16,512]{1,0:T(8,128)S(1)}, u32[]{:S(2)}, u32[]{:S(2)}) collective-permute-start(f32[16,512]{1,0:T(8,128)} %param.5), channel_id=1, source_target_pairs={{0,4},{1,5},{2,6},{3,7},{4,0},{5,1},{6,2},{7,3},{8,12},{9,13},{10,... | collective-permute-start | bytes 98312 | tf_op jit(solution)/shard_map/ppermute | solution.py:380
  5.5 17.2 %collective-permute-start.1 = (f32[2,16,512]{2,1,0:T(8,128)S(1)}, f32[2,16,512]{2,1,0:T(8,128)S(1)}, u32[]{:S(2)}, u32[]{:S(2)}) collective-permute-start(f32[2,16,512]{2,1,0:T(8,128)S(1)} %pad_maximum_fusion.l0_ref), channel_id=1, source_target_pairs={{0,1},{1,2},{2,3},{3,0},{4,5},{5,6},{6,7},{7,4},{8,9},{9,10},{10,1... | collective-permute-start | bytes 196616 | tf_op jit(solution)/shard_map/ppermute | solution.py:384
  6.7 16.0 %collective-permute-start.2 = (f32[2,16,512]{2,1,0:T(8,128)S(1)}, f32[2,16,512]{2,1,0:T(8,128)S(1)}, u32[]{:S(2)}, u32[]{:S(2)}) collective-permute-start(f32[2,16,512]{2,1,0:T(8,128)S(1)} %pad_maximum_fusion.l0_ref), channel_id=1, source_target_pairs={{0,2},{1,3},{2,0},{3,1},{4,6},{5,7},{6,4},{7,5},{8,10},{9,11},{10,... | collective-permute-start | bytes 196616 | tf_op jit(solution)/shard_map/ppermute | solution.py:384
  9.1 13.5 %collective-permute-start.3 = (f32[2,16,512]{2,1,0:T(8,128)S(1)}, f32[2,16,512]{2,1,0:T(8,128)S(1)}, u32[]{:S(2)}, u32[]{:S(2)}) collective-permute-start(f32[2,16,512]{2,1,0:T(8,128)S(1)} %pad_maximum_fusion.l0_ref), channel_id=1, source_target_pairs={{0,3},{1,0},{2,1},{3,2},{4,7},{5,4},{6,5},{7,6},{8,11},{9,8},{10,9... | collective-permute-start | bytes 196616 | tf_op jit(solution)/shard_map/ppermute | solution.py:384
  11.9 25.1 %all-to-all-start = ((f32[16,4,2048]{2,1,0:T(4,128)}), f32[16,4,2048]{2,1,0:T(4,128)S(1)}, u32[]{:S(2)}, u32[]{:S(2)}) async-start(f32[16,4,2048]{2,1,0:T(4,128)} %shard_map.92), calls=%async_computation | async-start | bytes 1048576 | tf_op jit(solution)/shard_map/all_to_all | solution.py:382
  30.5 16.1 %copy-start.1 = (f32[16,64,128]{2,1,0:T(8,128)S(1)}, f32[16,64,128]{2,1,0:T(8,128)}, u32[]{:S(2)}) copy-start(f32[16,64,128]{2,1,0:T(8,128)} %param.9) | copy-start | bytes 1572868
  30.5 4.6 %collective-permute-start.7 = (f32[4,4,4,2048]{3,2,1,0:T(4,128)S(1)}, f32[4,4,4,2048]{3,2,1,0:T(4,128)S(1)}, u32[]{:S(2)}, u32[]{:S(2)}) collective-permute-start(f32[4,4,4,2048]{3,2,1,0:T(4,128)S(1)} %get-tuple-element.42), channel_id=1, source_target_pairs={{0,8},{8,0},{16,24},{24,16},{32,40},{40,32},{48,56},{56,48},{64,72... | collective-permute-start | bytes 1572872 | tf_op jit(solution)/shard_map/ppermute | solution.py:391
  35.2 8.3 %collective-permute-start.8 = (f32[2,4,4,2048]{3,2,1,0:T(4,128)S(1)}, f32[2,4,4,2048]{3,2,1,0:T(4,128)S(1)}, u32[]{:S(2)}, u32[]{:S(2)}) collective-permute-start(f32[2,4,4,2048]{3,2,1,0:T(4,128)S(1)} %slice.49), channel_id=1, source_target_pairs={{0,16},{8,24},{16,0},{24,8},{32,48},{40,56},{48,32},{56,40},{64,80... | collective-permute-start | bytes 786440 | tf_op jit(solution)/shard_map/ppermute | solution.py:395
  36.9 9.6 %collective-permute-start.4 = (f32[16,4,2048]{2,1,0:T(4,128)S(1)}, f32[16,4,2048]{2,1,0:T(4,128)S(1)}, u32[]{:S(2)}, u32[]{:S(2)}) collective-permute-start(f32[16,4,2048]{2,1,0:T(4,128)S(1)} %all-to-all-done.own_ref), channel_id=1, source_target_pairs={{0,8},{8,0},{16,24},{24,16},{32,40},{40,32},{48,56},{56,48},{64,72... | collective-permute-start | bytes 1572872 | tf_op jit(solution)/shard_map/ppermute | solution.py:386
  43.6 10.6 %collective-permute-start.9 = (f32[4,4,2048]{2,1,0:T(4,128)S(1)}, f32[4,4,2048]{2,1,0:T(4,128)S(1)}, u32[]{:S(2)}, u32[]{:S(2)}) collective-permute-start(f32[4,4,2048]{2,1,0:T(4,128)S(1)} %slice_bitcast_fusion), channel_id=1, source_target_pairs={{0,48},{8,56},{16,32},{24,40},{32,16},{40,24},{48,0},{56,8},{64,11... | collective-permute-start | bytes 393224 | tf_op jit(solution)/shard_map/ppermute | solution.py:396
  53.0 3.3 %collective-permute-start.5 = (f32[16,40,128]{2,1,0:T(8,128)S(1)}, f32[16,40,128]{2,1,0:T(8,128)S(1)}, u32[]{:S(2)}, u32[]{:S(2)}) collective-permute-start(f32[16,40,128]{2,1,0:T(8,128)S(1)} %get-tuple-element.29), channel_id=1, source_target_pairs={{0,8},{8,0},{16,24},{24,16},{32,40},{40,32},{48,56},{56,48},{64,72... | collective-permute-start | bytes 983048 | tf_op jit(solution)/shard_map/ppermute | solution.py:388
  54.2 10.5 %collective-permute-start.10 = (f32[2,4,2048]{2,1,0:T(4,128)S(1)}, f32[2,4,2048]{2,1,0:T(4,128)S(1)}, u32[]{:S(2)}, u32[]{:S(2)}) collective-permute-start(f32[2,4,2048]{2,1,0:T(4,128)S(1)} %slice.53), channel_id=1, source_target_pairs={{0,64},{8,72},{16,80},{24,88},{32,96},{40,104},{48,112},{56,120},{... | collective-permute-start | bytes 196616 | tf_op jit(solution)/shard_map/ppermute | solution.py:402
  60.5 43.3 %copy-start = (f32[128]{0:T(128)S(1)}, f32[128]{0:T(128)}, u32[]{:S(2)}) copy-start(f32[128]{0:T(128)} %param.8) | copy-start | bytes 1540
  60.5 18.8 %collective-permute-start.12 = (f32[2,2,16,512]{3,2,1,0:T(8,128)S(1)}, f32[2,2,16,512]{3,2,1,0:T(8,128)S(1)}, u32[]{:S(2)}, u32[]{:S(2)}) collective-permute-start(f32[2,2,16,512]{3,2,1,0:T(8,128)S(1)} %slice.56), channel_id=1, source_target_pairs={{0,1},{1,0},{2,3},{3,2},{4,5},{5,4},{6,7},{7,6},{8,9},{9,8},{10,11... | collective-permute-start | bytes 393224 | tf_op jit(solution)/shard_map/ppermute | solution.py:397
  60.9 12.6 %all-to-all-start.1 = ((f32[16,40,128]{2,1,0:T(8,128)}), f32[16,40,128]{2,1,0:T(8,128)S(1)}, u32[]{:S(2)}, u32[]{:S(2)}) async-start(f32[16,40,128]{2,1,0:T(8,128)} %add.21), calls=%async_computation.1 | async-start | bytes 655360 | tf_op jit(solution)/shard_map/all_to_all | solution.py:390
  74.2 13.4 %all-to-all-start.2 = ((f32[8,40,128]{2,1,0:T(8,128)}), f32[8,40,128]{2,1,0:T(8,128)S(1)}, u32[]{:S(2)}, u32[]{:S(2)}) async-start(f32[8,40,128]{2,1,0:T(8,128)} %shard_map.95), calls=%async_computation.2 | async-start | bytes 327680 | tf_op jit(solution)/shard_map/all_to_all | solution.py:399
  79.4 12.7 %collective-permute-start.13 = (f32[2,16,512]{2,1,0:T(8,128)S(1)}, f32[2,16,512]{2,1,0:T(8,128)S(1)}, u32[]{:S(2)}, u32[]{:S(2)}) collective-permute-start(f32[2,16,512]{2,1,0:T(8,128)S(1)} %slice_bitcast_fusion.2), channel_id=1, source_target_pairs={{0,3},{1,2},{2,1},{3,0},{4,7},{5,6},{6,5},{7,4},{8,11},{9,10},{10,... | collective-permute-start | bytes 196616 | tf_op jit(solution)/shard_map/ppermute | solution.py:398
  88.4 11.1 %all-to-all-start.3 = ((f32[16,32,128]{2,1,0:T(8,128)}), f32[16,32,128]{2,1,0:T(8,128)S(1)}, u32[]{:S(2)}, u32[]{:S(2)}) async-start(f32[16,32,128]{2,1,0:T(8,128)} %get-tuple-element.40), calls=%async_computation.3 | async-start | bytes 524288 | tf_op jit(solution)/shard_map/all_to_all | solution.py:405
  92.0 16.8 %collective-permute-start.11 = (f32[4,2048]{1,0:T(4,128)S(1)}, f32[4,2048]{1,0:T(4,128)S(1)}, u32[]{:S(2)}, u32[]{:S(2)}) collective-permute-start(f32[4,2048]{1,0:T(4,128)S(1)} %slice_bitcast_fusion.5), channel_id=1, source_target_pairs={{0,192},{8,200},{16,208},{24,216},{32,224},{40,232},{48,240},{56,2... | collective-permute-start | bytes 98312 | tf_op jit(solution)/shard_map/ppermute | solution.py:403
  99.5 9.3 %collective-permute-start.6 = (f32[16,32,128]{2,1,0:T(8,128)S(1)}, f32[16,32,128]{2,1,0:T(8,128)S(1)}, u32[]{:S(2)}, u32[]{:S(2)}) collective-permute-start(f32[16,32,128]{2,1,0:T(8,128)S(1)} %all-to-all-done.3.own_ref), channel_id=1, source_target_pairs={{0,8},{8,0},{16,24},{24,16},{32,40},{40,32},{48,56},{56,48},{64,72... | collective-permute-start | bytes 786440 | tf_op jit(solution)/shard_map/ppermute | solution.py:406
  103.5 5.3 %collective-permute-start.14 = (f32[16,512]{1,0:T(8,128)S(1)}, f32[16,512]{1,0:T(8,128)S(1)}, u32[]{:S(2)}, u32[]{:S(2)}) collective-permute-start(f32[16,512]{1,0:T(8,128)S(1)} %slice_bitcast_fusion.4), channel_id=1, source_target_pairs={{0,4},{1,5},{2,6},{3,7},{4,0},{5,1},{6,2},{7,3},{8,12},{9,13},{10,... | collective-permute-start | bytes 98312 | tf_op jit(solution)/shard_map/ppermute | solution.py:404

commit v6 on v5

--- a/solution.py
+++ b/solution.py
@@ -65,7 +65,7 @@
 
 
 def grads_kernel(l0_ref, l1_ref, l2_ref, l3_ref, g_hbm, w_hbm, goh_hbm, gol_hbm, own_ref, other_ref,
-                 a_scr, ac_scr, g_scr, w_scr, wp_scr, wc_scr, r_scr, goh_scr, gol_scr, t_scr, in_sem, out_sem):
+                 at_ref, gc_ref, bias_ref, a_scr, ac_scr, g_scr, w_scr, wp_scr, wc_scr, r_scr, goh_scr, gol_scr, t_scr, in_sem, out_sem):
     get_w = pltpu.make_async_copy(w_hbm, w_scr, in_sem.at[0])
     get_g = pltpu.make_async_copy(g_hbm, g_scr, in_sem.at[1])
     get_w.start()
@@ -74,12 +74,18 @@
     ah, al = split(a_scr[...])
     ac_scr[0:S, :] = ah
     ac_scr[S : 2 * S, :] = al
+    ath, atl = split(a_scr[...].T)
+    at_ref[:, 0:S] = ath
+    at_ref[:, S : 2 * S] = atl
+    at_ref[:, 2 * S : 3 * S] = ath
     get_w.wait()
     load_weight(w_scr, wp_scr)
     wh, wl = split(wp_scr[...])
     wc_scr[:, 0:Z] = wh
     wc_scr[:, Z : 2 * Z] = wl
+    wc_scr[:, 2 * Z : 3 * Z] = wh
     get_g.wait()
+    bias_ref[...] = jnp.broadcast_to(jnp.sum(g_scr[...], axis=0, keepdims=True), (8, Z))
 
     def puts(n):
         rows = pl.ds(pl.multiple_of(n * 128, 128), 128)
@@ -90,8 +96,11 @@
 
     @pl.loop(0, 4)
     def _(n):
-        gh, gl = split(g_scr[pl.ds(pl.multiple_of(n * 256, 256), 256), :])
-        r_scr[...] = dot(wc_scr[...], jnp.concatenate([gh, gh], axis=1), NT) + dot(wc_scr[:, 0:Z], gl, NT)
+        part = pl.ds(pl.multiple_of(n * 256, 256), 256)
+        gh, gl = split(g_scr[part, :])
+        gc_ref[part, 0:Z] = gh
+        gc_ref[part, Z : 2 * Z] = gl
+        r_scr[...] = dot(wc_scr[...], jnp.concatenate([gh, gh, gl], axis=1), NT)
         for ip in range(2):
             for ep in range(16):
                 x0 = r_scr[64 * ep : 64 * ep + 32, 128 * ip : 128 * ip + 128]
@@ -127,73 +136,86 @@
             put.wait()
 
 
-def outer_kernel(l0_ref, l1_ref, l2_ref, l3_ref, own_ref, other_ref, g_ref, oh_ref, ol_ref, bh_ref, bl_ref, gwo_ref, gwx_ref,
-                 a_scr, at_scr, b_scr, t_scr, r_scr, gc_scr, w_scr):
-    n = pl.program_id(0)
-
-    @pl.when(n == 0)
-    def _():
-        load_left((l0_ref, l1_ref, l2_ref, l3_ref), a_scr)
-        ath, atl = split(a_scr[...].T)
-        at_scr[:, 0:S] = ath
-        at_scr[:, S : 2 * S] = atl
-        for k in range(16):
-            b_scr[4 * k : 4 * k + 4, :] = own_ref[k]
-            b_scr[64 + 4 * k : 68 + 4 * k, :] = other_ref[k]
-        for m in range(16):
-            t_scr[128 * m : 128 * m + 128, :] = b_scr[:, 128 * m : 128 * m + 128].T
-        gh, gl = split(g_ref[...])
-        gc_scr[:, 0:Z] = gh
-        gc_scr[:, Z : 2 * Z] = gl
-
-    for e in range(8):
-        hi, lo = split(t_scr[pl.ds(8 * n + e, TJ, stride=C), :])
-        bh_ref[TJ * e : TJ * e + TJ, :] = hi
-        bl_ref[TJ * e : TJ * e + TJ, :] = lo
-    for h in range(2):
-        bh = bh_ref[256 * h : 256 * h + 256, :]
-        bl = bl_ref[256 * h : 256 * h + 256, :]
-        r_scr[h] = dot(at_scr[...], jnp.concatenate([bh, bh], axis=1), NT) + dot(at_scr[:, 0:S], bl, NT)
+def outer_kernel(at_ref, gc_ref, bias_ref, own_ref, other_ref, oh_hbm, ol_hbm, bc_hbm, gwo_ref, gwx_ref,
+                 b_scr, t_scr, bc_scr, r0_scr, r1_scr, oh_scr, ol_scr, w_scr, b_sem, o_sem):
+    for k in range(16):
+        b_scr[4 * k : 4 * k + 4, :] = own_ref[k]
+        b_scr[64 + 4 * k : 68 + 4 * k, :] = other_ref[k]
+    for m in range(16):
+        t_scr[128 * m : 128 * m + 128, :] = b_scr[:, 128 * m : 128 * m + 128].T
+    for e in range(C):
+        hi, lo = split(t_scr[pl.ds(e, TJ, stride=C), :])
+        rows = slice(TJ * e, TJ * e + TJ)
+        bc_scr[rows, 0:S] = hi
+        bc_scr[rows, S : 2 * S] = hi
+        bc_scr[rows, 2 * S : 3 * S] = lo
+    puts = [pltpu.make_async_copy(bc_scr.at[:, S : 3 * S], bc_hbm, b_sem.at[0])]
+    puts[0].start()
+    r_scr = (r0_scr, r1_scr)
+
+    def multiply(n):
+        r_scr[n % 2][...] = dot(at_ref[...], bc_scr[256 * n : 256 * n + 256, :], NT)
+
+    def weigh(m):
+        rows = slice(256 * m, 256 * m + 256)
+        hi = jnp.concatenate([oh_scr[q, rows, :] for q in range(4)], axis=1)
+        lo = jnp.concatenate([ol_scr[q, rows, :] for q in range(4)], axis=1)
+        r = dot(hi, gc_ref[...])
+        w_scr[rows, :] = (r[:, :Z] + r[:, Z:] + dot(lo, gc_ref[:, 0:Z])) * (1.0 / S)
+
+    multiply(0)
+    for n in range(8):
+        if n < 7:
+            multiply(n + 1)
+        if n in (2, 4, 6):
+            weigh(n // 2 - 1)
         for ep in range(2):
             for ip in range(8):
-                x0 = r_scr[h, 64 * ip : 64 * ip + 32, 128 * ep : 128 * ep + 128]
-                x1 = r_scr[h, 64 * ip + 32 : 64 * ip + 64, 128 * ep : 128 * ep + 128]
+                x0 = r_scr[n % 2][64 * ip : 64 * ip + 32, 128 * ep : 128 * ep + 128]
+                x1 = r_scr[n % 2][64 * ip + 32 : 64 * ip + 64, 128 * ep : 128 * ep + 128]
                 for k, y in enumerate(half_swap(x0, x1)):
                     hi, lo = split(y)
-                    row = (4 * h + 2 * ep + k) * C
-                    oh_ref[row : row + C, 128 * ip : 128 * ip + 128] = hi
-                    ol_ref[row : row + C, 128 * ip : 128 * ip + 128] = lo
-    r = dot(oh_ref[...], gc_scr[...])
-    rows = pl.ds(pl.multiple_of(n * 256, 256), 256)
-    w_scr[rows, :] = (r[:, :Z] + r[:, Z:] + dot(ol_ref[...], gc_scr[:, 0:Z])) * (1.0 / S)
-
-    @pl.when(n == 3)
-    def _():
-        core = core_index()
-        bias = jnp.broadcast_to(jnp.sum(g_ref[...], axis=0, keepdims=True), (8, Z))
-        for k in range(16):
-            lo = w_scr[pl.ds(k, C, stride=C), :]
-            hi = w_scr[pl.ds(16 + k, C, stride=C), :]
-            gwo_ref[k, 0:C, :] = jnp.where(core == 0, lo, hi)
-            gwx_ref[k, 0:C, :] = jnp.where(core == 0, hi, lo)
-            gwo_ref[k, C : C + 8, :] = bias
-            gwx_ref[k, C : C + 8, :] = bias
-
-
-def pair_kernel(oh_hbm, ol_hbm, w_hbm, b_ref, p_hbm, oh_scr, ol_scr, w_scr, wp_scr, wc_scr, p_scr, in_sem, out_sem):
-    get_w = pltpu.make_async_copy(w_hbm, w_scr, in_sem.at[0])
-    get_h = pltpu.make_async_copy(oh_hbm, oh_scr, in_sem.at[1])
-    get_l = pltpu.make_async_copy(ol_hbm, ol_scr, in_sem.at[2])
+                    row = (4 * n + 2 * ep + k) * C
+                    cols = slice(128 * (ip % 2), 128 * (ip % 2) + 128)
+                    oh_scr[ip // 2, row : row + C, cols] = hi
+                    ol_scr[ip // 2, row : row + C, cols] = lo
+        if n % 2 == 1:
+            rows = slice(128 * (n - 1), 128 * (n + 1))
+            for i, (src, dst) in enumerate(((oh_scr, oh_hbm), (ol_scr, ol_hbm))):
+                put = pltpu.make_async_copy(src.at[:, rows, :], dst.at[:, rows, :], o_sem.at[i, n // 2])
+                put.start()
+                puts.append(put)
+    weigh(3)
+    core = core_index()
+    for k in range(16):
+        lo = w_scr[pl.ds(k, C, stride=C), :]
+        hi = w_scr[pl.ds(16 + k, C, stride=C), :]
+        gwo_ref[k, 0:C, :] = jnp.where(core == 0, lo, hi)
+        gwx_ref[k, 0:C, :] = jnp.where(core == 0, hi, lo)
+        gwo_ref[k, C : C + 8, :] = bias_ref[...]
+        gwx_ref[k, C : C + 8, :] = bias_ref[...]
+    for put in puts:
+        put.wait()
+
+
+def pair_kernel(oh_hbm, ol_hbm, w_hbm, b_ref, p_hbm, oh_scr, ol_scr, w_scr, wp_scr, wc_scr, p_scr, w_sem, in_sem, out_sem):
+    get_w = pltpu.make_async_copy(w_hbm, w_scr, w_sem.at[0])
     get_w.start()
-    get_h.start()
-    get_l.start()
+
+    def gets(n):
+        return (
+            pltpu.make_async_copy(oh_hbm.at[n], oh_scr.at[n], in_sem.at[0, n]),
+            pltpu.make_async_copy(ol_hbm.at[n], ol_scr.at[n], in_sem.at[1, n]),
+        )
+
+    for n in range(4):
+        for get in gets(n):
+            get.start()
     get_w.wait()
     load_weight(w_scr, wp_scr)
     wth, wtl = split(wp_scr[...].T)
     wc_scr[0:Z, :] = wth
     wc_scr[Z : 2 * Z, :] = wtl
-    get_h.wait()
-    get_l.wait()
 
     def put(n):
         rows = pl.ds(pl.multiple_of(n * 256, 256), 256)
@@ -201,37 +223,46 @@
 
     @pl.loop(0, 4)
     def _(n):
-        cols = pl.ds(pl.multiple_of(n * 256, 256), 256)
-        r = dot(wc_scr[...], oh_scr[:, cols])
-        r = r[:Z] + r[Z:] + dot(wc_scr[0:Z, :], ol_scr[:, cols])
-        p_scr[cols, :] = (r * (1.0 / S)).T + b_ref[...]
+        for get in gets(n):
+            get.wait()
+        r = dot(wc_scr[...], oh_scr[n])
+        r = r[:Z] + r[Z:] + dot(wc_scr[0:Z, :], ol_scr[n])
+        p_scr[pl.ds(pl.multiple_of(n * 256, 256), 256), :] = (r * (1.0 / S)).T + b_ref[...]
         put(n).start()
 
     for n in range(4):
         put(n).wait()
 
 
-def grad_left_kernel(goh_ref, gol_ref, bh_ref, bl_ref, gl_ref, s_scr):
-    n = pl.program_id(0)
-
-    bh = bh_ref[...]
-    r = dot(goh_ref[...], jnp.concatenate([bh, bl_ref[...]], axis=1))
-    r = (r[:, :S] + r[:, S:] + dot(gol_ref[...], bh)) * (1.0 / S)
-    s_scr[:, pl.ds(pl.multiple_of(n * 256, 256), 256)] = r.T
-
-    @pl.when(n == 1)
-    def _():
-        core = core_index()
-        col = lax.axis_index("col")
-        for q in range(8):
-            own = s_scr[8 * q : 8 * q + 8, :]
-            other = s_scr[64 + 8 * q : 72 + 8 * q, :]
-            lo = jnp.where(core == 0, own, other)
-            hi = jnp.where(core == 0, other, own)
-            xx = slot_of((q % 4) ^ lax.rem(col, 4))
-            zz = lax.rem(q // 4 + 2 - col // 4, 2)
-            gl_ref[xx, zz, 0:8, :] = jnp.concatenate([lo[0:4], hi[0:4]], axis=0)
-            gl_ref[xx, zz, 8:16, :] = jnp.concatenate([lo[4:8], hi[4:8]], axis=0)
+def grad_left_kernel(goh_hbm, gol_hbm, bc_hbm, gl_ref, goh_scr, gol_scr, bc_scr, s_scr, b_sem, in_sem):
+    get_b = pltpu.make_async_copy(bc_hbm, bc_scr, b_sem.at[0])
+    get_b.start()
+    gets = []
+    for n in range(4):
+        rows = slice(128 * n, 128 * n + 128)
+        for i, (src, dst) in enumerate(((goh_hbm, goh_scr), (gol_hbm, gol_scr))):
+            get = pltpu.make_async_copy(src.at[rows, :], dst.at[rows, :], in_sem.at[i, n])
+            get.start()
+            gets.append(get)
+    get_b.wait()
+    for n in range(2):
+        for get in gets[4 * n : 4 * n + 4]:
+            get.wait()
+        rows = slice(256 * n, 256 * n + 256)
+        r = dot(goh_scr[rows, :], bc_scr[...])
+        r = (r[:, :S] + r[:, S:] + dot(gol_scr[rows, :], bc_scr[:, 0:S])) * (1.0 / S)
+        s_scr[:, rows] = r.T
+    core = core_index()
+    col = lax.axis_index("col")
+    for q in range(8):
+        own = s_scr[8 * q : 8 * q + 8, :]
+        other = s_scr[64 + 8 * q : 72 + 8 * q, :]
+        lo = jnp.where(core == 0, own, other)
+        hi = jnp.where(core == 0, other, own)
+        xx = slot_of((q % 4) ^ lax.rem(col, 4))
+        zz = lax.rem(q // 4 + 2 - col // 4, 2)
+        gl_ref[xx, zz, 0:8, :] = jnp.concatenate([lo[0:4], hi[0:4]], axis=0)
+        gl_ref[xx, zz, 8:16, :] = jnp.concatenate([lo[4:8], hi[4:8]], axis=0)
 
 
 def copies_kernel(x_ref, out_ref):
@@ -270,10 +301,6 @@
 
 def whole(shape):
     return pl.BlockSpec(shape, lambda n: (0,) * len(shape))
-
-
-def rows_of(shape):
-    return pl.BlockSpec(shape, lambda n: (n, 0))
 
 
 def call(kernel, ins, outs, scratch, flops, nbytes, steps=4, limit=40):
@@ -289,9 +316,7 @@
     )
 
 
-LEFT = whole((2, 16, IC))
 RIGHT = whole((16, 4, JE))
-WHOLE_G = whole((IJ, Z))
 WEIGHT = whole((CE, Z))
 ANY = pl.BlockSpec(memory_space=pl.ANY)
 VM = pl.BlockSpec(memory_space=pltpu.VMEM)
@@ -314,31 +339,34 @@
 grads_call = flat_call(
     grads_kernel,
     [VM] * 4 + [ANY] * 2,
-    [(pltpu.HBM((IC, JE), BF16), ANY)] * 2 + [GR_PART] * 2,
-    [((S, IC), F32), ((2 * S, IC), BF16), ((IJ, Z), F32), ((CE, Z), F32), ((CE, Z), F32), ((CE, 2 * Z), BF16),
+    [(pltpu.HBM((IC, JE), BF16), ANY)] * 2 + [GR_PART] * 2
+    + [(jax.ShapeDtypeStruct((IC, 3 * S), BF16), VM), (jax.ShapeDtypeStruct((IJ, 2 * Z), BF16), VM), (jax.ShapeDtypeStruct((8, Z), F32), VM)],
+    [((S, IC), F32), ((2 * S, IC), BF16), ((IJ, Z), F32), ((CE, Z), F32), ((CE, Z), F32), ((CE, 3 * Z), BF16),
      ((CE, 256), F32), ((IC, JE), BF16), ((IC, JE), BF16), ((JE, S), F32)],
     [(2,), (2, 4)],
     2 * 10**9, 6 << 20)
-outer_call = call(
+GW_PART = (jax.ShapeDtypeStruct((16, 40, Z), F32), VM)
+outer_call = flat_call(
     outer_kernel,
-    [LEFT, LEFT, LEFT, LEFT, RIGHT, RIGHT, WHOLE_G],
-    [((CE, IJ), BF16, rows_of((256, IJ)))] * 2 + [((JE, S), BF16, rows_of((512, S)))] * 2
-    + [((16, 40, Z), F32, whole((16, 40, Z)))] * 2,
-    [((S, IC), F32), ((IC, 2 * S), BF16), ((S, JE), F32), ((JE, S), F32), ((2, IC, 256), F32), ((IJ, 2 * Z), BF16), ((CE, Z), F32)],
+    [VM] * 5,
+    [(pltpu.HBM((4, CE, 256), BF16), ANY)] * 2 + [(pltpu.HBM((JE, 2 * S), BF16), ANY)] + [GW_PART] * 2,
+    [((S, JE), F32), ((JE, S), F32), ((JE, 3 * S), BF16), ((IC, 256), F32), ((IC, 256), F32), ((4, CE, 256), BF16), ((4, CE, 256), BF16), ((CE, Z), F32)],
+    [(1,), (2, 4)],
     2 * 10**9, 7 << 20)
 pair_call = flat_call(
     pair_kernel,
     [ANY] * 3 + [VM],
     [(pltpu.HBM((IJ, Z), F32), ANY)],
-    [((CE, IJ), BF16), ((CE, IJ), BF16), ((CE, Z), F32), ((CE, Z), F32), ((2 * Z, CE), BF16), ((IJ, Z), F32)],
-    [(3,), (4,)],
+    [((4, CE, 256), BF16), ((4, CE, 256), BF16), ((CE, Z), F32), ((CE, Z), F32), ((2 * Z, CE), BF16), ((IJ, Z), F32)],
+    [(1,), (2, 4), (4,)],
     10**9, 5 << 20)
-grad_left_call = call(
+grad_left_call = flat_call(
     grad_left_kernel,
-    [rows_of((256, JE))] * 2 + [whole((JE, S))] * 2,
-    [((4, 2, 16, IC), F32, whole((4, 2, 16, IC)))],
-    [((S, IC), F32)],
-    10**9, 6 << 20, 2)
+    [ANY] * 3,
+    [(jax.ShapeDtypeStruct((4, 2, 16, IC), F32), VM)],
+    [((IC, JE), BF16), ((IC, JE), BF16), ((JE, 2 * S), BF16), ((S, IC), F32)],
+    [(1,), (2, 4)],
+    10**9, 6 << 20)
 join_call = call(
     join_kernel,
     [whole((16, C, Z))] * 2 + [whole((2, 4, JE)), whole((4, JE)), whole((2, 16, IC)), whole((16, IC))],
@@ -382,14 +410,14 @@
     right_own = lax.all_to_all(copies, "row", 0, 0, axis_index_groups=YZ)
     left_pair = jnp.stack([left, left_far])
     pieces = [left_pair] + [lax.ppermute(left_pair, "col", p) for p in X_PERMS]
-    goh, gol, gr_own, gr_other = grads_call(*pieces, *in_hbm(g, w_out))
+    goh, gol, gr_own, gr_other, left_parts, g_parts, bias = grads_call(*pieces, *in_hbm(g, w_out))
     right_other = lax.ppermute(right_own, "row", CORE)
-    oh, ol, bh, bl, gw_own, gw_other = outer_call(*pieces, right_own, right_other, g)
+    oh, ol, bc, gw_own, gw_other = outer_call(left_parts, g_parts, bias, right_own, right_other)
     gw = gw_own + lax.ppermute(gw_other, "row", CORE)
-    gw, goh, gol, bh, bl = tie((gw, goh, gol, bh, bl))
+    gw, goh, gol, bc = tie((gw, goh, gol, bc))
     gw = lax.all_to_all(gw, BOTH, 0, 0, axis_index_groups=XY)
     gr = gr_own + lax.ppermute(gr_other, "row", CORE)
-    (gl,) = grad_left_call(*in_hbm(goh, gol, bh, bl))
+    (gl,) = grad_left_call(*in_hbm(goh, gol, bc))
     (gw,) = spread_call(gw)
     gw, oh, ol = tie((gw, oh, ol))
     gr = gr[:2] + lax.ppermute(gr[2:], "row", Y_FLIP[1])

time: 110 us -> 104 us (0.945)
  waiting for transfers between devices: 30.1 us -> 23.8 us
  Pallas kernels: 26.6 us -> 25.4 us
    all_to_all x1, waiting for transfers between devices: 8.83 us -> 2.48 us  [body(): gw = lax.all_to_all(gw, BOTH, 0, 0, axis_index_groups=XY)]
    pallas_call x3, Pallas kernels: 17.7 us -> 16.5 us  [the longest x1 7.83 us: body(): grads_call(*pieces, *in_hbm(g, w_out))]
    ppermute x3, starting transfers between devices: 4.81 us -> 3.6 us  [body(): pieces = [left_pair] + [lax.ppermute(left_pair, 'col', p) for p in X_PERMS]]
    ppermute x1, starting transfers between devices: 0.4 us -> 1.5 us  [body(): gl = gl[:2] + lax.ppermute(gl[2:], 'col', X_FLIP[1])]
  transfers between devices with their start and end apart: 19 -> 19, of which waited for: 6 -> 6; matrix products, arithmetic and copies ran while one was open for 1% -> 1% of each run, Pallas kernels for 23% -> 24%
where the time goes in v6:
time: 104 us; the launch traced here: 103 us
  starting transfers between devices  51 us (49%)
  Pallas kernels  25.4 us (24%)
  waiting for transfers between devices  23.8 us (23%)
  other arithmetic  1.82 us (2%)
    all_to_all x1, starting transfers between devices, body(): right_own = lax.all_to_all(copies, 'row', 0, 0, axis_index_groups=YZ)  10.7 us
    all_to_all x1, waiting for transfers between devices, body(): gw = lax.all_to_all(gw, BOTH, 0, 0, axis_index_groups=Z8)  8.17 us
    pallas_call x1, Pallas kernels, body(): grads_call(*pieces, *in_hbm(g, w_out))  7.83 us
    all_to_all x1, waiting for transfers between devices, body(): gw_own = lax.all_to_all(gw, BOTH, 0, 0, axis_index_groups=XY)  7.36 us
    all_to_all x1, starting transfers between devices, body(): gw = lax.all_to_all(gw, BOTH, 0, 0, axis_index_groups=Z8)  5.97 us
    pallas_call x1, Pallas kernels, body(): pair_out, = pair_call(*in_hbm(oh, ol, w_out), b_out.reshape(1, Z))  5.05 us
    pallas_call x1, Pallas kernels, body(): outer_call(left_parts, g_parts, bias, right_own, right_other)  4.67 us
    ppermute x1, starting transfers between devices, body(): gw_other = lax.ppermute(gw_own, 'row', CORE)  4.04 us
  transfers between devices with their start and end apart: 19, of which 6 were waited for; matrix products, arithmetic and copies ran while one was open for 1% of the time, Pallas kernels for 24%

profile of v6, /device:TPU:1, one launch (start us, length us, event | category | flops | bytes accessed | tf_op | source)
XLA Modules:
  0.0 102.9 jit_solution(14270803692650898660)
XLA Ops:
  0.6 2.5 %collective-permute-start = (f32[16,512]{1,0:T(8,128)}, f32[16,512]{1,0:T(8,128)S(1)}, u32[]{:S(2)}, u32[]{:S(2)}) collective-permute-start(f32[16,512]{1,0:T(8,128)} %param.5), channel_id=1, source_target_pairs={{0,4},{1,5},{2,6},{3,7},{4,0},{5,1},{6,2},{7,3},{8,12},{9,13},{10,... | collective-permute-start | bytes 98312 | tf_op jit(solution)/shard_map/ppermute | solution.py:408
  3.2 1.5 %collective-permute-done = f32[16,512]{1,0:T(8,128)S(1)} collective-permute-done((f32[16,512]{1,0:T(8,128)}, f32[16,512]{1,0:T(8,128)S(1)}, u32[]{:S(2)}, u32[]{:S(2)}) %collective-permute-start) | collective-permute-done | bytes 32800 | tf_op jit(solution)/shard_map/ppermute | solution.py:408
  4.7 0.8 pad_maximum_fusion.l0_ref
  5.5 2.5 %collective-permute-start.3 = (f32[2,16,512]{2,1,0:T(8,128)S(1)}, f32[2,16,512]{2,1,0:T(8,128)S(1)}, u32[]{:S(2)}, u32[]{:S(2)}) collective-permute-start(f32[2,16,512]{2,1,0:T(8,128)S(1)} %pad_maximum_fusion.l0_ref), channel_id=1, source_target_pairs={{0,3},{1,0},{2,1},{3,2},{4,7},{5,4},{6,5},{7,6},{8,11},{9,8},{10,9... | collective-permute-start | bytes 196616 | tf_op jit(solution)/shard_map/ppermute | solution.py:412
  7.9 0.5 collective-permute-start.2
  8.5 0.6 collective-permute-start.1
  9.1 1.6 %shard_map.93 = f32[16,4,2048]{2,1,0:T(4,128)} custom-call(f32[4,2048]{1,0:T(4,128)} %x_ref.1), custom_call_target="tpu_custom_call" | custom-call | flops 100000 | bytes 524288 | tf_op jit(solution)/shard_map/pallas_call | solution.py:409
  10.6 10.7 %all-to-all-start = ((f32[16,4,2048]{2,1,0:T(4,128)}), f32[16,4,2048]{2,1,0:T(4,128)S(1)}, u32[]{:S(2)}, u32[]{:S(2)}) async-start(f32[16,4,2048]{2,1,0:T(4,128)} %shard_map.93), calls=%async_computation | async-start | bytes 1048576 | tf_op jit(solution)/shard_map/all_to_all | solution.py:410
  21.4 0.0 collective-permute-done.3.l3_ref
  21.4 0.0 collective-permute-done.2.l2_ref
  21.4 0.0 collective-permute-done.1.l1_ref
  21.4 7.8 %shard_map.92 = (bf16[512,2048]{1,0:T(8,128)(2,1)}, bf16[512,2048]{1,0:T(8,128)(2,1)}, f32[4,4,4,2048]{3,2,1,0:T(4,128)S(1)}, f32[4,4,4,2048]{3,2,1,0:T(4,128)S(...) custom-call(f32[2,16,512]{2,1,0:T(8,128)S(1)} %pad_maximum_fusion.l0_ref, ...), custom_call_target="tpu_custom_call" | custom-call | flops 2000000000 | bytes 6291456 | tf_op jit(solution)/shard_map/pallas_call | solution.py:413
  29.3 3.0 %collective-permute-start.7 = (f32[4,4,4,2048]{3,2,1,0:T(4,128)S(1)}, f32[4,4,4,2048]{3,2,1,0:T(4,128)S(1)}, u32[]{:S(2)}, u32[]{:S(2)}) collective-permute-start(f32[4,4,4,2048]{3,2,1,0:T(4,128)S(1)} %get-tuple-element.45), channel_id=1, source_target_pairs={{0,8},{8,0},{16,24},{24,16},{32,40},{40,32},{48,56},{56,48},{64,72... | collective-permute-start | bytes 1572872 | tf_op jit(solution)/shard_map/ppermute | solution.py:419
  32.3 1.5 %collective-permute-done.7 = f32[4,4,4,2048]{3,2,1,0:T(4,128)S(1)} collective-permute-done((f32[4,4,4,2048]{3,2,1,0:T(4,128)S(1)}, f32[4,4,4,2048]{3,2,1,0:T(4,128)S(1)}, u32[]{:S(2)}, u32[]{:S(2)}) %collective-permute-start.7) | collective-permute-done | bytes 524320 | tf_op jit(solution)/shard_map/ppermute | solution.py:419
  33.8 0.1 add.22
  34.0 1.7 %collective-permute-start.8 = (f32[2,4,4,2048]{3,2,1,0:T(4,128)S(1)}, f32[2,4,4,2048]{3,2,1,0:T(4,128)S(1)}, u32[]{:S(2)}, u32[]{:S(2)}) collective-permute-start(f32[2,4,4,2048]{3,2,1,0:T(4,128)S(1)} %slice.49), channel_id=1, source_target_pairs={{0,16},{8,24},{16,0},{24,8},{32,48},{40,56},{48,32},{56,40},{64,80... | collective-permute-start | bytes 786440 | tf_op jit(solution)/shard_map/ppermute | solution.py:423
  35.7 0.0 all-to-all-done.own_ref
  35.7 3.9 %collective-permute-start.4 = (f32[16,4,2048]{2,1,0:T(4,128)S(1)}, f32[16,4,2048]{2,1,0:T(4,128)S(1)}, u32[]{:S(2)}, u32[]{:S(2)}) collective-permute-start(f32[16,4,2048]{2,1,0:T(4,128)S(1)} %all-to-all-done.own_ref), channel_id=1, source_target_pairs={{0,8},{8,0},{16,24},{24,16},{32,40},{40,32},{48,56},{56,48},{64,72... | collective-permute-start | bytes 1572872 | tf_op jit(solution)/shard_map/ppermute | solution.py:414
  39.6 2.7 %collective-permute-done.8 = f32[2,4,4,2048]{3,2,1,0:T(4,128)S(1)} collective-permute-done((f32[2,4,4,2048]{3,2,1,0:T(4,128)S(1)}, f32[2,4,4,2048]{3,2,1,0:T(4,128)S(1)}, u32[]{:S(2)}, u32[]{:S(2)}) %collective-permute-start.8) | collective-permute-done | bytes 262176 | tf_op jit(solution)/shard_map/ppermute | solution.py:423
  42.3 0.1 slice_add_fusion
  42.4 2.9 %collective-permute-start.9 = (f32[4,4,2048]{2,1,0:T(4,128)S(1)}, f32[4,4,2048]{2,1,0:T(4,128)S(1)}, u32[]{:S(2)}, u32[]{:S(2)}) collective-permute-start(f32[4,4,2048]{2,1,0:T(4,128)S(1)} %slice_bitcast_fusion), channel_id=1, source_target_pairs={{0,48},{8,56},{16,32},{24,40},{32,16},{40,24},{48,0},{56,8},{64,11... | collective-permute-start | bytes 393224 | tf_op jit(solution)/shard_map/ppermute | solution.py:424
  45.3 0.0 collective-permute-done.4.other_ref
  45.3 4.7 %shard_map.94 = (bf16[4,1024,256]{2,1,0:T(8,128)(2,1)}, bf16[4,1024,256]{2,1,0:T(8,128)(2,1)}, bf16[2048,256]{1,0:T(8,128)(2,1)}, f32[16,40,128]{2,1,0:T(8,128)S(1)}, f32[16,40,128]{2,1,0:T(8,128)S(1)}) custom-call(bf16[512,384]{1,0:T(8,128)(2,1)S(1)} %get-tuple-element.29.at_ref, bf16[1024,256]{1,0:T(8,128)(2,1)S(1)} %get-tuple-element.30.gc_ref, ...), custom_call_target="tpu_custom_call" | custom-call | flops 2000000000 | bytes 7340032 | tf_op jit(solution)/shard_map/pallas_call | solution.py:415
  50.0 1.2 %collective-permute-start.5 = (f32[16,40,128]{2,1,0:T(8,128)S(1)}, f32[16,40,128]{2,1,0:T(8,128)S(1)}, u32[]{:S(2)}, u32[]{:S(2)}) collective-permute-start(f32[16,40,128]{2,1,0:T(8,128)S(1)} %get-tuple-element.33), channel_id=1, source_target_pairs={{0,8},{8,0},{16,24},{24,16},{32,40},{40,32},{48,56},{56,48},{64,72... | collective-permute-start | bytes 983048 | tf_op jit(solution)/shard_map/ppermute | solution.py:416
  51.2 0.0 collective-permute-done.9
  51.3 2.2 %collective-permute-start.10 = (f32[2,4,2048]{2,1,0:T(4,128)S(1)}, f32[2,4,2048]{2,1,0:T(4,128)S(1)}, u32[]{:S(2)}, u32[]{:S(2)}) collective-permute-start(f32[2,4,2048]{2,1,0:T(4,128)S(1)} %slice.53), channel_id=1, source_target_pairs={{0,64},{8,72},{16,80},{24,88},{32,96},{40,104},{48,112},{56,120},{... | collective-permute-start | bytes 196616 | tf_op jit(solution)/shard_map/ppermute | solution.py:430
  53.5 0.0 collective-permute-done.5
  53.5 0.8 add.21
  54.3 3.5 %all-to-all-start.1 = ((f32[16,40,128]{2,1,0:T(8,128)}), f32[16,40,128]{2,1,0:T(8,128)S(1)}, u32[]{:S(2)}, u32[]{:S(2)}) async-start(f32[16,40,128]{2,1,0:T(8,128)} %add.21), calls=%async_computation.1 | async-start | bytes 655360 | tf_op jit(solution)/shard_map/all_to_all | solution.py:418
  57.8 4.0 %shard_map.98 = f32[4,2,16,512]{3,2,1,0:T(8,128)S(1)} custom-call(bf16[512,2048]{1,0:T(8,128)(2,1)} %get-tuple-element.46.goh_hbm, bf16[512,2048]{1,0:T(8,128)(2,1)} %get-tuple-element.47.gol_hbm, bf16[2048,256]{1,0:T(8,128)(2,1)} %get-tuple-element.48.bc_hbm), custom_call_target="tpu_custom_call" | custom-call | flops 1000000000 | bytes 6291456 | tf_op jit(solution)/shard_map/pallas_call | solution.py:420
  61.8 0.0 copy-start
  61.9 1.5 %collective-permute-start.12 = (f32[2,2,16,512]{3,2,1,0:T(8,128)S(1)}, f32[2,2,16,512]{3,2,1,0:T(8,128)S(1)}, u32[]{:S(2)}, u32[]{:S(2)}) collective-permute-start(f32[2,2,16,512]{3,2,1,0:T(8,128)S(1)} %slice.56), channel_id=1, source_target_pairs={{0,1},{1,0},{2,3},{3,2},{4,5},{5,4},{6,7},{7,6},{8,9},{9,8},{10,11... | collective-permute-start | bytes 393224 | tf_op jit(solution)/shard_map/ppermute | solution.py:425
  63.4 0.0 collective-permute-done.10
  63.4 2.5 %all-to-all-done.1.x_ref = f32[16,40,128]{2,1,0:T(8,128)S(1)} async-done(((f32[16,40,128]{2,1,0:T(8,128)}), f32[16,40,128]{2,1,0:T(8,128)S(1)}, u32[]{:S(2)}, u32[]{:S(2)}) %all-to-all-start.1) | async-done | bytes 327712 | tf_op jit(solution)/shard_map/all_to_all | solution.py:418
  65.9 0.7 shard_map.95
  66.6 6.0 %all-to-all-start.2 = ((f32[8,40,128]{2,1,0:T(8,128)}), f32[8,40,128]{2,1,0:T(8,128)S(1)}, u32[]{:S(2)}, u32[]{:S(2)}) async-start(f32[8,40,128]{2,1,0:T(8,128)} %shard_map.95), calls=%async_computation.2 | async-start | bytes 327680 | tf_op jit(solution)/shard_map/all_to_all | solution.py:427
  72.5 0.0 collective-permute-done.12
  72.6 0.1 collective-permute-start.13
  72.7 8.2 %all-to-all-done.2.x_ref = f32[8,40,128]{2,1,0:T(8,128)S(1)} async-done(((f32[8,40,128]{2,1,0:T(8,128)}), f32[8,40,128]{2,1,0:T(8,128)S(1)}, u32[]{:S(2)}, u32[]{:S(2)}) %all-to-all-start.2) | async-done | bytes 163872 | tf_op jit(solution)/shard_map/all_to_all | solution.py:427
  80.9 0.7 shard_map.97
  81.6 3.5 %all-to-all-start.3 = ((f32[16,32,128]{2,1,0:T(8,128)}), f32[16,32,128]{2,1,0:T(8,128)S(1)}, u32[]{:S(2)}, u32[]{:S(2)}) async-start(f32[16,32,128]{2,1,0:T(8,128)} %get-tuple-element.43), calls=%async_computation.3 | async-start | bytes 524288 | tf_op jit(solution)/shard_map/all_to_all | solution.py:433
  85.2 0.1 collective-permute-start.11
  85.3 0.0 collective-permute-done.13
  85.3 7.4 %all-to-all-done.3.own_ref = f32[16,32,128]{2,1,0:T(8,128)S(1)} async-done(((f32[16,32,128]{2,1,0:T(8,128)}), f32[16,32,128]{2,1,0:T(8,128)S(1)}, u32[]{:S(2)}, u32[]{:S(2)}) %all-to-all-start.3) | async-done | bytes 262176 | tf_op jit(solution)/shard_map/all_to_all | solution.py:433
  92.7 4.0 %collective-permute-start.6 = (f32[16,32,128]{2,1,0:T(8,128)S(1)}, f32[16,32,128]{2,1,0:T(8,128)S(1)}, u32[]{:S(2)}, u32[]{:S(2)}) collective-permute-start(f32[16,32,128]{2,1,0:T(8,128)S(1)} %all-to-all-done.3.own_ref), channel_id=1, source_target_pairs={{0,8},{8,0},{16,24},{24,16},{32,40},{40,32},{48,56},{56,48},{64,72... | collective-permute-start | bytes 786440 | tf_op jit(solution)/shard_map/ppermute | solution.py:434
  96.7 0.3 collective-permute-start.14
  97.0 0.0 copy-done
  97.0 5.1 %shard_map.96 = f32[1024,128]{1,0:T(8,128)} custom-call(bf16[4,1024,256]{2,1,0:T(8,128)(2,1)} %get-tuple-element.40.oh_hbm, bf16[4,1024,256]{2,1,0:T(8,128)(2,1)} %get-tuple-element.41.ol_hbm, f32[1024,128]{1,0:T(8,128)} %w_hbm.3, f32[1,128]{1,0:T(1,128)S(1)} %bitcast.22), custom_call_target="tpu_custom_call" | custom-call | flops 1000000000 | bytes 5242880 | tf_op jit(solution)/shard_map/pallas_call | solution.py:428
  102.1 0.0 collective-permute-done.11.r1_ref
  102.1 0.0 collective-permute-done.14.l1_ref
  102.1 0.0 collective-permute-done.6.other_ref
  102.1 0.8 shard_map.99
  (11 shorter events, 0.2 us)
Async XLA Ops:
  0.6 4.1 %collective-permute-start = (f32[16,512]{1,0:T(8,128)}, f32[16,512]{1,0:T(8,128)S(1)}, u32[]{:S(2)}, u32[]{:S(2)}) collective-permute-start(f32[16,512]{1,0:T(8,128)} %param.5), channel_id=1, source_target_pairs={{0,4},{1,5},{2,6},{3,7},{4,0},{5,1},{6,2},{7,3},{8,12},{9,13},{10,... | collective-permute-start | bytes 98312 | tf_op jit(solution)/shard_map/ppermute | solution.py:408
  5.5 15.9 %collective-permute-start.3 = (f32[2,16,512]{2,1,0:T(8,128)S(1)}, f32[2,16,512]{2,1,0:T(8,128)S(1)}, u32[]{:S(2)}, u32[]{:S(2)}) collective-permute-start(f32[2,16,512]{2,1,0:T(8,128)S(1)} %pad_maximum_fusion.l0_ref), channel_id=1, source_target_pairs={{0,3},{1,0},{2,1},{3,2},{4,7},{5,4},{6,5},{7,6},{8,11},{9,8},{10,9... | collective-permute-start | bytes 196616 | tf_op jit(solution)/shard_map/ppermute | solution.py:412
  7.9 13.5 %collective-permute-start.2 = (f32[2,16,512]{2,1,0:T(8,128)S(1)}, f32[2,16,512]{2,1,0:T(8,128)S(1)}, u32[]{:S(2)}, u32[]{:S(2)}) collective-permute-start(f32[2,16,512]{2,1,0:T(8,128)S(1)} %pad_maximum_fusion.l0_ref), channel_id=1, source_target_pairs={{0,2},{1,3},{2,0},{3,1},{4,6},{5,7},{6,4},{7,5},{8,10},{9,11},{10,... | collective-permute-start | bytes 196616 | tf_op jit(solution)/shard_map/ppermute | solution.py:412
  8.5 13.0 %collective-permute-start.1 = (f32[2,16,512]{2,1,0:T(8,128)S(1)}, f32[2,16,512]{2,1,0:T(8,128)S(1)}, u32[]{:S(2)}, u32[]{:S(2)}) collective-permute-start(f32[2,16,512]{2,1,0:T(8,128)S(1)} %pad_maximum_fusion.l0_ref), channel_id=1, source_target_pairs={{0,1},{1,2},{2,3},{3,0},{4,5},{5,6},{6,7},{7,4},{8,9},{9,10},{10,1... | collective-permute-start | bytes 196616 | tf_op jit(solution)/shard_map/ppermute | solution.py:412
  10.6 25.1 %all-to-all-start = ((f32[16,4,2048]{2,1,0:T(4,128)}), f32[16,4,2048]{2,1,0:T(4,128)S(1)}, u32[]{:S(2)}, u32[]{:S(2)}) async-start(f32[16,4,2048]{2,1,0:T(4,128)} %shard_map.93), calls=%async_computation | async-start | bytes 1048576 | tf_op jit(solution)/shard_map/all_to_all | solution.py:410
  29.3 4.6 %collective-permute-start.7 = (f32[4,4,4,2048]{3,2,1,0:T(4,128)S(1)}, f32[4,4,4,2048]{3,2,1,0:T(4,128)S(1)}, u32[]{:S(2)}, u32[]{:S(2)}) collective-permute-start(f32[4,4,4,2048]{3,2,1,0:T(4,128)S(1)} %get-tuple-element.45), channel_id=1, source_target_pairs={{0,8},{8,0},{16,24},{24,16},{32,40},{40,32},{48,56},{56,48},{64,72... | collective-permute-start | bytes 1572872 | tf_op jit(solution)/shard_map/ppermute | solution.py:419
  34.0 8.3 %collective-permute-start.8 = (f32[2,4,4,2048]{3,2,1,0:T(4,128)S(1)}, f32[2,4,4,2048]{3,2,1,0:T(4,128)S(1)}, u32[]{:S(2)}, u32[]{:S(2)}) collective-permute-start(f32[2,4,4,2048]{3,2,1,0:T(4,128)S(1)} %slice.49), channel_id=1, source_target_pairs={{0,16},{8,24},{16,0},{24,8},{32,48},{40,56},{48,32},{56,40},{64,80... | collective-permute-start | bytes 786440 | tf_op jit(solution)/shard_map/ppermute | solution.py:423
  35.7 9.6 %collective-permute-start.4 = (f32[16,4,2048]{2,1,0:T(4,128)S(1)}, f32[16,4,2048]{2,1,0:T(4,128)S(1)}, u32[]{:S(2)}, u32[]{:S(2)}) collective-permute-start(f32[16,4,2048]{2,1,0:T(4,128)S(1)} %all-to-all-done.own_ref), channel_id=1, source_target_pairs={{0,8},{8,0},{16,24},{24,16},{32,40},{40,32},{48,56},{56,48},{64,72... | collective-permute-start | bytes 1572872 | tf_op jit(solution)/shard_map/ppermute | solution.py:414
  42.4 8.9 %collective-permute-start.9 = (f32[4,4,2048]{2,1,0:T(4,128)S(1)}, f32[4,4,2048]{2,1,0:T(4,128)S(1)}, u32[]{:S(2)}, u32[]{:S(2)}) collective-permute-start(f32[4,4,2048]{2,1,0:T(4,128)S(1)} %slice_bitcast_fusion), channel_id=1, source_target_pairs={{0,48},{8,56},{16,32},{24,40},{32,16},{40,24},{48,0},{56,8},{64,11... | collective-permute-start | bytes 393224 | tf_op jit(solution)/shard_map/ppermute | solution.py:424
  50.0 3.5 %collective-permute-start.5 = (f32[16,40,128]{2,1,0:T(8,128)S(1)}, f32[16,40,128]{2,1,0:T(8,128)S(1)}, u32[]{:S(2)}, u32[]{:S(2)}) collective-permute-start(f32[16,40,128]{2,1,0:T(8,128)S(1)} %get-tuple-element.33), channel_id=1, source_target_pairs={{0,8},{8,0},{16,24},{24,16},{32,40},{40,32},{48,56},{56,48},{64,72... | collective-permute-start | bytes 983048 | tf_op jit(solution)/shard_map/ppermute | solution.py:416
  51.3 12.1 %collective-permute-start.10 = (f32[2,4,2048]{2,1,0:T(4,128)S(1)}, f32[2,4,2048]{2,1,0:T(4,128)S(1)}, u32[]{:S(2)}, u32[]{:S(2)}) collective-permute-start(f32[2,4,2048]{2,1,0:T(4,128)S(1)} %slice.53), channel_id=1, source_target_pairs={{0,64},{8,72},{16,80},{24,88},{32,96},{40,104},{48,112},{56,120},{... | collective-permute-start | bytes 196616 | tf_op jit(solution)/shard_map/ppermute | solution.py:430
  54.3 11.6 %all-to-all-start.1 = ((f32[16,40,128]{2,1,0:T(8,128)}), f32[16,40,128]{2,1,0:T(8,128)S(1)}, u32[]{:S(2)}, u32[]{:S(2)}) async-start(f32[16,40,128]{2,1,0:T(8,128)} %add.21), calls=%async_computation.1 | async-start | bytes 655360 | tf_op jit(solution)/shard_map/all_to_all | solution.py:418
  61.8 35.2 %copy-start = (f32[128]{0:T(128)S(1)}, f32[128]{0:T(128)}, u32[]{:S(2)}) copy-start(f32[128]{0:T(128)} %param.8) | copy-start | bytes 1540
  61.9 10.7 %collective-permute-start.12 = (f32[2,2,16,512]{3,2,1,0:T(8,128)S(1)}, f32[2,2,16,512]{3,2,1,0:T(8,128)S(1)}, u32[]{:S(2)}, u32[]{:S(2)}) collective-permute-start(f32[2,2,16,512]{3,2,1,0:T(8,128)S(1)} %slice.56), channel_id=1, source_target_pairs={{0,1},{1,0},{2,3},{3,2},{4,5},{5,4},{6,7},{7,6},{8,9},{9,8},{10,11... | collective-permute-start | bytes 393224 | tf_op jit(solution)/shard_map/ppermute | solution.py:425
  66.6 14.3 %all-to-all-start.2 = ((f32[8,40,128]{2,1,0:T(8,128)}), f32[8,40,128]{2,1,0:T(8,128)S(1)}, u32[]{:S(2)}, u32[]{:S(2)}) async-start(f32[8,40,128]{2,1,0:T(8,128)} %shard_map.95), calls=%async_computation.2 | async-start | bytes 327680 | tf_op jit(solution)/shard_map/all_to_all | solution.py:427
  72.6 12.7 %collective-permute-start.13 = (f32[2,16,512]{2,1,0:T(8,128)S(1)}, f32[2,16,512]{2,1,0:T(8,128)S(1)}, u32[]{:S(2)}, u32[]{:S(2)}) collective-permute-start(f32[2,16,512]{2,1,0:T(8,128)S(1)} %slice_bitcast_fusion.2), channel_id=1, source_target_pairs={{0,3},{1,2},{2,1},{3,0},{4,7},{5,6},{6,5},{7,4},{8,11},{9,10},{10,... | collective-permute-start | bytes 196616 | tf_op jit(solution)/shard_map/ppermute | solution.py:426
  81.6 11.1 %all-to-all-start.3 = ((f32[16,32,128]{2,1,0:T(8,128)}), f32[16,32,128]{2,1,0:T(8,128)S(1)}, u32[]{:S(2)}, u32[]{:S(2)}) async-start(f32[16,32,128]{2,1,0:T(8,128)} %get-tuple-element.43), calls=%async_computation.3 | async-start | bytes 524288 | tf_op jit(solution)/shard_map/all_to_all | solution.py:433
  85.2 16.9 %collective-permute-start.11 = (f32[4,2048]{1,0:T(4,128)S(1)}, f32[4,2048]{1,0:T(4,128)S(1)}, u32[]{:S(2)}, u32[]{:S(2)}) collective-permute-start(f32[4,2048]{1,0:T(4,128)S(1)} %slice_bitcast_fusion.5), channel_id=1, source_target_pairs={{0,192},{8,200},{16,208},{24,216},{32,224},{40,232},{48,240},{56,2... | collective-permute-start | bytes 98312 | tf_op jit(solution)/shard_map/ppermute | solution.py:431
  92.7 9.4 %collective-permute-start.6 = (f32[16,32,128]{2,1,0:T(8,128)S(1)}, f32[16,32,128]{2,1,0:T(8,128)S(1)}, u32[]{:S(2)}, u32[]{:S(2)}) collective-permute-start(f32[16,32,128]{2,1,0:T(8,128)S(1)} %all-to-all-done.3.own_ref), channel_id=1, source_target_pairs={{0,8},{8,0},{16,24},{24,16},{32,40},{40,32},{48,56},{56,48},{64,72... | collective-permute-start | bytes 786440 | tf_op jit(solution)/shard_map/ppermute | solution.py:434
  96.7 5.4 %collective-permute-start.14 = (f32[16,512]{1,0:T(8,128)S(1)}, f32[16,512]{1,0:T(8,128)S(1)}, u32[]{:S(2)}, u32[]{:S(2)}) collective-permute-start(f32[16,512]{1,0:T(8,128)S(1)} %slice_bitcast_fusion.4), channel_id=1, source_target_pairs={{0,4},{1,5},{2,6},{3,7},{4,0},{5,1},{6,2},{7,3},{8,12},{9,13},{10,... | collective-permute-start | bytes 98312 | tf_op jit(solution)/shard_map/ppermute | solution.py:432

commit v7 on v6

--- a/solution.py
+++ b/solution.py
@@ -1,3 +1,5 @@
+import functools
+
 import jax
 import jax.numpy as jnp
 from jax import lax
@@ -129,8 +131,8 @@
         for k in range(16):
             yy = slot_of((k % 4) ^ y)
             zz = slot_of((k // 4) ^ z)
-            own_ref[yy, zz, :, 128 * m : 128 * m + 128] = block[4 * k : 4 * k + 4]
-            other_ref[yy, zz, :, 128 * m : 128 * m + 128] = block[64 + 4 * k : 68 + 4 * k]
+            own_ref[zz, yy, :, 128 * m : 128 * m + 128] = block[4 * k : 4 * k + 4]
+            other_ref[zz, yy, :, 128 * m : 128 * m + 128] = block[64 + 4 * k : 68 + 4 * k]
     for n in range(4):
         for put in puts(n):
             put.wait()
@@ -157,7 +159,7 @@
         r_scr[n % 2][...] = dot(at_ref[...], bc_scr[256 * n : 256 * n + 256, :], NT)
 
     def weigh(m):
-        rows = slice(256 * m, 256 * m + 256)
+        rows = slice(512 * m, 512 * m + 512)
         hi = jnp.concatenate([oh_scr[q, rows, :] for q in range(4)], axis=1)
         lo = jnp.concatenate([ol_scr[q, rows, :] for q in range(4)], axis=1)
         r = dot(hi, gc_ref[...])
@@ -167,8 +169,8 @@
     for n in range(8):
         if n < 7:
             multiply(n + 1)
-        if n in (2, 4, 6):
-            weigh(n // 2 - 1)
+        if n == 4:
+            weigh(0)
         for ep in range(2):
             for ip in range(8):
                 x0 = r_scr[n % 2][64 * ip : 64 * ip + 32, 128 * ep : 128 * ep + 128]
@@ -185,7 +187,7 @@
                 put = pltpu.make_async_copy(src.at[:, rows, :], dst.at[:, rows, :], o_sem.at[i, n // 2])
                 put.start()
                 puts.append(put)
-    weigh(3)
+    weigh(1)
     core = core_index()
     for k in range(16):
         lo = w_scr[pl.ds(k, C, stride=C), :]
@@ -198,40 +200,35 @@
         put.wait()
 
 
-def pair_kernel(oh_hbm, ol_hbm, w_hbm, b_ref, p_hbm, oh_scr, ol_scr, w_scr, wp_scr, wc_scr, p_scr, w_sem, in_sem, out_sem):
+def pair_kernel(first, oh_hbm, ol_hbm, w_hbm, b_ref, *refs):
+    p_hbm, oh_scr, ol_scr, w_scr, wp_scr, wc_scr, p_scr, w_sem, in_sem, out_sem = refs[-10:]
     get_w = pltpu.make_async_copy(w_hbm, w_scr, w_sem.at[0])
     get_w.start()
-
-    def gets(n):
-        return (
-            pltpu.make_async_copy(oh_hbm.at[n], oh_scr.at[n], in_sem.at[0, n]),
-            pltpu.make_async_copy(ol_hbm.at[n], ol_scr.at[n], in_sem.at[1, n]),
-        )
-
-    for n in range(4):
-        for get in gets(n):
+    gets = []
+    for n in range(2):
+        for i, (src, dst) in enumerate(((oh_hbm, oh_scr), (ol_hbm, ol_scr))):
+            get = pltpu.make_async_copy(src.at[first + n], dst.at[n], in_sem.at[i, n])
             get.start()
+            gets.append(get)
     get_w.wait()
     load_weight(w_scr, wp_scr)
     wth, wtl = split(wp_scr[...].T)
     wc_scr[0:Z, :] = wth
     wc_scr[Z : 2 * Z, :] = wtl
-
-    def put(n):
-        rows = pl.ds(pl.multiple_of(n * 256, 256), 256)
-        return pltpu.make_async_copy(p_scr.at[rows, :], p_hbm.at[rows, :], out_sem.at[n])
-
-    @pl.loop(0, 4)
-    def _(n):
-        for get in gets(n):
+    puts = []
+    for n in range(2):
+        for get in gets[2 * n : 2 * n + 2]:
             get.wait()
         r = dot(wc_scr[...], oh_scr[n])
         r = r[:Z] + r[Z:] + dot(wc_scr[0:Z, :], ol_scr[n])
-        p_scr[pl.ds(pl.multiple_of(n * 256, 256), 256), :] = (r * (1.0 / S)).T + b_ref[...]
-        put(n).start()
-
-    for n in range(4):
-        put(n).wait()
+        p_scr[256 * n : 256 * n + 256, :] = (r * (1.0 / S)).T + b_ref[...]
+        put = pltpu.make_async_copy(
+            p_scr.at[256 * n : 256 * n + 256, :],
+            p_hbm.at[256 * (first + n) : 256 * (first + n) + 256, :], out_sem.at[n])
+        put.start()
+        puts.append(put)
+    for put in puts:
+        put.wait()
 
 
 def grad_left_kernel(goh_hbm, gol_hbm, bc_hbm, gl_ref, goh_scr, gol_scr, bc_scr, s_scr, b_sem, in_sem):
@@ -245,13 +242,10 @@
             get.start()
             gets.append(get)
     get_b.wait()
-    for n in range(2):
-        for get in gets[4 * n : 4 * n + 4]:
-            get.wait()
-        rows = slice(256 * n, 256 * n + 256)
-        r = dot(goh_scr[rows, :], bc_scr[...])
-        r = (r[:, :S] + r[:, S:] + dot(gol_scr[rows, :], bc_scr[:, 0:S])) * (1.0 / S)
-        s_scr[:, rows] = r.T
+    for get in gets:
+        get.wait()
+    r = dot(goh_scr[...], bc_scr[...])
+    s_scr[...] = ((r[:, :S] + r[:, S:] + dot(gol_scr[...], bc_scr[:, 0:S])) * (1.0 / S)).T
     core = core_index()
     col = lax.axis_index("col")
     for q in range(8):
@@ -323,13 +317,14 @@
 DMA = pltpu.SemaphoreType.DMA
 
 
-def flat_call(kernel, ins, outs, scratch, sems, flops, nbytes):
+def flat_call(kernel, ins, outs, scratch, sems, flops, nbytes, alias=None):
     return pl.pallas_call(
         kernel,
         in_specs=ins,
         out_specs=[spec for _, spec in outs],
         out_shape=[shape for shape, _ in outs],
         scratch_shapes=[pltpu.VMEM(s, d) for s, d in scratch] + [DMA(s) for s in sems],
+        input_output_aliases=alias or {},
         cost_estimate=pl.CostEstimate(flops=flops, bytes_accessed=nbytes, transcendentals=0),
         compiler_params=pltpu.CompilerParams(vmem_limit_bytes=40 << 20),
     )
@@ -353,13 +348,16 @@
     [((S, JE), F32), ((JE, S), F32), ((JE, 3 * S), BF16), ((IC, 256), F32), ((IC, 256), F32), ((4, CE, 256), BF16), ((4, CE, 256), BF16), ((CE, Z), F32)],
     [(1,), (2, 4)],
     2 * 10**9, 7 << 20)
-pair_call = flat_call(
-    pair_kernel,
-    [ANY] * 3 + [VM],
-    [(pltpu.HBM((IJ, Z), F32), ANY)],
-    [((4, CE, 256), BF16), ((4, CE, 256), BF16), ((CE, Z), F32), ((CE, Z), F32), ((2 * Z, CE), BF16), ((IJ, Z), F32)],
-    [(1,), (2, 4), (4,)],
-    10**9, 5 << 20)
+pair_calls = [
+    flat_call(
+        functools.partial(pair_kernel, first),
+        [ANY] * 3 + [VM] + [ANY] * (first // 2),
+        [(pltpu.HBM((IJ, Z), F32), ANY)],
+        [((2, CE, 256), BF16), ((2, CE, 256), BF16), ((CE, Z), F32), ((CE, Z), F32), ((2 * Z, CE), BF16), ((512, Z), F32)],
+        [(1,), (2, 2), (2,)],
+        5 * 10**8, 3 << 20, {4: 0} if first else None)
+    for first in (0, 2)
+]
 grad_left_call = flat_call(
     grad_left_kernel,
     [ANY] * 3,
@@ -420,15 +418,16 @@
     (gl,) = grad_left_call(*in_hbm(goh, gol, bc))
     (gw,) = spread_call(gw)
     gw, oh, ol = tie((gw, oh, ol))
-    gr = gr[:2] + lax.ppermute(gr[2:], "row", Y_FLIP[1])
-    gr = gr[0] + lax.ppermute(gr[1], "row", Y_FLIP[3])
+    gr = gr[:2] + lax.ppermute(gr[2:], "row", Z_FLIP[1])
+    gr = gr[0] + lax.ppermute(gr[1], "row", Z_FLIP[3])
     gl = gl[:2] + lax.ppermute(gl[2:], "col", X_FLIP[1])
     gl = gl[0] + lax.ppermute(gl[1], "col", X_FLIP[3])
     gw = lax.all_to_all(gw, BOTH, 0, 0, axis_index_groups=Z8)
-    (pair_out,) = pair_call(*in_hbm(oh, ol, w_out), b_out.reshape(1, Z))
+    (pair_half,) = pair_calls[0](*in_hbm(oh, ol, w_out), b_out.reshape(1, Z))
+    (pair_out,) = pair_calls[1](*in_hbm(oh, ol, w_out), b_out.reshape(1, Z), pair_half)
     gw, grad_bias = final_call(gw)
-    gr = gr[:2] + lax.ppermute(gr[2:], "row", Z_FLIP[1])
-    gr_part = lax.ppermute(gr[1], "row", Z_FLIP[3])
+    gr = gr[:2] + lax.ppermute(gr[2:], "row", Y_FLIP[1])
+    gr_part = lax.ppermute(gr[1], "row", Y_FLIP[3])
     gl_part = lax.ppermute(gl[1], "col", H_PERM)
     gw_own = lax.all_to_all(gw, BOTH, 0, 0, axis_index_groups=XY)
     gw_other = lax.ppermute(gw_own, "row", CORE)

time: 104 us -> 115 us (1.11)
  starting transfers between devices: 51 us -> 55.7 us
  waiting for transfers between devices: 23.8 us -> 28.1 us
  Pallas kernels: 25.4 us -> 28 us
    ppermute x1, waiting for transfers between devices: 0.01 us -> 8.97 us  [body(): gr = gr[:2] + lax.ppermute(gr[2:], 'row', Z_FLIP[1])]
    ppermute x1, starting transfers between devices: 4.04 us -> 6.89 us  [body(): gw_other = lax.ppermute(gw_own, 'row', CORE)]
    ppermute x1, waiting for transfers between devices: 2.67 us -> 0.01 us  [body(): gr = gr[:2] + lax.ppermute(gr[2:], 'row', Y_FLIP[1])]
    pallas_call x1 -> x2, Pallas kernels: 5.05 us -> 7.69 us  [the longest x1 3.85 us: body(): pair_calls[1](*in_hbm(oh, ol, w_out), b_out.reshape(1, Z), pair_half)]
    all_to_all x1, waiting for transfers between devices: 7.36 us -> 4.86 us  [body(): gw_own = lax.all_to_all(gw, BOTH, 0, 0, axis_index_groups=XY)]
    ppermute x2, starting transfers between devices: 3.06 us -> 5.22 us  [the longest x1 2.61 us: body(): gr_part = lax.ppermute(gr[1], 'row', Y_FLIP[3])]
    all_to_all x1, starting transfers between devices: 3.55 us -> 5.6 us  [body(): gw = lax.all_to_all(gw, BOTH, 0, 0, axis_index_groups=XY)]
    all_to_all x1, starting transfers between devices: 5.97 us -> 4.3 us  [body(): gw = lax.all_to_all(gw, BOTH, 0, 0, axis_index_groups=Z8)]
where the time goes in v7:
time: 115 us; the launch traced here: 114 us
  starting transfers between devices  55.7 us (48%)
  waiting for transfers between devices  28.1 us (24%)
  Pallas kernels  28 us (24%)
  other arithmetic  1.82 us (2%)
    all_to_all x1, starting transfers between devices, body(): right_own = lax.all_to_all(copies, 'row', 0, 0, axis_index_groups=YZ)  10.7 us
    ppermute x1, waiting for transfers between devices, body(): gr = gr[:2] + lax.ppermute(gr[2:], 'row', Z_FLIP[1])  8.97 us
    all_to_all x1, waiting for transfers between devices, body(): gw = lax.all_to_all(gw, BOTH, 0, 0, axis_index_groups=Z8)  8.13 us
    pallas_call x1, Pallas kernels, body(): grads_call(*pieces, *in_hbm(g, w_out))  7.83 us
    ppermute x1, starting transfers between devices, body(): gw_other = lax.ppermute(gw_own, 'row', CORE)  6.89 us
    all_to_all x1, starting transfers between devices, body(): gw = lax.all_to_all(gw, BOTH, 0, 0, axis_index_groups=XY)  5.6 us
    all_to_all x1, waiting for transfers between devices, body(): gw_own = lax.all_to_all(gw, BOTH, 0, 0, axis_index_groups=XY)  4.86 us
    pallas_call x1, Pallas kernels, body(): outer_call(left_parts, g_parts, bias, right_own, right_other)  4.69 us
  transfers between devices with their start and end apart: 19, of which 6 were waited for; matrix products, arithmetic and copies ran while one was open for 1% of the time, Pallas kernels for 24%

profile of v7, /device:TPU:1, one launch (start us, length us, event | category | flops | bytes accessed | tf_op | source)
XLA Modules:
  0.0 114.5 jit_solution(12712052053964883801)
XLA Ops:
  0.6 2.5 %collective-permute-start = (f32[16,512]{1,0:T(8,128)}, f32[16,512]{1,0:T(8,128)S(1)}, u32[]{:S(2)}, u32[]{:S(2)}) collective-permute-start(f32[16,512]{1,0:T(8,128)} %param.5), channel_id=1, source_target_pairs={{0,4},{1,5},{2,6},{3,7},{4,0},{5,1},{6,2},{7,3},{8,12},{9,13},{10,... | collective-permute-start | bytes 98312 | tf_op jit(solution)/shard_map/ppermute | solution.py:406
  3.2 1.5 %collective-permute-done = f32[16,512]{1,0:T(8,128)S(1)} collective-permute-done((f32[16,512]{1,0:T(8,128)}, f32[16,512]{1,0:T(8,128)S(1)}, u32[]{:S(2)}, u32[]{:S(2)}) %collective-permute-start) | collective-permute-done | bytes 32800 | tf_op jit(solution)/shard_map/ppermute | solution.py:406
  4.7 0.8 pad_maximum_fusion.l0_ref
  5.5 2.5 %collective-permute-start.3 = (f32[2,16,512]{2,1,0:T(8,128)S(1)}, f32[2,16,512]{2,1,0:T(8,128)S(1)}, u32[]{:S(2)}, u32[]{:S(2)}) collective-permute-start(f32[2,16,512]{2,1,0:T(8,128)S(1)} %pad_maximum_fusion.l0_ref), channel_id=1, source_target_pairs={{0,3},{1,0},{2,1},{3,2},{4,7},{5,4},{6,5},{7,6},{8,11},{9,8},{10,9... | collective-permute-start | bytes 196616 | tf_op jit(solution)/shard_map/ppermute | solution.py:410
  7.9 0.5 collective-permute-start.2
  8.5 0.6 collective-permute-start.1
  9.1 1.6 %shard_map.93 = f32[16,4,2048]{2,1,0:T(4,128)} custom-call(f32[4,2048]{1,0:T(4,128)} %x_ref.1), custom_call_target="tpu_custom_call" | custom-call | flops 100000 | bytes 524288 | tf_op jit(solution)/shard_map/pallas_call | solution.py:407
  10.6 10.7 %all-to-all-start = ((f32[16,4,2048]{2,1,0:T(4,128)}), f32[16,4,2048]{2,1,0:T(4,128)S(1)}, u32[]{:S(2)}, u32[]{:S(2)}) async-start(f32[16,4,2048]{2,1,0:T(4,128)} %shard_map.93), calls=%async_computation | async-start | bytes 1048576 | tf_op jit(solution)/shard_map/all_to_all | solution.py:408
  21.4 0.0 collective-permute-done.3.l3_ref
  21.4 0.0 collective-permute-done.2.l2_ref
  21.4 0.0 collective-permute-done.1.l1_ref
  21.4 7.8 %shard_map.92 = (bf16[512,2048]{1,0:T(8,128)(2,1)}, bf16[512,2048]{1,0:T(8,128)(2,1)}, f32[4,4,4,2048]{3,2,1,0:T(4,128)S(1)}, f32[4,4,4,2048]{3,2,1,0:T(4,128)S(...) custom-call(f32[2,16,512]{2,1,0:T(8,128)S(1)} %pad_maximum_fusion.l0_ref, ...), custom_call_target="tpu_custom_call" | custom-call | flops 2000000000 | bytes 6291456 | tf_op jit(solution)/shard_map/pallas_call | solution.py:411
  29.3 3.0 %collective-permute-start.7 = (f32[4,4,4,2048]{3,2,1,0:T(4,128)S(1)}, f32[4,4,4,2048]{3,2,1,0:T(4,128)S(1)}, u32[]{:S(2)}, u32[]{:S(2)}) collective-permute-start(f32[4,4,4,2048]{3,2,1,0:T(4,128)S(1)} %get-tuple-element.45), channel_id=1, source_target_pairs={{0,8},{8,0},{16,24},{24,16},{32,40},{40,32},{48,56},{56,48},{64,72... | collective-permute-start | bytes 1572872 | tf_op jit(solution)/shard_map/ppermute | solution.py:417
  32.3 1.5 %collective-permute-done.7 = f32[4,4,4,2048]{3,2,1,0:T(4,128)S(1)} collective-permute-done((f32[4,4,4,2048]{3,2,1,0:T(4,128)S(1)}, f32[4,4,4,2048]{3,2,1,0:T(4,128)S(1)}, u32[]{:S(2)}, u32[]{:S(2)}) %collective-permute-start.7) | collective-permute-done | bytes 524320 | tf_op jit(solution)/shard_map/ppermute | solution.py:417
  33.8 0.1 add.22
  34.0 2.6 %collective-permute-start.8 = (f32[2,4,4,2048]{3,2,1,0:T(4,128)S(1)}, f32[2,4,4,2048]{3,2,1,0:T(4,128)S(1)}, u32[]{:S(2)}, u32[]{:S(2)}) collective-permute-start(f32[2,4,4,2048]{3,2,1,0:T(4,128)S(1)} %slice.49), channel_id=1, source_target_pairs={{0,64},{8,72},{16,80},{24,88},{32,96},{40,104},{48,112},{56,120},{... | collective-permute-start | bytes 786440 | tf_op jit(solution)/shard_map/ppermute | solution.py:421
  36.6 0.0 all-to-all-done.own_ref
  36.6 3.0 %collective-permute-start.4 = (f32[16,4,2048]{2,1,0:T(4,128)S(1)}, f32[16,4,2048]{2,1,0:T(4,128)S(1)}, u32[]{:S(2)}, u32[]{:S(2)}) collective-permute-start(f32[16,4,2048]{2,1,0:T(4,128)S(1)} %all-to-all-done.own_ref), channel_id=1, source_target_pairs={{0,8},{8,0},{16,24},{24,16},{32,40},{40,32},{48,56},{56,48},{64,72... | collective-permute-start | bytes 1572872 | tf_op jit(solution)/shard_map/ppermute | solution.py:412
  39.6 9.0 %collective-permute-done.8 = f32[2,4,4,2048]{3,2,1,0:T(4,128)S(1)} collective-permute-done((f32[2,4,4,2048]{3,2,1,0:T(4,128)S(1)}, f32[2,4,4,2048]{3,2,1,0:T(4,128)S(1)}, u32[]{:S(2)}, u32[]{:S(2)}) %collective-permute-start.8) | collective-permute-done | bytes 262176 | tf_op jit(solution)/shard_map/ppermute | solution.py:421
  48.6 0.1 slice_add_fusion
  48.7 2.6 %collective-permute-start.9 = (f32[4,4,2048]{2,1,0:T(4,128)S(1)}, f32[4,4,2048]{2,1,0:T(4,128)S(1)}, u32[]{:S(2)}, u32[]{:S(2)}) collective-permute-start(f32[4,4,2048]{2,1,0:T(4,128)S(1)} %slice_bitcast_fusion), channel_id=1, source_target_pairs={{0,192},{8,200},{16,208},{24,216},{32,224},{40,232},{48,240},{56,2... | collective-permute-start | bytes 393224 | tf_op jit(solution)/shard_map/ppermute | solution.py:422
  51.3 0.0 collective-permute-done.4.other_ref
  51.3 4.7 %shard_map.94 = (bf16[4,1024,256]{2,1,0:T(8,128)(2,1)}, bf16[4,1024,256]{2,1,0:T(8,128)(2,1)}, bf16[2048,256]{1,0:T(8,128)(2,1)}, f32[16,40,128]{2,1,0:T(8,128)S(1)}, f32[16,40,128]{2,1,0:T(8,128)S(1)}) custom-call(bf16[512,384]{1,0:T(8,128)(2,1)S(1)} %get-tuple-element.29.at_ref, bf16[1024,256]{1,0:T(8,128)(2,1)S(1)} %get-tuple-element.30.gc_ref, ...), custom_call_target="tpu_custom_call" | custom-call | flops 2000000000 | bytes 7340032 | tf_op jit(solution)/shard_map/pallas_call | solution.py:413
  56.0 1.3 %collective-permute-start.5 = (f32[16,40,128]{2,1,0:T(8,128)S(1)}, f32[16,40,128]{2,1,0:T(8,128)S(1)}, u32[]{:S(2)}, u32[]{:S(2)}) collective-permute-start(f32[16,40,128]{2,1,0:T(8,128)S(1)} %get-tuple-element.33), channel_id=1, source_target_pairs={{0,8},{8,0},{16,24},{24,16},{32,40},{40,32},{48,56},{56,48},{64,72... | collective-permute-start | bytes 983048 | tf_op jit(solution)/shard_map/ppermute | solution.py:414
  57.3 0.0 collective-permute-done.9
  57.4 1.4 %collective-permute-start.10 = (f32[2,4,2048]{2,1,0:T(4,128)S(1)}, f32[2,4,2048]{2,1,0:T(4,128)S(1)}, u32[]{:S(2)}, u32[]{:S(2)}) collective-permute-start(f32[2,4,2048]{2,1,0:T(4,128)S(1)} %slice.53), channel_id=1, source_target_pairs={{0,16},{8,24},{16,0},{24,8},{32,48},{40,56},{48,32},{56,40},{64,80... | collective-permute-start | bytes 196616 | tf_op jit(solution)/shard_map/ppermute | solution.py:429
  58.8 0.0 collective-permute-done.5
  58.8 0.8 add.21
  59.6 5.6 %all-to-all-start.1 = ((f32[16,40,128]{2,1,0:T(8,128)}), f32[16,40,128]{2,1,0:T(8,128)S(1)}, u32[]{:S(2)}, u32[]{:S(2)}) async-start(f32[16,40,128]{2,1,0:T(8,128)} %add.21), calls=%async_computation.1 | async-start | bytes 655360 | tf_op jit(solution)/shard_map/all_to_all | solution.py:416
  65.2 3.9 %shard_map.99 = f32[4,2,16,512]{3,2,1,0:T(8,128)S(1)} custom-call(bf16[512,2048]{1,0:T(8,128)(2,1)} %get-tuple-element.46.goh_hbm, bf16[512,2048]{1,0:T(8,128)(2,1)} %get-tuple-element.47.gol_hbm, bf16[2048,256]{1,0:T(8,128)(2,1)} %get-tuple-element.48.bc_hbm), custom_call_target="tpu_custom_call" | custom-call | flops 1000000000 | bytes 6291456 | tf_op jit(solution)/shard_map/pallas_call | solution.py:418
  69.1 0.0 copy-start
  69.1 1.4 %collective-permute-start.12 = (f32[2,2,16,512]{3,2,1,0:T(8,128)S(1)}, f32[2,2,16,512]{3,2,1,0:T(8,128)S(1)}, u32[]{:S(2)}, u32[]{:S(2)}) collective-permute-start(f32[2,2,16,512]{3,2,1,0:T(8,128)S(1)} %slice.56), channel_id=1, source_target_pairs={{0,1},{1,0},{2,3},{3,2},{4,5},{5,4},{6,7},{7,6},{8,9},{9,8},{10,11... | collective-permute-start | bytes 393224 | tf_op jit(solution)/shard_map/ppermute | solution.py:423
  70.6 0.0 collective-permute-done.10
  70.6 3.1 %all-to-all-done.1.x_ref = f32[16,40,128]{2,1,0:T(8,128)S(1)} async-done(((f32[16,40,128]{2,1,0:T(8,128)}), f32[16,40,128]{2,1,0:T(8,128)S(1)}, u32[]{:S(2)}, u32[]{:S(2)}) %all-to-all-start.1) | async-done | bytes 327712 | tf_op jit(solution)/shard_map/all_to_all | solution.py:416
  73.6 0.7 shard_map.95
  74.3 4.3 %all-to-all-start.2 = ((f32[8,40,128]{2,1,0:T(8,128)}), f32[8,40,128]{2,1,0:T(8,128)S(1)}, u32[]{:S(2)}, u32[]{:S(2)}) async-start(f32[8,40,128]{2,1,0:T(8,128)} %shard_map.95), calls=%async_computation.2 | async-start | bytes 327680 | tf_op jit(solution)/shard_map/all_to_all | solution.py:425
  78.6 0.0 collective-permute-done.12
  78.7 0.1 collective-permute-start.13
  78.8 8.1 %all-to-all-done.2.x_ref = f32[8,40,128]{2,1,0:T(8,128)S(1)} async-done(((f32[8,40,128]{2,1,0:T(8,128)}), f32[8,40,128]{2,1,0:T(8,128)S(1)}, u32[]{:S(2)}, u32[]{:S(2)}) %all-to-all-start.2) | async-done | bytes 163872 | tf_op jit(solution)/shard_map/all_to_all | solution.py:425
  86.9 0.7 shard_map.98
  87.7 3.5 %all-to-all-start.3 = ((f32[16,32,128]{2,1,0:T(8,128)}), f32[16,32,128]{2,1,0:T(8,128)S(1)}, u32[]{:S(2)}, u32[]{:S(2)}) async-start(f32[16,32,128]{2,1,0:T(8,128)} %get-tuple-element.43), calls=%async_computation.3 | async-start | bytes 524288 | tf_op jit(solution)/shard_map/all_to_all | solution.py:432
  91.2 2.6 %collective-permute-start.11 = (f32[4,2048]{1,0:T(4,128)S(1)}, f32[4,2048]{1,0:T(4,128)S(1)}, u32[]{:S(2)}, u32[]{:S(2)}) collective-permute-start(f32[4,2048]{1,0:T(4,128)S(1)} %slice_bitcast_fusion.5), channel_id=1, source_target_pairs={{0,48},{8,56},{16,32},{24,40},{32,16},{40,24},{48,0},{56,8},{64,11... | collective-permute-start | bytes 98312 | tf_op jit(solution)/shard_map/ppermute | solution.py:430
  93.8 0.0 collective-permute-done.13
  93.8 4.9 %all-to-all-done.3.own_ref = f32[16,32,128]{2,1,0:T(8,128)S(1)} async-done(((f32[16,32,128]{2,1,0:T(8,128)}), f32[16,32,128]{2,1,0:T(8,128)S(1)}, u32[]{:S(2)}, u32[]{:S(2)}) %all-to-all-start.3) | async-done | bytes 262176 | tf_op jit(solution)/shard_map/all_to_all | solution.py:432
  98.7 6.9 %collective-permute-start.6 = (f32[16,32,128]{2,1,0:T(8,128)S(1)}, f32[16,32,128]{2,1,0:T(8,128)S(1)}, u32[]{:S(2)}, u32[]{:S(2)}) collective-permute-start(f32[16,32,128]{2,1,0:T(8,128)S(1)} %all-to-all-done.3.own_ref), channel_id=1, source_target_pairs={{0,8},{8,0},{16,24},{24,16},{32,40},{40,32},{48,56},{56,48},{64,72... | collective-permute-start | bytes 786440 | tf_op jit(solution)/shard_map/ppermute | solution.py:433
  105.6 0.3 collective-permute-start.14
  105.9 0.0 copy-done
  105.9 3.8 %shard_map.96.refs_0_ = f32[1024,128]{1,0:T(8,128)} custom-call(bf16[4,1024,256]{2,1,0:T(8,128)(2,1)} %get-tuple-element.40.oh_hbm, bf16[4,1024,256]{2,1,0:T(8,128)(2,1)} %get-tuple-element.41.ol_hbm, f32[1024,128]{1,0:T(8,128)} %w_hbm.5, f32[1,128]{1,0:T(1,128)S(1)} %bitcast.22), custom_call_target="tpu_custom_call" | custom-call | flops 500000000 | bytes 3145728 | tf_op jit(solution)/shard_map/pallas_call | solution.py:426
  109.7 3.8 %shard_map.97 = f32[1024,128]{1,0:T(8,128)} custom-call(bf16[4,1024,256]{2,1,0:T(8,128)(2,1)} %get-tuple-element.40.oh_hbm, bf16[4,1024,256]{2,1,0:T(8,128)(2,1)} %get-tuple-element.41.ol_hbm, f32[1024,128]{1,0:T(8,128)} %w_hbm.5, f32[1,128]{1,0:T(1,128)S(1)} %bitcast.23, f32[1024,128]{1,0:T(8,128)} %shard_map.96.refs_0_), custom_call_target="tpu_custom_call", output_to_operand_aliasing={{}: (4, {})} | custom-call | flops 500000000 | bytes 3145728 | tf_op jit(solution)/shard_map/pallas_call | solution.py:427
  113.6 0.0 collective-permute-done.11.r1_ref
  113.6 0.0 collective-permute-done.14.l1_ref
  113.6 0.0 collective-permute-done.6.other_ref
  113.6 0.8 shard_map.100
  (11 shorter events, 0.2 us)
Async XLA Ops:
  0.6 4.1 %collective-permute-start = (f32[16,512]{1,0:T(8,128)}, f32[16,512]{1,0:T(8,128)S(1)}, u32[]{:S(2)}, u32[]{:S(2)}) collective-permute-start(f32[16,512]{1,0:T(8,128)} %param.5), channel_id=1, source_target_pairs={{0,4},{1,5},{2,6},{3,7},{4,0},{5,1},{6,2},{7,3},{8,12},{9,13},{10,... | collective-permute-start | bytes 98312 | tf_op jit(solution)/shard_map/ppermute | solution.py:406
  5.5 15.9 %collective-permute-start.3 = (f32[2,16,512]{2,1,0:T(8,128)S(1)}, f32[2,16,512]{2,1,0:T(8,128)S(1)}, u32[]{:S(2)}, u32[]{:S(2)}) collective-permute-start(f32[2,16,512]{2,1,0:T(8,128)S(1)} %pad_maximum_fusion.l0_ref), channel_id=1, source_target_pairs={{0,3},{1,0},{2,1},{3,2},{4,7},{5,4},{6,5},{7,6},{8,11},{9,8},{10,9... | collective-permute-start | bytes 196616 | tf_op jit(solution)/shard_map/ppermute | solution.py:410
  7.9 13.5 %collective-permute-start.2 = (f32[2,16,512]{2,1,0:T(8,128)S(1)}, f32[2,16,512]{2,1,0:T(8,128)S(1)}, u32[]{:S(2)}, u32[]{:S(2)}) collective-permute-start(f32[2,16,512]{2,1,0:T(8,128)S(1)} %pad_maximum_fusion.l0_ref), channel_id=1, source_target_pairs={{0,2},{1,3},{2,0},{3,1},{4,6},{5,7},{6,4},{7,5},{8,10},{9,11},{10,... | collective-permute-start | bytes 196616 | tf_op jit(solution)/shard_map/ppermute | solution.py:410
  8.5 13.0 %collective-permute-start.1 = (f32[2,16,512]{2,1,0:T(8,128)S(1)}, f32[2,16,512]{2,1,0:T(8,128)S(1)}, u32[]{:S(2)}, u32[]{:S(2)}) collective-permute-start(f32[2,16,512]{2,1,0:T(8,128)S(1)} %pad_maximum_fusion.l0_ref), channel_id=1, source_target_pairs={{0,1},{1,2},{2,3},{3,0},{4,5},{5,6},{6,7},{7,4},{8,9},{9,10},{10,1... | collective-permute-start | bytes 196616 | tf_op jit(solution)/shard_map/ppermute | solution.py:410
  10.6 26.0 %all-to-all-start = ((f32[16,4,2048]{2,1,0:T(4,128)}), f32[16,4,2048]{2,1,0:T(4,128)S(1)}, u32[]{:S(2)}, u32[]{:S(2)}) async-start(f32[16,4,2048]{2,1,0:T(4,128)} %shard_map.93), calls=%async_computation | async-start | bytes 1048576 | tf_op jit(solution)/shard_map/all_to_all | solution.py:408
  29.3 4.6 %collective-permute-start.7 = (f32[4,4,4,2048]{3,2,1,0:T(4,128)S(1)}, f32[4,4,4,2048]{3,2,1,0:T(4,128)S(1)}, u32[]{:S(2)}, u32[]{:S(2)}) collective-permute-start(f32[4,4,4,2048]{3,2,1,0:T(4,128)S(1)} %get-tuple-element.45), channel_id=1, source_target_pairs={{0,8},{8,0},{16,24},{24,16},{32,40},{40,32},{48,56},{56,48},{64,72... | collective-permute-start | bytes 1572872 | tf_op jit(solution)/shard_map/ppermute | solution.py:417
  34.0 14.6 %collective-permute-start.8 = (f32[2,4,4,2048]{3,2,1,0:T(4,128)S(1)}, f32[2,4,4,2048]{3,2,1,0:T(4,128)S(1)}, u32[]{:S(2)}, u32[]{:S(2)}) collective-permute-start(f32[2,4,4,2048]{3,2,1,0:T(4,128)S(1)} %slice.49), channel_id=1, source_target_pairs={{0,64},{8,72},{16,80},{24,88},{32,96},{40,104},{48,112},{56,120},{... | collective-permute-start | bytes 786440 | tf_op jit(solution)/shard_map/ppermute | solution.py:421
  36.6 14.7 %collective-permute-start.4 = (f32[16,4,2048]{2,1,0:T(4,128)S(1)}, f32[16,4,2048]{2,1,0:T(4,128)S(1)}, u32[]{:S(2)}, u32[]{:S(2)}) collective-permute-start(f32[16,4,2048]{2,1,0:T(4,128)S(1)} %all-to-all-done.own_ref), channel_id=1, source_target_pairs={{0,8},{8,0},{16,24},{24,16},{32,40},{40,32},{48,56},{56,48},{64,72... | collective-permute-start | bytes 1572872 | tf_op jit(solution)/shard_map/ppermute | solution.py:412
  48.7 8.6 %collective-permute-start.9 = (f32[4,4,2048]{2,1,0:T(4,128)S(1)}, f32[4,4,2048]{2,1,0:T(4,128)S(1)}, u32[]{:S(2)}, u32[]{:S(2)}) collective-permute-start(f32[4,4,2048]{2,1,0:T(4,128)S(1)} %slice_bitcast_fusion), channel_id=1, source_target_pairs={{0,192},{8,200},{16,208},{24,216},{32,224},{40,232},{48,240},{56,2... | collective-permute-start | bytes 393224 | tf_op jit(solution)/shard_map/ppermute | solution.py:422
  56.0 2.8 %collective-permute-start.5 = (f32[16,40,128]{2,1,0:T(8,128)S(1)}, f32[16,40,128]{2,1,0:T(8,128)S(1)}, u32[]{:S(2)}, u32[]{:S(2)}) collective-permute-start(f32[16,40,128]{2,1,0:T(8,128)S(1)} %get-tuple-element.33), channel_id=1, source_target_pairs={{0,8},{8,0},{16,24},{24,16},{32,40},{40,32},{48,56},{56,48},{64,72... | collective-permute-start | bytes 983048 | tf_op jit(solution)/shard_map/ppermute | solution.py:414
  57.4 13.2 %collective-permute-start.10 = (f32[2,4,2048]{2,1,0:T(4,128)S(1)}, f32[2,4,2048]{2,1,0:T(4,128)S(1)}, u32[]{:S(2)}, u32[]{:S(2)}) collective-permute-start(f32[2,4,2048]{2,1,0:T(4,128)S(1)} %slice.53), channel_id=1, source_target_pairs={{0,16},{8,24},{16,0},{24,8},{32,48},{40,56},{48,32},{56,40},{64,80... | collective-permute-start | bytes 196616 | tf_op jit(solution)/shard_map/ppermute | solution.py:429
  59.6 14.1 %all-to-all-start.1 = ((f32[16,40,128]{2,1,0:T(8,128)}), f32[16,40,128]{2,1,0:T(8,128)S(1)}, u32[]{:S(2)}, u32[]{:S(2)}) async-start(f32[16,40,128]{2,1,0:T(8,128)} %add.21), calls=%async_computation.1 | async-start | bytes 655360 | tf_op jit(solution)/shard_map/all_to_all | solution.py:416
  69.1 36.8 %copy-start = (f32[128]{0:T(128)S(1)}, f32[128]{0:T(128)}, u32[]{:S(2)}) copy-start(f32[128]{0:T(128)} %param.8) | copy-start | bytes 1540
  69.1 9.5 %collective-permute-start.12 = (f32[2,2,16,512]{3,2,1,0:T(8,128)S(1)}, f32[2,2,16,512]{3,2,1,0:T(8,128)S(1)}, u32[]{:S(2)}, u32[]{:S(2)}) collective-permute-start(f32[2,2,16,512]{3,2,1,0:T(8,128)S(1)} %slice.56), channel_id=1, source_target_pairs={{0,1},{1,0},{2,3},{3,2},{4,5},{5,4},{6,7},{7,6},{8,9},{9,8},{10,11... | collective-permute-start | bytes 393224 | tf_op jit(solution)/shard_map/ppermute | solution.py:423
  74.3 12.6 %all-to-all-start.2 = ((f32[8,40,128]{2,1,0:T(8,128)}), f32[8,40,128]{2,1,0:T(8,128)S(1)}, u32[]{:S(2)}, u32[]{:S(2)}) async-start(f32[8,40,128]{2,1,0:T(8,128)} %shard_map.95), calls=%async_computation.2 | async-start | bytes 327680 | tf_op jit(solution)/shard_map/all_to_all | solution.py:425
  78.7 15.1 %collective-permute-start.13 = (f32[2,16,512]{2,1,0:T(8,128)S(1)}, f32[2,16,512]{2,1,0:T(8,128)S(1)}, u32[]{:S(2)}, u32[]{:S(2)}) collective-permute-start(f32[2,16,512]{2,1,0:T(8,128)S(1)} %slice_bitcast_fusion.2), channel_id=1, source_target_pairs={{0,3},{1,2},{2,1},{3,0},{4,7},{5,6},{6,5},{7,4},{8,11},{9,10},{10,... | collective-permute-start | bytes 196616 | tf_op jit(solution)/shard_map/ppermute | solution.py:424
  87.7 11.0 %all-to-all-start.3 = ((f32[16,32,128]{2,1,0:T(8,128)}), f32[16,32,128]{2,1,0:T(8,128)S(1)}, u32[]{:S(2)}, u32[]{:S(2)}) async-start(f32[16,32,128]{2,1,0:T(8,128)} %get-tuple-element.43), calls=%async_computation.3 | async-start | bytes 524288 | tf_op jit(solution)/shard_map/all_to_all | solution.py:432
  91.2 22.4 %collective-permute-start.11 = (f32[4,2048]{1,0:T(4,128)S(1)}, f32[4,2048]{1,0:T(4,128)S(1)}, u32[]{:S(2)}, u32[]{:S(2)}) collective-permute-start(f32[4,2048]{1,0:T(4,128)S(1)} %slice_bitcast_fusion.5), channel_id=1, source_target_pairs={{0,48},{8,56},{16,32},{24,40},{32,16},{40,24},{48,0},{56,8},{64,11... | collective-permute-start | bytes 98312 | tf_op jit(solution)/shard_map/ppermute | solution.py:430
  98.7 14.9 %collective-permute-start.6 = (f32[16,32,128]{2,1,0:T(8,128)S(1)}, f32[16,32,128]{2,1,0:T(8,128)S(1)}, u32[]{:S(2)}, u32[]{:S(2)}) collective-permute-start(f32[16,32,128]{2,1,0:T(8,128)S(1)} %all-to-all-done.3.own_ref), channel_id=1, source_target_pairs={{0,8},{8,0},{16,24},{24,16},{32,40},{40,32},{48,56},{56,48},{64,72... | collective-permute-start | bytes 786440 | tf_op jit(solution)/shard_map/ppermute | solution.py:433
  105.6 8.0 %collective-permute-start.14 = (f32[16,512]{1,0:T(8,128)S(1)}, f32[16,512]{1,0:T(8,128)S(1)}, u32[]{:S(2)}, u32[]{:S(2)}) collective-permute-start(f32[16,512]{1,0:T(8,128)S(1)} %slice_bitcast_fusion.4), channel_id=1, source_target_pairs={{0,4},{1,5},{2,6},{3,7},{4,0},{5,1},{6,2},{7,3},{8,12},{9,13},{10,... | collective-permute-start | bytes 98312 | tf_op jit(solution)/shard_map/ppermute | solution.py:431

commit v8 on v7

--- a/solution.py
+++ b/solution.py
@@ -131,8 +131,8 @@
         for k in range(16):
             yy = slot_of((k % 4) ^ y)
             zz = slot_of((k // 4) ^ z)
-            own_ref[zz, yy, :, 128 * m : 128 * m + 128] = block[4 * k : 4 * k + 4]
-            other_ref[zz, yy, :, 128 * m : 128 * m + 128] = block[64 + 4 * k : 68 + 4 * k]
+            own_ref[yy, zz, :, 128 * m : 128 * m + 128] = block[4 * k : 4 * k + 4]
+            other_ref[yy, zz, :, 128 * m : 128 * m + 128] = block[64 + 4 * k : 68 + 4 * k]
     for n in range(4):
         for put in puts(n):
             put.wait()
@@ -418,16 +418,16 @@
     (gl,) = grad_left_call(*in_hbm(goh, gol, bc))
     (gw,) = spread_call(gw)
     gw, oh, ol = tie((gw, oh, ol))
-    gr = gr[:2] + lax.ppermute(gr[2:], "row", Z_FLIP[1])
-    gr = gr[0] + lax.ppermute(gr[1], "row", Z_FLIP[3])
+    gr = gr[:2] + lax.ppermute(gr[2:], "row", Y_FLIP[1])
+    gr = gr[0] + lax.ppermute(gr[1], "row", Y_FLIP[3])
     gl = gl[:2] + lax.ppermute(gl[2:], "col", X_FLIP[1])
     gl = gl[0] + lax.ppermute(gl[1], "col", X_FLIP[3])
     gw = lax.all_to_all(gw, BOTH, 0, 0, axis_index_groups=Z8)
     (pair_half,) = pair_calls[0](*in_hbm(oh, ol, w_out), b_out.reshape(1, Z))
     (pair_out,) = pair_calls[1](*in_hbm(oh, ol, w_out), b_out.reshape(1, Z), pair_half)
     gw, grad_bias = final_call(gw)
-    gr = gr[:2] + lax.ppermute(gr[2:], "row", Y_FLIP[1])
-    gr_part = lax.ppermute(gr[1], "row", Y_FLIP[3])
+    gr = gr[:2] + lax.ppermute(gr[2:], "row", Z_FLIP[1])
+    gr_part = lax.ppermute(gr[1], "row", Z_FLIP[3])
     gl_part = lax.ppermute(gl[1], "col", H_PERM)
     gw_own = lax.all_to_all(gw, BOTH, 0, 0, axis_index_groups=XY)
     gw_other = lax.ppermute(gw_own, "row", CORE)

time: 115 us -> 106 us (0.922)
  starting transfers between devices: 55.7 us -> 51 us
  waiting for transfers between devices: 28.1 us -> 23.9 us
    ppermute x1, waiting for transfers between devices: 8.97 us -> 0.01 us  [body(): gr = gr[:2] + lax.ppermute(gr[2:], 'row', Z_FLIP[1])]
    ppermute x1, starting transfers between devices: 6.89 us -> 4.04 us  [body(): gw_other = lax.ppermute(gw_own, 'row', CORE)]
    ppermute x1, waiting for transfers between devices: 0.01 us -> 2.67 us  [body(): gr = gr[:2] + lax.ppermute(gr[2:], 'row', Y_FLIP[1])]
    all_to_all x1, waiting for transfers between devices: 4.86 us -> 7.36 us  [body(): gw_own = lax.all_to_all(gw, BOTH, 0, 0, axis_index_groups=XY)]
    ppermute x2, starting transfers between devices: 5.22 us -> 3.06 us  [the longest x1 2.93 us: body(): gr = gr[0] + lax.ppermute(gr[1], 'row', Y_FLIP[3])]
    all_to_all x1, starting transfers between devices: 5.6 us -> 3.55 us  [body(): gw = lax.all_to_all(gw, BOTH, 0, 0, axis_index_groups=XY)]
    all_to_all x1, starting transfers between devices: 4.3 us -> 5.97 us  [body(): gw = lax.all_to_all(gw, BOTH, 0, 0, axis_index_groups=Z8)]
  transfers between devices with their start and end apart: 19 -> 19, of which waited for: 6 -> 6; matrix products, arithmetic and copies ran while one was open for 1% -> 1% of each run, Pallas kernels for 24% -> 26%
where the time goes in v8:
time: 106 us
  starting transfers between devices  51 us (48%)
  Pallas kernels  28 us (26%)
  waiting for transfers between devices  23.9 us (23%)
  other arithmetic  1.82 us (2%)
    all_to_all x1, starting transfers between devices, body(): right_own = lax.all_to_all(copies, 'row', 0, 0, axis_index_groups=YZ)  10.7 us
    all_to_all x1, waiting for transfers between devices, body(): gw = lax.all_to_all(gw, BOTH, 0, 0, axis_index_groups=Z8)  8.17 us
    pallas_call x1, Pallas kernels, body(): grads_call(*pieces, *in_hbm(g, w_out))  7.83 us
    all_to_all x1, waiting for transfers between devices, body(): gw_own = lax.all_to_all(gw, BOTH, 0, 0, axis_index_groups=XY)  7.36 us
    all_to_all x1, starting transfers between devices, body(): gw = lax.all_to_all(gw, BOTH, 0, 0, axis_index_groups=Z8)  5.97 us
    pallas_call x1, Pallas kernels, body(): outer_call(left_parts, g_parts, bias, right_own, right_other)  4.69 us
    ppermute x1, starting transfers between devices, body(): gw_other = lax.ppermute(gw_own, 'row', CORE)  4.04 us
    ppermute x1, starting transfers between devices, body(): right_other = lax.ppermute(right_own, 'row', CORE)  3.89 us
  transfers between devices with their start and end apart: 19, of which 6 were waited for; matrix products, arithmetic and copies ran while one was open for 1% of the time, Pallas kernels for 26%

profile of v8, /device:TPU:1, one launch (start us, length us, event | category | flops | bytes accessed | tf_op | source)
XLA Modules:
  0.0 105.6 jit_solution(11390415101937720124)
XLA Ops:
  0.6 2.5 %collective-permute-start = (f32[16,512]{1,0:T(8,128)}, f32[16,512]{1,0:T(8,128)S(1)}, u32[]{:S(2)}, u32[]{:S(2)}) collective-permute-start(f32[16,512]{1,0:T(8,128)} %param.5), channel_id=1, source_target_pairs={{0,4},{1,5},{2,6},{3,7},{4,0},{5,1},{6,2},{7,3},{8,12},{9,13},{10,... | collective-permute-start | bytes 98312 | tf_op jit(solution)/shard_map/ppermute | solution.py:406
  3.2 1.5 %collective-permute-done = f32[16,512]{1,0:T(8,128)S(1)} collective-permute-done((f32[16,512]{1,0:T(8,128)}, f32[16,512]{1,0:T(8,128)S(1)}, u32[]{:S(2)}, u32[]{:S(2)}) %collective-permute-start) | collective-permute-done | bytes 32800 | tf_op jit(solution)/shard_map/ppermute | solution.py:406
  4.7 0.8 pad_maximum_fusion.l0_ref
  5.5 2.5 %collective-permute-start.3 = (f32[2,16,512]{2,1,0:T(8,128)S(1)}, f32[2,16,512]{2,1,0:T(8,128)S(1)}, u32[]{:S(2)}, u32[]{:S(2)}) collective-permute-start(f32[2,16,512]{2,1,0:T(8,128)S(1)} %pad_maximum_fusion.l0_ref), channel_id=1, source_target_pairs={{0,3},{1,0},{2,1},{3,2},{4,7},{5,4},{6,5},{7,6},{8,11},{9,8},{10,9... | collective-permute-start | bytes 196616 | tf_op jit(solution)/shard_map/ppermute | solution.py:410
  7.9 0.5 collective-permute-start.2
  8.5 0.6 collective-permute-start.1
  9.1 1.6 %shard_map.93 = f32[16,4,2048]{2,1,0:T(4,128)} custom-call(f32[4,2048]{1,0:T(4,128)} %x_ref.1), custom_call_target="tpu_custom_call" | custom-call | flops 100000 | bytes 524288 | tf_op jit(solution)/shard_map/pallas_call | solution.py:407
  10.6 10.7 %all-to-all-start = ((f32[16,4,2048]{2,1,0:T(4,128)}), f32[16,4,2048]{2,1,0:T(4,128)S(1)}, u32[]{:S(2)}, u32[]{:S(2)}) async-start(f32[16,4,2048]{2,1,0:T(4,128)} %shard_map.93), calls=%async_computation | async-start | bytes 1048576 | tf_op jit(solution)/shard_map/all_to_all | solution.py:408
  21.4 0.0 collective-permute-done.3.l3_ref
  21.4 0.0 collective-permute-done.2.l2_ref
  21.4 0.0 collective-permute-done.1.l1_ref
  21.4 7.8 %shard_map.92 = (bf16[512,2048]{1,0:T(8,128)(2,1)}, bf16[512,2048]{1,0:T(8,128)(2,1)}, f32[4,4,4,2048]{3,2,1,0:T(4,128)S(1)}, f32[4,4,4,2048]{3,2,1,0:T(4,128)S(...) custom-call(f32[2,16,512]{2,1,0:T(8,128)S(1)} %pad_maximum_fusion.l0_ref, ...), custom_call_target="tpu_custom_call" | custom-call | flops 2000000000 | bytes 6291456 | tf_op jit(solution)/shard_map/pallas_call | solution.py:411
  29.3 3.0 %collective-permute-start.7 = (f32[4,4,4,2048]{3,2,1,0:T(4,128)S(1)}, f32[4,4,4,2048]{3,2,1,0:T(4,128)S(1)}, u32[]{:S(2)}, u32[]{:S(2)}) collective-permute-start(f32[4,4,4,2048]{3,2,1,0:T(4,128)S(1)} %get-tuple-element.45), channel_id=1, source_target_pairs={{0,8},{8,0},{16,24},{24,16},{32,40},{40,32},{48,56},{56,48},{64,72... | collective-permute-start | bytes 1572872 | tf_op jit(solution)/shard_map/ppermute | solution.py:417
  32.3 1.5 %collective-permute-done.7 = f32[4,4,4,2048]{3,2,1,0:T(4,128)S(1)} collective-permute-done((f32[4,4,4,2048]{3,2,1,0:T(4,128)S(1)}, f32[4,4,4,2048]{3,2,1,0:T(4,128)S(1)}, u32[]{:S(2)}, u32[]{:S(2)}) %collective-permute-start.7) | collective-permute-done | bytes 524320 | tf_op jit(solution)/shard_map/ppermute | solution.py:417
  33.8 0.1 add.22
  34.0 1.7 %collective-permute-start.8 = (f32[2,4,4,2048]{3,2,1,0:T(4,128)S(1)}, f32[2,4,4,2048]{3,2,1,0:T(4,128)S(1)}, u32[]{:S(2)}, u32[]{:S(2)}) collective-permute-start(f32[2,4,4,2048]{3,2,1,0:T(4,128)S(1)} %slice.49), channel_id=1, source_target_pairs={{0,16},{8,24},{16,0},{24,8},{32,48},{40,56},{48,32},{56,40},{64,80... | collective-permute-start | bytes 786440 | tf_op jit(solution)/shard_map/ppermute | solution.py:421
  35.7 0.0 all-to-all-done.own_ref
  35.7 3.9 %collective-permute-start.4 = (f32[16,4,2048]{2,1,0:T(4,128)S(1)}, f32[16,4,2048]{2,1,0:T(4,128)S(1)}, u32[]{:S(2)}, u32[]{:S(2)}) collective-permute-start(f32[16,4,2048]{2,1,0:T(4,128)S(1)} %all-to-all-done.own_ref), channel_id=1, source_target_pairs={{0,8},{8,0},{16,24},{24,16},{32,40},{40,32},{48,56},{56,48},{64,72... | collective-permute-start | bytes 1572872 | tf_op jit(solution)/shard_map/ppermute | solution.py:412
  39.6 2.7 %collective-permute-done.8 = f32[2,4,4,2048]{3,2,1,0:T(4,128)S(1)} collective-permute-done((f32[2,4,4,2048]{3,2,1,0:T(4,128)S(1)}, f32[2,4,4,2048]{3,2,1,0:T(4,128)S(1)}, u32[]{:S(2)}, u32[]{:S(2)}) %collective-permute-start.8) | collective-permute-done | bytes 262176 | tf_op jit(solution)/shard_map/ppermute | solution.py:421
  42.3 0.1 slice_add_fusion
  42.4 2.9 %collective-permute-start.9 = (f32[4,4,2048]{2,1,0:T(4,128)S(1)}, f32[4,4,2048]{2,1,0:T(4,128)S(1)}, u32[]{:S(2)}, u32[]{:S(2)}) collective-permute-start(f32[4,4,2048]{2,1,0:T(4,128)S(1)} %slice_bitcast_fusion), channel_id=1, source_target_pairs={{0,48},{8,56},{16,32},{24,40},{32,16},{40,24},{48,0},{56,8},{64,11... | collective-permute-start | bytes 393224 | tf_op jit(solution)/shard_map/ppermute | solution.py:422
  45.3 0.0 collective-permute-done.4.other_ref
  45.3 4.7 %shard_map.94 = (bf16[4,1024,256]{2,1,0:T(8,128)(2,1)}, bf16[4,1024,256]{2,1,0:T(8,128)(2,1)}, bf16[2048,256]{1,0:T(8,128)(2,1)}, f32[16,40,128]{2,1,0:T(8,128)S(1)}, f32[16,40,128]{2,1,0:T(8,128)S(1)}) custom-call(bf16[512,384]{1,0:T(8,128)(2,1)S(1)} %get-tuple-element.29.at_ref, bf16[1024,256]{1,0:T(8,128)(2,1)S(1)} %get-tuple-element.30.gc_ref, ...), custom_call_target="tpu_custom_call" | custom-call | flops 2000000000 | bytes 7340032 | tf_op jit(solution)/shard_map/pallas_call | solution.py:413
  50.0 1.2 %collective-permute-start.5 = (f32[16,40,128]{2,1,0:T(8,128)S(1)}, f32[16,40,128]{2,1,0:T(8,128)S(1)}, u32[]{:S(2)}, u32[]{:S(2)}) collective-permute-start(f32[16,40,128]{2,1,0:T(8,128)S(1)} %get-tuple-element.33), channel_id=1, source_target_pairs={{0,8},{8,0},{16,24},{24,16},{32,40},{40,32},{48,56},{56,48},{64,72... | collective-permute-start | bytes 983048 | tf_op jit(solution)/shard_map/ppermute | solution.py:414
  51.3 0.0 collective-permute-done.9
  51.3 2.2 %collective-permute-start.10 = (f32[2,4,2048]{2,1,0:T(4,128)S(1)}, f32[2,4,2048]{2,1,0:T(4,128)S(1)}, u32[]{:S(2)}, u32[]{:S(2)}) collective-permute-start(f32[2,4,2048]{2,1,0:T(4,128)S(1)} %slice.53), channel_id=1, source_target_pairs={{0,64},{8,72},{16,80},{24,88},{32,96},{40,104},{48,112},{56,120},{... | collective-permute-start | bytes 196616 | tf_op jit(solution)/shard_map/ppermute | solution.py:429
  53.5 0.0 collective-permute-done.5
  53.5 0.8 add.21
  54.3 3.5 %all-to-all-start.1 = ((f32[16,40,128]{2,1,0:T(8,128)}), f32[16,40,128]{2,1,0:T(8,128)S(1)}, u32[]{:S(2)}, u32[]{:S(2)}) async-start(f32[16,40,128]{2,1,0:T(8,128)} %add.21), calls=%async_computation.1 | async-start | bytes 655360 | tf_op jit(solution)/shard_map/all_to_all | solution.py:416
  57.8 3.9 %shard_map.99 = f32[4,2,16,512]{3,2,1,0:T(8,128)S(1)} custom-call(bf16[512,2048]{1,0:T(8,128)(2,1)} %get-tuple-element.46.goh_hbm, bf16[512,2048]{1,0:T(8,128)(2,1)} %get-tuple-element.47.gol_hbm, bf16[2048,256]{1,0:T(8,128)(2,1)} %get-tuple-element.48.bc_hbm), custom_call_target="tpu_custom_call" | custom-call | flops 1000000000 | bytes 6291456 | tf_op jit(solution)/shard_map/pallas_call | solution.py:418
  61.7 0.0 copy-start
  61.8 1.5 %collective-permute-start.12 = (f32[2,2,16,512]{3,2,1,0:T(8,128)S(1)}, f32[2,2,16,512]{3,2,1,0:T(8,128)S(1)}, u32[]{:S(2)}, u32[]{:S(2)}) collective-permute-start(f32[2,2,16,512]{3,2,1,0:T(8,128)S(1)} %slice.56), channel_id=1, source_target_pairs={{0,1},{1,0},{2,3},{3,2},{4,5},{5,4},{6,7},{7,6},{8,9},{9,8},{10,11... | collective-permute-start | bytes 393224 | tf_op jit(solution)/shard_map/ppermute | solution.py:423
  63.3 0.0 collective-permute-done.10
  63.3 2.6 %all-to-all-done.1.x_ref = f32[16,40,128]{2,1,0:T(8,128)S(1)} async-done(((f32[16,40,128]{2,1,0:T(8,128)}), f32[16,40,128]{2,1,0:T(8,128)S(1)}, u32[]{:S(2)}, u32[]{:S(2)}) %all-to-all-start.1) | async-done | bytes 327712 | tf_op jit(solution)/shard_map/all_to_all | solution.py:416
  65.9 0.7 shard_map.95
  66.6 6.0 %all-to-all-start.2 = ((f32[8,40,128]{2,1,0:T(8,128)}), f32[8,40,128]{2,1,0:T(8,128)S(1)}, u32[]{:S(2)}, u32[]{:S(2)}) async-start(f32[8,40,128]{2,1,0:T(8,128)} %shard_map.95), calls=%async_computation.2 | async-start | bytes 327680 | tf_op jit(solution)/shard_map/all_to_all | solution.py:425
  72.6 0.0 collective-permute-done.12
  72.6 0.1 collective-permute-start.13
  72.7 8.2 %all-to-all-done.2.x_ref = f32[8,40,128]{2,1,0:T(8,128)S(1)} async-done(((f32[8,40,128]{2,1,0:T(8,128)}), f32[8,40,128]{2,1,0:T(8,128)S(1)}, u32[]{:S(2)}, u32[]{:S(2)}) %all-to-all-start.2) | async-done | bytes 163872 | tf_op jit(solution)/shard_map/all_to_all | solution.py:425
  80.9 0.7 shard_map.98
  81.6 3.5 %all-to-all-start.3 = ((f32[16,32,128]{2,1,0:T(8,128)}), f32[16,32,128]{2,1,0:T(8,128)S(1)}, u32[]{:S(2)}, u32[]{:S(2)}) async-start(f32[16,32,128]{2,1,0:T(8,128)} %get-tuple-element.43), calls=%async_computation.3 | async-start | bytes 524288 | tf_op jit(solution)/shard_map/all_to_all | solution.py:432
  85.2 0.1 collective-permute-start.11
  85.3 0.0 collective-permute-done.13
  85.3 7.4 %all-to-all-done.3.own_ref = f32[16,32,128]{2,1,0:T(8,128)S(1)} async-done(((f32[16,32,128]{2,1,0:T(8,128)}), f32[16,32,128]{2,1,0:T(8,128)S(1)}, u32[]{:S(2)}, u32[]{:S(2)}) %all-to-all-start.3) | async-done | bytes 262176 | tf_op jit(solution)/shard_map/all_to_all | solution.py:432
  92.7 4.0 %collective-permute-start.6 = (f32[16,32,128]{2,1,0:T(8,128)S(1)}, f32[16,32,128]{2,1,0:T(8,128)S(1)}, u32[]{:S(2)}, u32[]{:S(2)}) collective-permute-start(f32[16,32,128]{2,1,0:T(8,128)S(1)} %all-to-all-done.3.own_ref), channel_id=1, source_target_pairs={{0,8},{8,0},{16,24},{24,16},{32,40},{40,32},{48,56},{56,48},{64,72... | collective-permute-start | bytes 786440 | tf_op jit(solution)/shard_map/ppermute | solution.py:433
  96.7 0.3 collective-permute-start.14
  97.0 0.0 copy-done
  97.0 3.8 %shard_map.96.refs_0_ = f32[1024,128]{1,0:T(8,128)} custom-call(bf16[4,1024,256]{2,1,0:T(8,128)(2,1)} %get-tuple-element.40.oh_hbm, bf16[4,1024,256]{2,1,0:T(8,128)(2,1)} %get-tuple-element.41.ol_hbm, f32[1024,128]{1,0:T(8,128)} %w_hbm.5, f32[1,128]{1,0:T(1,128)S(1)} %bitcast.22), custom_call_target="tpu_custom_call" | custom-call | flops 500000000 | bytes 3145728 | tf_op jit(solution)/shard_map/pallas_call | solution.py:426
  100.9 3.8 %shard_map.97 = f32[1024,128]{1,0:T(8,128)} custom-call(bf16[4,1024,256]{2,1,0:T(8,128)(2,1)} %get-tuple-element.40.oh_hbm, bf16[4,1024,256]{2,1,0:T(8,128)(2,1)} %get-tuple-element.41.ol_hbm, f32[1024,128]{1,0:T(8,128)} %w_hbm.5, f32[1,128]{1,0:T(1,128)S(1)} %bitcast.23, f32[1024,128]{1,0:T(8,128)} %shard_map.96.refs_0_), custom_call_target="tpu_custom_call", output_to_operand_aliasing={{}: (4, {})} | custom-call | flops 500000000 | bytes 3145728 | tf_op jit(solution)/shard_map/pallas_call | solution.py:427
  104.7 0.0 collective-permute-done.11.r1_ref
  104.7 0.0 collective-permute-done.14.l1_ref
  104.7 0.0 collective-permute-done.6.other_ref
  104.8 0.8 shard_map.100
  (11 shorter events, 0.2 us)
Async XLA Ops:
  0.6 4.1 %collective-permute-start = (f32[16,512]{1,0:T(8,128)}, f32[16,512]{1,0:T(8,128)S(1)}, u32[]{:S(2)}, u32[]{:S(2)}) collective-permute-start(f32[16,512]{1,0:T(8,128)} %param.5), channel_id=1, source_target_pairs={{0,4},{1,5},{2,6},{3,7},{4,0},{5,1},{6,2},{7,3},{8,12},{9,13},{10,... | collective-permute-start | bytes 98312 | tf_op jit(solution)/shard_map/ppermute | solution.py:406
  5.5 15.9 %collective-permute-start.3 = (f32[2,16,512]{2,1,0:T(8,128)S(1)}, f32[2,16,512]{2,1,0:T(8,128)S(1)}, u32[]{:S(2)}, u32[]{:S(2)}) collective-permute-start(f32[2,16,512]{2,1,0:T(8,128)S(1)} %pad_maximum_fusion.l0_ref), channel_id=1, source_target_pairs={{0,3},{1,0},{2,1},{3,2},{4,7},{5,4},{6,5},{7,6},{8,11},{9,8},{10,9... | collective-permute-start | bytes 196616 | tf_op jit(solution)/shard_map/ppermute | solution.py:410
  7.9 13.5 %collective-permute-start.2 = (f32[2,16,512]{2,1,0:T(8,128)S(1)}, f32[2,16,512]{2,1,0:T(8,128)S(1)}, u32[]{:S(2)}, u32[]{:S(2)}) collective-permute-start(f32[2,16,512]{2,1,0:T(8,128)S(1)} %pad_maximum_fusion.l0_ref), channel_id=1, source_target_pairs={{0,2},{1,3},{2,0},{3,1},{4,6},{5,7},{6,4},{7,5},{8,10},{9,11},{10,... | collective-permute-start | bytes 196616 | tf_op jit(solution)/shard_map/ppermute | solution.py:410
  8.5 13.0 %collective-permute-start.1 = (f32[2,16,512]{2,1,0:T(8,128)S(1)}, f32[2,16,512]{2,1,0:T(8,128)S(1)}, u32[]{:S(2)}, u32[]{:S(2)}) collective-permute-start(f32[2,16,512]{2,1,0:T(8,128)S(1)} %pad_maximum_fusion.l0_ref), channel_id=1, source_target_pairs={{0,1},{1,2},{2,3},{3,0},{4,5},{5,6},{6,7},{7,4},{8,9},{9,10},{10,1... | collective-permute-start | bytes 196616 | tf_op jit(solution)/shard_map/ppermute | solution.py:410
  10.6 25.1 %all-to-all-start = ((f32[16,4,2048]{2,1,0:T(4,128)}), f32[16,4,2048]{2,1,0:T(4,128)S(1)}, u32[]{:S(2)}, u32[]{:S(2)}) async-start(f32[16,4,2048]{2,1,0:T(4,128)} %shard_map.93), calls=%async_computation | async-start | bytes 1048576 | tf_op jit(solution)/shard_map/all_to_all | solution.py:408
  29.3 4.6 %collective-permute-start.7 = (f32[4,4,4,2048]{3,2,1,0:T(4,128)S(1)}, f32[4,4,4,2048]{3,2,1,0:T(4,128)S(1)}, u32[]{:S(2)}, u32[]{:S(2)}) collective-permute-start(f32[4,4,4,2048]{3,2,1,0:T(4,128)S(1)} %get-tuple-element.45), channel_id=1, source_target_pairs={{0,8},{8,0},{16,24},{24,16},{32,40},{40,32},{48,56},{56,48},{64,72... | collective-permute-start | bytes 1572872 | tf_op jit(solution)/shard_map/ppermute | solution.py:417
  34.0 8.3 %collective-permute-start.8 = (f32[2,4,4,2048]{3,2,1,0:T(4,128)S(1)}, f32[2,4,4,2048]{3,2,1,0:T(4,128)S(1)}, u32[]{:S(2)}, u32[]{:S(2)}) collective-permute-start(f32[2,4,4,2048]{3,2,1,0:T(4,128)S(1)} %slice.49), channel_id=1, source_target_pairs={{0,16},{8,24},{16,0},{24,8},{32,48},{40,56},{48,32},{56,40},{64,80... | collective-permute-start | bytes 786440 | tf_op jit(solution)/shard_map/ppermute | solution.py:421
  35.7 9.6 %collective-permute-start.4 = (f32[16,4,2048]{2,1,0:T(4,128)S(1)}, f32[16,4,2048]{2,1,0:T(4,128)S(1)}, u32[]{:S(2)}, u32[]{:S(2)}) collective-permute-start(f32[16,4,2048]{2,1,0:T(4,128)S(1)} %all-to-all-done.own_ref), channel_id=1, source_target_pairs={{0,8},{8,0},{16,24},{24,16},{32,40},{40,32},{48,56},{56,48},{64,72... | collective-permute-start | bytes 1572872 | tf_op jit(solution)/shard_map/ppermute | solution.py:412
  42.4 8.9 %collective-permute-start.9 = (f32[4,4,2048]{2,1,0:T(4,128)S(1)}, f32[4,4,2048]{2,1,0:T(4,128)S(1)}, u32[]{:S(2)}, u32[]{:S(2)}) collective-permute-start(f32[4,4,2048]{2,1,0:T(4,128)S(1)} %slice_bitcast_fusion), channel_id=1, source_target_pairs={{0,48},{8,56},{16,32},{24,40},{32,16},{40,24},{48,0},{56,8},{64,11... | collective-permute-start | bytes 393224 | tf_op jit(solution)/shard_map/ppermute | solution.py:422
  50.0 3.5 %collective-permute-start.5 = (f32[16,40,128]{2,1,0:T(8,128)S(1)}, f32[16,40,128]{2,1,0:T(8,128)S(1)}, u32[]{:S(2)}, u32[]{:S(2)}) collective-permute-start(f32[16,40,128]{2,1,0:T(8,128)S(1)} %get-tuple-element.33), channel_id=1, source_target_pairs={{0,8},{8,0},{16,24},{24,16},{32,40},{40,32},{48,56},{56,48},{64,72... | collective-permute-start | bytes 983048 | tf_op jit(solution)/shard_map/ppermute | solution.py:414
  51.3 12.0 %collective-permute-start.10 = (f32[2,4,2048]{2,1,0:T(4,128)S(1)}, f32[2,4,2048]{2,1,0:T(4,128)S(1)}, u32[]{:S(2)}, u32[]{:S(2)}) collective-permute-start(f32[2,4,2048]{2,1,0:T(4,128)S(1)} %slice.53), channel_id=1, source_target_pairs={{0,64},{8,72},{16,80},{24,88},{32,96},{40,104},{48,112},{56,120},{... | collective-permute-start | bytes 196616 | tf_op jit(solution)/shard_map/ppermute | solution.py:429
  54.3 11.6 %all-to-all-start.1 = ((f32[16,40,128]{2,1,0:T(8,128)}), f32[16,40,128]{2,1,0:T(8,128)S(1)}, u32[]{:S(2)}, u32[]{:S(2)}) async-start(f32[16,40,128]{2,1,0:T(8,128)} %add.21), calls=%async_computation.1 | async-start | bytes 655360 | tf_op jit(solution)/shard_map/all_to_all | solution.py:416
  61.7 35.3 %copy-start = (f32[128]{0:T(128)S(1)}, f32[128]{0:T(128)}, u32[]{:S(2)}) copy-start(f32[128]{0:T(128)} %param.8) | copy-start | bytes 1540
  61.8 10.8 %collective-permute-start.12 = (f32[2,2,16,512]{3,2,1,0:T(8,128)S(1)}, f32[2,2,16,512]{3,2,1,0:T(8,128)S(1)}, u32[]{:S(2)}, u32[]{:S(2)}) collective-permute-start(f32[2,2,16,512]{3,2,1,0:T(8,128)S(1)} %slice.56), channel_id=1, source_target_pairs={{0,1},{1,0},{2,3},{3,2},{4,5},{5,4},{6,7},{7,6},{8,9},{9,8},{10,11... | collective-permute-start | bytes 393224 | tf_op jit(solution)/shard_map/ppermute | solution.py:423
  66.6 14.3 %all-to-all-start.2 = ((f32[8,40,128]{2,1,0:T(8,128)}), f32[8,40,128]{2,1,0:T(8,128)S(1)}, u32[]{:S(2)}, u32[]{:S(2)}) async-start(f32[8,40,128]{2,1,0:T(8,128)} %shard_map.95), calls=%async_computation.2 | async-start | bytes 327680 | tf_op jit(solution)/shard_map/all_to_all | solution.py:425
  72.6 12.7 %collective-permute-start.13 = (f32[2,16,512]{2,1,0:T(8,128)S(1)}, f32[2,16,512]{2,1,0:T(8,128)S(1)}, u32[]{:S(2)}, u32[]{:S(2)}) collective-permute-start(f32[2,16,512]{2,1,0:T(8,128)S(1)} %slice_bitcast_fusion.2), channel_id=1, source_target_pairs={{0,3},{1,2},{2,1},{3,0},{4,7},{5,6},{6,5},{7,4},{8,11},{9,10},{10,... | collective-permute-start | bytes 196616 | tf_op jit(solution)/shard_map/ppermute | solution.py:424
  81.6 11.1 %all-to-all-start.3 = ((f32[16,32,128]{2,1,0:T(8,128)}), f32[16,32,128]{2,1,0:T(8,128)S(1)}, u32[]{:S(2)}, u32[]{:S(2)}) async-start(f32[16,32,128]{2,1,0:T(8,128)} %get-tuple-element.43), calls=%async_computation.3 | async-start | bytes 524288 | tf_op jit(solution)/shard_map/all_to_all | solution.py:432
  85.2 19.6 %collective-permute-start.11 = (f32[4,2048]{1,0:T(4,128)S(1)}, f32[4,2048]{1,0:T(4,128)S(1)}, u32[]{:S(2)}, u32[]{:S(2)}) collective-permute-start(f32[4,2048]{1,0:T(4,128)S(1)} %slice_bitcast_fusion.5), channel_id=1, source_target_pairs={{0,192},{8,200},{16,208},{24,216},{32,224},{40,232},{48,240},{56,2... | collective-permute-start | bytes 98312 | tf_op jit(solution)/shard_map/ppermute | solution.py:430
  92.7 12.1 %collective-permute-start.6 = (f32[16,32,128]{2,1,0:T(8,128)S(1)}, f32[16,32,128]{2,1,0:T(8,128)S(1)}, u32[]{:S(2)}, u32[]{:S(2)}) collective-permute-start(f32[16,32,128]{2,1,0:T(8,128)S(1)} %all-to-all-done.3.own_ref), channel_id=1, source_target_pairs={{0,8},{8,0},{16,24},{24,16},{32,40},{40,32},{48,56},{56,48},{64,72... | collective-permute-start | bytes 786440 | tf_op jit(solution)/shard_map/ppermute | solution.py:433
  96.7 8.0 %collective-permute-start.14 = (f32[16,512]{1,0:T(8,128)S(1)}, f32[16,512]{1,0:T(8,128)S(1)}, u32[]{:S(2)}, u32[]{:S(2)}) collective-permute-start(f32[16,512]{1,0:T(8,128)S(1)} %slice_bitcast_fusion.4), channel_id=1, source_target_pairs={{0,4},{1,5},{2,6},{3,7},{4,0},{5,1},{6,2},{7,3},{8,12},{9,13},{10,... | collective-permute-start | bytes 98312 | tf_op jit(solution)/shard_map/ppermute | solution.py:431
